TPU v7x, 32 devices: a whole 2x2x4 slice. The times are simulated.
32 devices in a mesh: groups: 2 (over x), cols: 16 (over z, y, core).
Axes of the slice: x: 2, y: 2, z: 4, core: 2. Of those that a mesh axis runs over, the one named last changes fastest.
Arguments:
- left_feat: bfloat16 [4, 64, 256, 256], P('groups', None, 'cols'), parts along dimension 0, may hold values from -6 to 6
- right_feat: bfloat16 [4, 64, 256, 256], P('groups', None, 'cols'), parts along dimension 0, may hold values from -6 to 6
- bounds: int32 [4], P('groups'), parts along dimension 0, may hold values from 16 to 64, as said below
- disparity: int32 [4, 64, 256], P('groups', None, 'cols'), parts along dimension 0, may hold values from 0 to 63, as said below
- hidden_fine: bfloat16 [4, 64, 256, 128], P('groups', None, 'cols'), parts along dimension 0, may hold values from -1 to 1
- hidden_coarse: bfloat16 [4, 8, 32, 128], P('groups', None, 'cols'), parts along dimension 0, may hold values from -1 to 1
- motion_weight: bfloat16 [36, 128], replicated, may hold values from -1 to 1
- fine_gates: bfloat16 [9, 384, 256], replicated, may hold values from -0.109375 to 0.109375
- fine_candidate: bfloat16 [9, 384, 128], replicated, may hold values from -0.109375 to 0.109375
- coarse_gates: bfloat16 [9, 256, 256], replicated, may hold values from -0.125 to 0.125
- coarse_candidate: bfloat16 [9, 256, 128], replicated, may hold values from -0.125 to 0.125
Outputs:
- hidden_fine_new: bfloat16 [4, 64, 256, 128], P('groups', None, 'cols'), parts along dimension 0
- hidden_coarse_new: bfloat16 [4, 8, 32, 128], P('groups', None, 'cols'), parts along dimension 0
There are 2 independent parts, one for each index of `groups`. A program takes and returns all parts, laid end to end along the dimension named above; an argument that names none is the same for every part. Nothing has to cross between parts.
Inputs may be any that keep to these rules, and one draw needn't show every extreme that they name: bounds[i] bounds the disparities of image pair i; in every draw one image pair has exactly 64. `disparity`: every entry lies below its image pair's bound; in every draw some entry equals 63.
All inputs are finite; a program needn't handle non-finite values.
Results may differ from a plain program's by a relative error of at most 0.0043.
Values may be sent and summed in bfloat16 or wider, within the bound.
No kernel may reach another device: no remote copies, remote signals or barrier semaphores. Data moves between devices by JAX's collectives and lax.ppermute only.
A program may use at most 64 MiB of HBM per device.

v0:
```python
import jax
import jax.numpy as jnp
from jax import lax
from jax.sharding import PartitionSpec as P

LEVELS = 4
RADIUS = 4
MAXD = 64


def with_halo(value, sides, width):
    for axis, dim in sides:
        peers, length = (lax.axis_size(axis), value.shape[dim])
        up = [(i, (i + 1) % peers) for i in range(peers)]
        down = [(j, i) for i, j in up]
        last = lax.slice_in_dim(value, length - width, length, axis=dim)
        first = lax.slice_in_dim(value, 0, width, axis=dim)
        before = lax.ppermute(last, axis, up)
        after = lax.ppermute(first, axis, down)
        value = jnp.concatenate([before, value, after], axis=dim)
    return value


def from_behind(value, axis, steps):
    count = lax.axis_size(axis)
    pairs = [(source, (source + steps) % count) for source in range(count)]
    return lax.ppermute(value, axis, pairs)


def convolve(padded, weight):
    images, rows_pad, cols_pad, channels = padded.shape
    rows_out = rows_pad - 2
    cols_out = cols_pad - 2
    summed = jnp.zeros((images * rows_out * cols_out, weight.shape[2]), jnp.float32)
    for row_off in range(3):
        for col_off in range(3):
            window = padded[
                :, row_off : row_off + rows_out, col_off : col_off + cols_out, :
            ].reshape(-1, channels)
            summed = summed + jnp.dot(
                window, weight[3 * row_off + col_off], preferred_element_type=jnp.float32
            )
    return summed.reshape(images, rows_out, cols_out, weight.shape[2])


def pad_rows(field):
    return jnp.pad(field, ((0, 0), (1, 1), (0, 0), (0, 0)))


def gru_level(state, extra, gates_weight, cand_weight):
    hidden_width = state.shape[-1]
    gru_input = jnp.concatenate([state, extra], -1)
    widened = with_halo(gru_input, (("cols", 2),), 1)
    gates = jax.nn.sigmoid(convolve(pad_rows(widened), gates_weight))
    update_gate = gates[..., :hidden_width]
    reset_state = (gates[..., hidden_width:] * state.astype(jnp.float32)).astype(jnp.bfloat16)
    reset_wide = with_halo(reset_state, (("cols", 2),), 1)
    cand_input = jnp.concatenate([reset_wide, widened[..., hidden_width:]], -1)
    candidate = jnp.tanh(convolve(pad_rows(cand_input), cand_weight))
    updated = (1.0 - update_gate) * state.astype(jnp.float32) + update_gate * candidate
    return updated.astype(jnp.bfloat16)


def correlate(left_feat, right_cat, limits, npanel):
    images, rows_here, cols_here, channels = left_feat.shape
    span = right_cat.shape[2]
    scores = jnp.einsum(
        "irxc,irec->irxe", left_feat, right_cat, preferred_element_type=jnp.float32
    ) * channels ** (-0.5)
    flattened = scores.reshape(images, rows_here, cols_here * span)
    flattened = jnp.pad(flattened, ((0, 0), (0, 0), (0, cols_here)))
    diagonal = flattened.reshape(images, rows_here, cols_here, span + 1)
    top_index = npanel * cols_here
    cost = diagonal[..., top_index - MAXD + 1 : top_index + 1][..., ::-1]
    valid = jnp.arange(MAXD, dtype=jnp.int32)[None, None, None, :] < limits
    return jnp.where(valid, cost, 0.0)


def pyramid_lookup(cost, disparity):
    features = []
    volume = cost
    for octave in range(LEVELS):
        if octave > 0:
            volume = 0.5 * (volume[..., 0::2] + volume[..., 1::2])
        entries = volume.shape[-1]
        center = disparity // 2**octave
        position = center[..., None] + jnp.arange(2 * RADIUS + 1, dtype=jnp.int32) - RADIUS
        onehot = position[..., None] == jnp.arange(entries, dtype=jnp.int32)
        features.append(jnp.sum(jnp.where(onehot, volume[..., None, :], 0.0), axis=-1))
    return jnp.concatenate(features, -1)


def motion_features(cost, disparity, motion_weight):
    lookup = pyramid_lookup(cost, disparity).astype(jnp.bfloat16)
    motion = jax.nn.relu(
        jnp.dot(
            lookup.reshape(-1, lookup.shape[-1]), motion_weight, preferred_element_type=jnp.float32
        )
    )
    return motion.astype(jnp.bfloat16)


def local(
    left_feat,
    right_feat,
    bounds,
    disparity,
    hidden_fine,
    hidden_coarse,
    motion_weight,
    fine_gates,
    fine_candidate,
    coarse_gates,
    coarse_candidate,
):
    images, rows_here, cols_here, channels = left_feat.shape
    hidden_width = hidden_fine.shape[-1]
    npanel = (MAXD - 1) // cols_here + 1
    pieces = [right_feat]
    current = right_feat
    for offset in range(npanel):
        current = from_behind(current, "cols", 1)
        pieces.append(current)
    right_cat = jnp.concatenate(list(reversed(pieces)), axis=2)
    cost = correlate(left_feat, right_cat, bounds[:, None, None, None], npanel)
    motion = motion_features(cost, disparity, motion_weight).reshape(
        images, rows_here, cols_here, hidden_width
    )
    pooled = hidden_fine.astype(jnp.float32).reshape(
        images, rows_here // 8, 8, cols_here // 8, 8, hidden_width
    )
    pooled = jnp.mean(pooled, axis=(2, 4)).astype(jnp.bfloat16)
    coarse_new = gru_level(hidden_coarse, pooled, coarse_gates, coarse_candidate)
    upsampled = jnp.repeat(jnp.repeat(coarse_new, 8, axis=1), 8, axis=2)
    fine_new = gru_level(
        hidden_fine, jnp.concatenate([motion, upsampled], -1), fine_gates, fine_candidate
    )
    return (fine_new, coarse_new)


def solution(mesh):
    return jax.shard_map(
        local,
        mesh=mesh,
        in_specs=(
            P("groups", None, "cols", None),
            P("groups", None, "cols", None),
            P("groups"),
            P("groups", None, "cols"),
            P("groups", None, "cols", None),
            P("groups", None, "cols", None),
            P(),
            P(),
            P(),
            P(),
            P(),
        ),
        out_specs=(P("groups", None, "cols", None), P("groups", None, "cols", None)),
        check_vma=False,
    )
```

profile of v0, /device:TPU:0, one launch (start us, length us, event | category | flops | bytes accessed | tf_op | source)
XLA Modules:
  0.0 148.1 jit_solution(8581753170040057556)
XLA Ops:
  3.2 5.1 %collective-permute-start.5 = (bf16[2,8,1,256]{3,2,1,0:T(2,128)(2,1)S(1)}, bf16[2,8,1,256]{3,2,1,0:T(2,128)(2,1)S(1)}, u32[]{:S(2)}, u32[]{:S(2)}) collective-permute-start(bf16[2,8,1,256]{3,2,1,0:T(2,128)(2,1)S(1)} %get-tuple-element.47), channel_id=1, source_target_pairs={{1,0},{2,1},{3,2},{4,3},{5,4},{6,5},{7,6},{8,7},{9,8},{10,9},{11,1... | collective-permute-start | bytes 24584 | tf_op jit(solution)/shard_map/ppermute | solution.py:19
  21.4 4.1 %collective-permute-done = bf16[2,64,16,256]{3,2,1,0:T(8,128)(2,1)S(1)} collective-permute-done((bf16[2,64,16,256]{3,2,1,0:T(8,128)(2,1)}, bf16[2,64,16,256]{3,2,1,0:T(8,128)(2,1)S(1)}, u32[]{:S(2)}, u32[]{:S(2)}) %collective-permute-start) | collective-permute-done | bytes 1048608 | tf_op jit(solution)/shard_map/ppermute | solution.py:27
  25.5 4.5 %collective-permute-start.7 = (bf16[2,8,1,128]{3,2,1,0:T(2,128)(2,1)S(1)}, bf16[2,8,1,128]{3,2,1,0:T(2,128)(2,1)S(1)}, u32[]{:S(2)}, u32[]{:S(2)}) collective-permute-start(bf16[2,8,1,128]{3,2,1,0:T(2,128)(2,1)S(1)} %get-tuple-element.49), channel_id=1, source_target_pairs={{1,0},{2,1},{3,2},{4,3},{5,4},{6,5},{7,6},{8,7},{9,8},{10,9},{11,1... | collective-permute-start | bytes 12296 | tf_op jit(solution)/shard_map/ppermute | solution.py:19
  30.6 11.8 %collective-permute-done.6 = bf16[2,8,1,128]{3,2,1,0:T(2,128)(2,1)S(1)} collective-permute-done((bf16[2,8,1,128]{3,2,1,0:T(2,128)(2,1)S(1)}, bf16[2,8,1,128]{3,2,1,0:T(2,128)(2,1)S(1)}, u32[]{:S(2)}, u32[]{:S(2)}) %collective-permute-start.6) | collective-permute-done | bytes 4128 | tf_op jit(solution)/shard_map/ppermute | solution.py:18
  48.6 12.3 %collective-permute-done.2 = bf16[2,64,16,256]{3,2,1,0:T(8,128)(2,1)S(1)} collective-permute-done((bf16[2,64,16,256]{3,2,1,0:T(8,128)(2,1)}, bf16[2,64,16,256]{3,2,1,0:T(8,128)(2,1)S(1)}, u32[]{:S(2)}, u32[]{:S(2)}) %collective-permute-start.2) | collective-permute-done | bytes 1048608 | tf_op jit(solution)/shard_map/ppermute | solution.py:27
  64.0 13.8 %collective-permute-done.3 = bf16[2,64,16,256]{3,2,1,0:T(8,128)(2,1)S(1)} collective-permute-done((bf16[2,64,16,256]{3,2,1,0:T(8,128)(2,1)S(1)}, bf16[2,64,16,256]{3,2,1,0:T(8,128)(2,1)S(1)}, u32[]{:S(2)}, u32[]{:S(2)}) %collective-permute-start.3) | collective-permute-done | bytes 1048608 | tf_op jit(solution)/shard_map/ppermute | solution.py:27
  78.0 1.4 constant_dynamic-update-slice_fusion.2
  79.8 2.5 %fusion.11 = f32[2,64,16,80]{3,2,1,0:T(8,128)} fusion(bf16[2,64,80,256]{3,2,1,0:T(8,128)(2,1)S(1)} %constant_dynamic-update-slice_fusion, bf16[2,64,16,256]{3,2,1,0:T(8,128)(2,1)S(1)} %copy-done), kind=kOutput, calls=%fused_computation.43 | convolution fusion | flops 84049920 | bytes 6946816 | tf_op jit(solution)/shard_map/irxc,irec->irxe/dot_general | solution.py:67
  82.3 1.7 %reshape.205 = f32[2,64,1280]{2,1,0:T(8,128)S(1)} reshape(f32[2,64,16,80]{3,2,1,0:T(8,128)} %fusion.11) | data formatting | bytes 1310720 | tf_op jit(solution)/shard_map/reshape | solution.py:70
  85.0 1.3 slice.382
  86.3 1.6 %copy.69 = f32[2,64,16,64]{1,3,2,0:T(8,128)S(1)} copy(f32[2,64,16,64]{3,2,1,0:T(8,128)} %slice.382) | data formatting | bytes 1048576
  89.1 1.4 broadcast_select_fusion
  91.3 2.2 %slice.292 = f32[2,64,16,32]{1,3,2,0:T(8,128)} slice(f32[2,64,16,64]{1,3,2,0:T(8,128)S(1)} %broadcast_select_fusion), slice={[0:2:1], [0:64:1], [0:16:1], [0:64:2]} | slice | bytes 524288 | tf_op jit(solution)/shard_map/slice | solution.py:84
  93.5 1.4 copy.54
  96.7 1.7 %select_reduce_fusion.1 = bf16[2,64,16,9]{1,3,2,0:T(8,128)(2,1)S(1)} fusion(f32[2,64,16,32]{1,3,2,0:T(8,128)S(1)} %add_multiply_fusion, s32[2,64,16,9]{1,3,2,0:T(8,128)S(1)} %copy-done.4), kind=kLoop, calls=%fused_computation.2 | loop fusion | flops 1751040 | bytes 372736 | tf_op jit(solution)/shard_map/reduce_sum | solution.py:89
  98.4 7.4 %select_reduce_fusion = bf16[2,64,16,9]{2,3,1,0:T(8,128)(2,1)S(1)} fusion(f32[2,64,16,64]{3,2,1,0:T(8,128)} %copy.54, s32[2,64,16,9]{2,3,1,0:T(8,128)S(1)} %copy.52), kind=kLoop, calls=%fused_computation | loop fusion | flops 3520512 | bytes 634880 | tf_op jit(solution)/shard_map/reduce_sum | solution.py:89
  111.6 1.4 collective-permute-done.9
  113.2 4.7 %collective-permute-done.8 = bf16[2,64,1,384]{3,1,2,0:T(8,128)(2,1)S(1)} collective-permute-done((bf16[2,64,1,384]{3,1,2,0:T(8,128)(2,1)S(1)}, bf16[2,64,1,384]{3,1,2,0:T(8,128)(2,1)S(1)}, u32[]{:S(2)}, u32[]{:S(2)}) %collective-permute-start.8) | collective-permute-done | bytes 98336 | tf_op jit(solution)/shard_map/ppermute | solution.py:18
  118.0 1.7 %pad_maximum_fusion = bf16[2,64,18,384]{3,2,1,0:T(8,128)(2,1)S(1)} fusion(bf16[2,64,1,384]{3,2,1,0:T(2,128)(2,1)S(1)} %copy.66, bf16[2,64,16,128]{3,2,1,0:T(8,128)(2,1)S(1)} %broadcast_bitcast_fusion, bf16[2,64,16,128]{3,2,1,0:T(8,128)(2,1)S(1)} %bitcast.197, bf16[2,64,16,128]{3,2,1,0:T(8,128)(2,1)S(1)} %copy-done.2, bf16[2,64,1,384]{3,2,1,0:T(2,128)(2,1)S(1)} %copy.65), kind=kLoop, calls=%fused_computation.27 | loop fusion | flops 8847360 | bytes 3538944 | tf_op jit(solution)/shard_map/concatenate | solution.py:20
  119.7 2.0 %pad_maximum_fusion.2 = (bf16[2,64,16,384]{3,2,1,0:T(8,128)(2,1)S(1)}, bf16[2,64,16,384]{3,2,1,0:T(8,128)(2,1)S(1)}) fusion(bf16[2,64,1,384]{3,2,1,0:T(2,128)(2,1)S(1)} %copy.66, bf16[2,64,16,128]{3,2,1,0:T(8,128)(2,1)S(1)} %broadcast_bitcast_fusion, bf16[2,64,16,128]{3,2,1,0:T(8,128)(2,1)S(1)} %bitcast.198, bf16[2,64,16,128]{3,2,1,0:T(8,128)(2,1)S(1)} %copy-done.2, ...), kind=kLoop, calls=%fused_computation.31 | loop fusion | flops 12582912 | bytes 4915200 | tf_op jit(solution)/shard_map/concatenate | solution.py:20
  121.7 2.3 %pad_slice_fusion.6 = (bf16[2,64,16,384]{3,2,1,0:T(8,128)(2,1)S(1)}, bf16[2,64,16,384]{3,2,1,0:T(8,128)(2,1)S(1)}, bf16[2,64,16,384]{3,2,1,0:T(8,128)(2,1)S(1)},...) fusion(bf16[2,64,18,384]{3,2,1,0:T(8,128)(2,1)S(1)} %pad_maximum, ...), kind=kLoop, calls=%fused_computation.52 | loop fusion | bytes 11206656 | tf_op jit(solution)/shard_map/slice | solution.py:37
  131.0 4.4 %collective-permute-start.11 = (bf16[2,64,1,128]{3,2,1,0:T(2,128)(2,1)S(1)}, bf16[2,64,1,128]{3,2,1,0:T(2,128)(2,1)S(1)}, u32[]{:S(2)}, u32[]{:S(2)}) collective-permute-start(bf16[2,64,1,128]{3,2,1,0:T(2,128)(2,1)S(1)} %get-tuple-element.24), channel_id=1, source_target_pairs={{1,0},{2,1},{3,2},{4,3},{5,4},{6,5},{7,6},{8,7},{9,8},{10,9},{11,1... | collective-permute-start | bytes 98312 | tf_op jit(solution)/shard_map/ppermute | solution.py:19
  135.5 1.8 %collective-permute-done.10 = bf16[2,64,1,128]{3,2,1,0:T(2,128)(2,1)S(1)} collective-permute-done((bf16[2,64,1,128]{3,2,1,0:T(2,128)(2,1)S(1)}, bf16[2,64,1,128]{3,2,1,0:T(2,128)(2,1)S(1)}, u32[]{:S(2)}, u32[]{:S(2)}) %collective-permute-start.10) | collective-permute-done | bytes 32800 | tf_op jit(solution)/shard_map/ppermute | solution.py:18
  138.2 3.4 %pad_slice_fusion = (bf16[2,64,16,384]{3,2,1,0:T(8,128)(2,1)S(1)}, bf16[2,64,16,384]{3,2,1,0:T(8,128)(2,1)S(1)}, bf16[2,64,16,384]{3,2,1,0:T(8,128)(2,1)S(1)}, b...) fusion(bf16[2,64,18,384]{3,2,1,0:T(8,128)(2,1)S(1)} %pad_maximu, ...), kind=kLoop, calls=%fused_computation.46 | loop fusion | bytes 21233664 | tf_op jit(solution)/shard_map/slice | solution.py:37
  (160 shorter events, 50.7 us)
Async XLA Ops:
  0.6 79.2 %copy-start = (bf16[2,64,16,256]{3,2,1,0:T(8,128)(2,1)S(1)}, bf16[2,64,16,256]{3,2,1,0:T(8,128)(2,1)}, u32[]{:S(2)}) copy-start(bf16[2,64,16,256]{3,2,1,0:T(8,128)(2,1)} %param.11) | copy-start | bytes 3145732
  0.6 10.7 %copy-start.11 = (bf16[2,8,2,128]{3,2,1,0:T(2,128)(2,1)S(1)}, bf16[2,8,2,128]{3,2,1,0:T(2,128)(2,1)}, u32[]{:S(2)}) copy-start(bf16[2,8,2,128]{3,2,1,0:T(2,128)(2,1)} %param.16) | copy-start | bytes 24580
  2.7 8.7 %collective-permute-start.4 = (bf16[2,8,1,256]{3,2,1,0:T(2,128)(2,1)S(1)}, bf16[2,8,1,256]{3,2,1,0:T(2,128)(2,1)S(1)}, u32[]{:S(2)}, u32[]{:S(2)}) collective-permute-start(bf16[2,8,1,256]{3,2,1,0:T(2,128)(2,1)S(1)} %get-tuple-element.46), channel_id=1, source_target_pairs={{0,1},{1,2},{2,3},{3,4},{4,5},{5,6},{6,7},{7,8},{8,9},{9,10},{10,1... | collective-permute-start | bytes 24584 | tf_op jit(solution)/shard_map/ppermute | solution.py:18
  3.2 8.2 %collective-permute-start.5 = (bf16[2,8,1,256]{3,2,1,0:T(2,128)(2,1)S(1)}, bf16[2,8,1,256]{3,2,1,0:T(2,128)(2,1)S(1)}, u32[]{:S(2)}, u32[]{:S(2)}) collective-permute-start(bf16[2,8,1,256]{3,2,1,0:T(2,128)(2,1)S(1)} %get-tuple-element.47), channel_id=1, source_target_pairs={{1,0},{2,1},{3,2},{4,3},{5,4},{6,5},{7,6},{8,7},{9,8},{10,9},{11,1... | collective-permute-start | bytes 24584 | tf_op jit(solution)/shard_map/ppermute | solution.py:19
  8.3 17.1 %collective-permute-start = (bf16[2,64,16,256]{3,2,1,0:T(8,128)(2,1)}, bf16[2,64,16,256]{3,2,1,0:T(8,128)(2,1)S(1)}, u32[]{:S(2)}, u32[]{:S(2)}) collective-permute-start(bf16[2,64,16,256]{3,2,1,0:T(8,128)(2,1)} %param.12), channel_id=1, source_target_pairs={{0,1},{1,2},{2,3},{3,4},{4,5},{5,6},{6,7},{7,8},{8,9},{9,10},{10,1... | collective-permute-start | bytes 3145736 | tf_op jit(solution)/shard_map/ppermute | solution.py:27
  9.8 20.2 %copy-start.14 = (s32[2]{0:T(128)S(1)}, s32[2]{0:T(128)}, u32[]{:S(2)}) copy-start(s32[2]{0:T(128)} %param.13) | copy-start | bytes 28
  25.4 38.5 %copy-start.6 = (bf16[2,64,16,256]{3,2,1,0:T(8,128)(2,1)}, bf16[2,64,16,256]{3,2,1,0:T(8,128)(2,1)S(1)}, u32[]{:S(2)}) copy-start(bf16[2,64,16,256]{3,2,1,0:T(8,128)(2,1)S(1)} %collective-permute-done) | copy-start | bytes 3145732
  25.4 18.3 %collective-permute-start.1 = (bf16[2,64,16,256]{3,2,1,0:T(8,128)(2,1)S(1)}, bf16[2,64,16,256]{3,2,1,0:T(8,128)(2,1)}, u32[]{:S(2)}, u32[]{:S(2)}) collective-permute-start(bf16[2,64,16,256]{3,2,1,0:T(8,128)(2,1)S(1)} %collective-permute-done), channel_id=1, source_target_pairs={{0,1},{1,2},{2,3},{3,4},{4,5},{5,6},{6,7},{7,8},{8,9},{9,10},{10,1... | collective-permute-start | bytes 3145736 | tf_op jit(solution)/shard_map/ppermute | solution.py:27
  25.5 17.0 %collective-permute-start.6 = (bf16[2,8,1,128]{3,2,1,0:T(2,128)(2,1)S(1)}, bf16[2,8,1,128]{3,2,1,0:T(2,128)(2,1)S(1)}, u32[]{:S(2)}, u32[]{:S(2)}) collective-permute-start(bf16[2,8,1,128]{3,2,1,0:T(2,128)(2,1)S(1)} %get-tuple-element.48), channel_id=1, source_target_pairs={{0,1},{1,2},{2,3},{3,4},{4,5},{5,6},{6,7},{7,8},{8,9},{9,10},{10,1... | collective-permute-start | bytes 12296 | tf_op jit(solution)/shard_map/ppermute | solution.py:18
  25.5 16.9 %collective-permute-start.7 = (bf16[2,8,1,128]{3,2,1,0:T(2,128)(2,1)S(1)}, bf16[2,8,1,128]{3,2,1,0:T(2,128)(2,1)S(1)}, u32[]{:S(2)}, u32[]{:S(2)}) collective-permute-start(bf16[2,8,1,128]{3,2,1,0:T(2,128)(2,1)S(1)} %get-tuple-element.49), channel_id=1, source_target_pairs={{1,0},{2,1},{3,2},{4,3},{5,4},{6,5},{7,6},{8,7},{9,8},{10,9},{11,1... | collective-permute-start | bytes 12296 | tf_op jit(solution)/shard_map/ppermute | solution.py:19
  43.7 17.1 %collective-permute-start.2 = (bf16[2,64,16,256]{3,2,1,0:T(8,128)(2,1)}, bf16[2,64,16,256]{3,2,1,0:T(8,128)(2,1)S(1)}, u32[]{:S(2)}, u32[]{:S(2)}) collective-permute-start(bf16[2,64,16,256]{3,2,1,0:T(8,128)(2,1)} %collective-permute-done.1), channel_id=1, source_target_pairs={{0,1},{1,2},{2,3},{3,4},{4,5},{5,6},{6,7},{7,8},{8,9},{9,10},{10,1... | collective-permute-start | bytes 3145736 | tf_op jit(solution)/shard_map/ppermute | solution.py:27
  60.9 16.9 %collective-permute-start.3 = (bf16[2,64,16,256]{3,2,1,0:T(8,128)(2,1)S(1)}, bf16[2,64,16,256]{3,2,1,0:T(8,128)(2,1)S(1)}, u32[]{:S(2)}, u32[]{:S(2)}) collective-permute-start(bf16[2,64,16,256]{3,2,1,0:T(8,128)(2,1)S(1)} %collective-permute-done.2), channel_id=1, source_target_pairs={{0,1},{1,2},{2,3},{3,4},{4,5},{5,6},{6,7},{7,8},{8,9},{9,10},{10,1... | collective-permute-start | bytes 3145736 | tf_op jit(solution)/shard_map/ppermute | solution.py:27
  63.8 14.1 %copy-start.12 = (bf16[2,8,2,128]{3,2,1,0:T(2,128)(2,1)}, bf16[2,8,2,128]{3,2,1,0:T(2,128)(2,1)S(1)}, u32[]{:S(2)}) copy-start(bf16[2,8,2,128]{3,2,1,0:T(2,128)(2,1)S(1)} %fusion.106) | copy-start | bytes 24580
  78.0 1.8 %copy-start.5 = (bf16[2,64,16,256]{3,2,1,0:T(8,128)(2,1)S(1)}, bf16[2,64,16,256]{3,2,1,0:T(8,128)(2,1)}, u32[]{:S(2)}) copy-start(bf16[2,64,16,256]{3,2,1,0:T(8,128)(2,1)} %param.12) | copy-start | bytes 3145732
  98.4 9.0 %copy-start.9 = (s32[2,64,16,9]{1,3,2,0:T(8,128)S(1)}, s32[2,64,16,9]{1,3,2,0:T(8,128)}, u32[]{:S(2)}) copy-start(s32[2,64,16,9]{1,3,2,0:T(8,128)} %get-tuple-element.51) | copy-start | bytes 221188
  105.8 2.5 %copy-start.8 = (s32[2,64,16,9]{1,3,2,0:T(8,128)S(1)}, s32[2,64,16,9]{1,3,2,0:T(8,128)}, u32[]{:S(2)}) copy-start(s32[2,64,16,9]{1,3,2,0:T(8,128)} %get-tuple-element.50) | copy-start | bytes 221188
  107.4 2.6 %copy-start.13 = (bf16[36,128]{1,0:T(8,128)(2,1)S(1)}, bf16[36,128]{1,0:T(8,128)(2,1)}, u32[]{:S(2)}) copy-start(bf16[36,128]{1,0:T(8,128)(2,1)} %param.17) | copy-start | bytes 27652
  108.3 2.1 %copy-start.2 = (bf16[2,64,16,128]{3,2,1,0:T(8,128)(2,1)S(1)}, bf16[2,64,16,128]{3,2,1,0:T(8,128)(2,1)}, u32[]{:S(2)}) copy-start(bf16[2,64,16,128]{3,2,1,0:T(8,128)(2,1)} %param.15) | copy-start | bytes 1572868
  110.8 2.3 %collective-permute-start.9 = (bf16[2,64,1,384]{3,1,2,0:T(8,128)(2,1)S(1)}, bf16[2,64,1,384]{3,1,2,0:T(8,128)(2,1)S(1)}, u32[]{:S(2)}, u32[]{:S(2)}) collective-permute-start(bf16[2,64,1,384]{3,1,2,0:T(8,128)(2,1)S(1)} %copy.64), channel_id=1, source_target_pairs={{1,0},{2,1},{3,2},{4,3},{5,4},{6,5},{7,6},{8,7},{9,8},{10,9},{11,1... | collective-permute-start | bytes 294920 | tf_op jit(solution)/shard_map/ppermute | solution.py:19
  110.9 7.0 %collective-permute-start.8 = (bf16[2,64,1,384]{3,1,2,0:T(8,128)(2,1)S(1)}, bf16[2,64,1,384]{3,1,2,0:T(8,128)(2,1)S(1)}, u32[]{:S(2)}, u32[]{:S(2)}) collective-permute-start(bf16[2,64,1,384]{3,1,2,0:T(8,128)(2,1)S(1)} %copy.63), channel_id=1, source_target_pairs={{0,1},{1,2},{2,3},{3,4},{4,5},{5,6},{6,7},{7,8},{8,9},{9,10},{10,1... | collective-permute-start | bytes 294920 | tf_op jit(solution)/shard_map/ppermute | solution.py:18
  121.7 2.3 %copy-start.3 = (bf16[9,384,256]{2,1,0:T(8,128)(2,1)S(1)}, bf16[9,384,256]{2,1,0:T(8,128)(2,1)}, u32[]{:S(2)}) copy-start(bf16[9,384,256]{2,1,0:T(8,128)(2,1)} %param.18) | copy-start | bytes 5308420
  130.9 6.4 %collective-permute-start.10 = (bf16[2,64,1,128]{3,2,1,0:T(2,128)(2,1)S(1)}, bf16[2,64,1,128]{3,2,1,0:T(2,128)(2,1)S(1)}, u32[]{:S(2)}, u32[]{:S(2)}) collective-permute-start(bf16[2,64,1,128]{3,2,1,0:T(2,128)(2,1)S(1)} %get-tuple-element.23), channel_id=1, source_target_pairs={{0,1},{1,2},{2,3},{3,4},{4,5},{5,6},{6,7},{7,8},{8,9},{9,10},{10,1... | collective-permute-start | bytes 98312 | tf_op jit(solution)/shard_map/ppermute | solution.py:18
  131.0 6.4 %collective-permute-start.11 = (bf16[2,64,1,128]{3,2,1,0:T(2,128)(2,1)S(1)}, bf16[2,64,1,128]{3,2,1,0:T(2,128)(2,1)S(1)}, u32[]{:S(2)}, u32[]{:S(2)}) collective-permute-start(bf16[2,64,1,128]{3,2,1,0:T(2,128)(2,1)S(1)} %get-tuple-element.24), channel_id=1, source_target_pairs={{1,0},{2,1},{3,2},{4,3},{5,4},{6,5},{7,6},{8,7},{9,8},{10,9},{11,1... | collective-permute-start | bytes 98312 | tf_op jit(solution)/shard_map/ppermute | solution.py:19
  138.2 3.4 %copy-start.10 = (bf16[9,384,128]{2,1,0:T(8,128)(2,1)S(1)}, bf16[9,384,128]{2,1,0:T(8,128)(2,1)}, u32[]{:S(2)}) copy-start(bf16[9,384,128]{2,1,0:T(8,128)(2,1)} %param.19) | copy-start | bytes 2654212
  (3 other events, 5.0 us)
where the time goes:
time: 149 us; the launch traced here: 148 us
  waiting for transfers between devices  49.9 us (33%)
  matrix products  32.8 us (22%)
  other arithmetic  24.6 us (17%)
  local copies, waits for them, and re-layouts  23.9 us (16%)
  starting transfers between devices  15.4 us (10%)
  between operations  1.52 us (1%)
    ppermute x4, waiting for transfers between devices, from_behind(): return lax.ppermute(value, axis, pairs)  30.1 us
    dot_general x36, matrix products, convolve(): jnp.dot(window, weight[3 * row_off + col_off], preferred_element_type=jnp...  30 us
    ppermute x4, waiting for transfers between devices, with_halo(): before = lax.ppermute(last, axis, up)  18.3 us
    ppermute x4, starting transfers between devices, with_halo(): after = lax.ppermute(first, axis, down)  14 us
    reduce_sum x4, other arithmetic, pyramid_lookup(): jnp.sum(jnp.where(onehot, volume[..., None, :], 0.0), axis=-1)  10.4 us
    slice x4, local copies, waits for them, and re-layouts, convolve(): padded[:, row_off:row_off + rows_out, col_off:col_off + cols_out, :]  5.84 us
    concatenate x4, other arithmetic, with_halo(): value = jnp.concatenate([before, value, after], axis=dim)  3.82 us
    unnamed x35, local copies, waits for them, and re-layouts  3.61 us
  transfers between devices with their start and end apart: 12, of which 7 were waited for; matrix products, arithmetic and copies ran while one was open for 16% of the time, Pallas kernels for 0%

commit v1 on v0

v1 whole, which is shorter than its diff:
```python
import functools

import jax
import jax.numpy as jnp
import numpy as np
from jax import lax
from jax.experimental import pallas as pl
from jax.experimental.pallas import tpu as pltpu
from jax.sharding import PartitionSpec as P

LEVELS = 4
RADIUS = 4
MAXD = 64
CHUNKS = 2
EDGE = (-2, 15, -1, 16, 0, 17, 0, 0)


def permute(value, target, take=lambda j: True):
    count = lax.axis_size("cols")
    pairs = [(j, target(j) % count) for j in range(count) if take(j)]
    return lax.ppermute(value, "cols", pairs)


def near(value):
    return pltpu.with_memory_space_constraint(value, pltpu.VMEM)


def dot(a, b):
    return jnp.dot(a, b, preferred_element_type=jnp.float32)


def onehot(shape, column):
    r = lax.broadcasted_iota(jnp.int32, shape, 0)
    c = lax.broadcasted_iota(jnp.int32, shape, 1)
    return jnp.where(column(r, c), 1.0, 0.0).astype(jnp.bfloat16)


def call(kernel, name, outs, scratch, args, limit=8, smem=0, **kw):
    vmem = pl.BlockSpec(memory_space=pltpu.VMEM)
    return pl.pallas_call(
        kernel,
        out_shape=tuple(pltpu.VMEM(shape, dtype) for shape, dtype in outs),
        in_specs=[pl.BlockSpec(memory_space=pltpu.SMEM)] * smem + [vmem] * (len(args) - smem),
        out_specs=(vmem,) * len(outs),
        scratch_shapes=scratch,
        compiler_params=pltpu.CompilerParams(vmem_limit_bytes=limit << 20),
        name=name,
        **kw,
    )(*args[:smem], *(near(a) for a in args[smem:]))


def pack_kernel(left, right, state, coarse, disp, to_next, to_prev, far, flat, pooled):
    images, rows, cols, channels = left.shape
    hid = state.shape[-1]
    many = images * rows
    wide = 16 * cols

    def end(q):
        return q + jnp.where(q >= 2, cols - 4, 0)

    ends = onehot((64, wide), lambda r, c: c == (r & 15) * cols + end(r >> 4))
    per_cell = onehot((8, wide), lambda r, c: (r == (c // (8 * cols)) * (cols // 8) + (c % cols) // 8))
    for b in range(many // 16):
        i, r0 = divmod(16 * b, rows)
        here = pl.ds(16 * b, 16)

        def put(ref, slot, value):
            ref[pl.ds(many * slot + 16 * b, 16), :] = value.astype(jnp.bfloat16)

        e = dot(ends, left[i, r0: r0 + 16].reshape(wide, channels))
        put(to_prev, 0, e[:16])
        put(to_prev, 1, e[16:32])
        put(to_next, 0, e[32:48])
        put(to_next, 1, e[48:])
        e = dot(ends, right[i, r0: r0 + 16].reshape(wide, channels))
        put(to_prev, 2, e[:16])
        put(to_prev, 3, e[16:32])
        put(far, 0, e[48:])
        fine = state[i, r0: r0 + 16].reshape(wide, hid)
        e = dot(ends, fine)
        put(to_prev, 4, jnp.concatenate([e[:16], e[16:32]], axis=1))
        put(to_next, 2, jnp.concatenate([e[32:48], e[48:]], axis=1))
        cells = 2 * (cols // 8)
        pooled[pl.ds(cells * b, cells), :] = (dot(per_cell, fine) * (1.0 / 64))[:cells]
    both = jnp.concatenate([coarse[...], pooled[...].astype(jnp.bfloat16)], axis=1)
    flat[...] = both
    to_next[pl.ds(3 * many, flat.shape[0]), :] = both
    to_prev[pl.ds(5 * many, flat.shape[0]), :] = both
    pick = onehot((16, cols), lambda r, c: (c == end(r)) & (r < 4))
    d = lax.dot_general(pick, disp[...].astype(jnp.float32).astype(jnp.bfloat16), (((1,), (1,)), ((), ())),
                        preferred_element_type=jnp.float32)
    d = jnp.concatenate([d, jnp.zeros((16, channels - many), jnp.float32)], axis=1).astype(jnp.bfloat16)
    to_next[pl.ds(3 * many + flat.shape[0], 16), :] = d
    to_prev[pl.ds(5 * many + flat.shape[0], 16), :] = d


def edge_kernel(prev, foll, far, to_next, to_prev, state, disp, left_edge, right_edge, disp24, hid_edge, hid3, wide):
    images, rows, cols, hid = state.shape
    many = images * rows
    channels = prev.shape[1]
    last = prev.shape[0] - 16
    spread8 = onehot((128, 96), lambda r, c: c == (r & 7) * 16 + (r >> 3))
    spread16 = onehot((256, 48), lambda r, c: c == jnp.where((r & 15) == 15, 2, jnp.where((r & 15) < 2, r & 15, 9)) * 16 + (r >> 4))

    own = disp[...].astype(jnp.float32).astype(jnp.bfloat16)
    d24 = dot(own, onehot((cols, cols + 8), lambda r, c: (r == c) | ((c == cols + 1) & (r == cols - 1))
                          | ((c == cols + 4) & (r == 0))))
    for ref, first, slots in ((prev, last, ((2, 0), (3, 2))), (foll, foll.shape[0] - 16, ((0, 3), (1, 5)))):
        rows16 = ref[pl.ds(first, 16), :many]
        place = onehot((16, cols + 8), lambda r, c: ((r == slots[0][0]) & (c == cols + slots[0][1]))
                       | ((r == slots[1][0]) & (c == cols + slots[1][1])))
        d24 += lax.dot_general(rows16, place, (((0,), (0,)), ((), ())), preferred_element_type=jnp.float32)
    d24 = d24.astype(jnp.bfloat16)
    slots = cols + 8
    repeat = onehot((16 * slots, 16), lambda r, c: c == r // slots)
    match = lax.broadcasted_iota(jnp.int32, (16 * slots, slots), 0) % slots \
        == lax.broadcasted_iota(jnp.int32, (16 * slots, slots), 1)
    ones = jnp.ones((slots, 128), jnp.bfloat16)

    for i in range(images):
        for line in (0, rows + 1):
            hid3[i, line] = jnp.zeros((cols, 3 * hid), jnp.bfloat16)
            hid_edge[i, pl.ds(8 * line, 8), :] = jnp.zeros((8, hid), jnp.float32)
    for b in range(many // 16):
        i, r0 = divmod(16 * b, rows)

        def get(ref, slot):
            return ref[pl.ds(many * slot + 16 * b, 16), :]

        e = dot(spread8, jnp.concatenate([get(prev, 0), get(to_next, 1), get(prev, 1), get(foll, 0), get(to_prev, 0),
                                          get(foll, 1)], axis=0))
        left_edge[i, r0: r0 + 16] = e.reshape(16, 8, channels).astype(jnp.bfloat16)
        e = dot(spread16, jnp.concatenate([get(foll, 2), get(foll, 3), get(far, 0)], axis=0))
        right_edge[i, r0: r0 + 16] = e.reshape(16, 16, channels).astype(jnp.bfloat16)
        hp, hn, on, op = get(prev, 2), get(foll, 4), get(to_next, 2), get(to_prev, 4)
        e = dot(spread8, jnp.concatenate([hp[:, :hid], on[:, hid:], hp[:, hid:], hn[:, :hid], op[:, :hid], hn[:, hid:]],
                                         axis=0))
        hid_edge[i, pl.ds(8 + 8 * r0, 128), :] = e
        for k in range(16):
            wide[pl.ds(32 * k + 8, cols), :] = state[i, r0 + k].astype(jnp.float32)
        wide[pl.ds(7, 16, stride=32), :] = hp[:, hid:].astype(jnp.float32)
        wide[pl.ds(8 + cols, 16, stride=32), :] = hn[:, :hid].astype(jnp.float32)
        for k in range(16):
            hid3[i, 1 + r0 + k] = jnp.concatenate(
                [wide[pl.ds(32 * k + 7 + t, cols), :].astype(jnp.bfloat16) for t in range(3)], axis=1)
        spread = jnp.where(match, dot(repeat, d24[16 * b: 16 * b + 16]), 0.0).astype(jnp.bfloat16)
        disp24[i, r0: r0 + 16] = dot(spread, ones).astype(jnp.int32).reshape(16, slots, 128)


def coarse_kernel(behind2, prev, flat, foll, ahead2, gates, cand, fine_gates, fine_cand, new, up_z, up_r, up_q, up_edge,
                  columns, shifted, scratch):
    count = flat.shape[0]
    cells = count // 2
    hid = new.shape[1]
    images = up_edge.shape[0]
    tall = cells // images

    def moved(value, by):
        row = lax.broadcasted_iota(jnp.int32, value.shape, 0) % tall
        if by > 0:
            return jnp.where(row == 0, 0.0, pltpu.roll(value, 1, 0))
        return jnp.where(row == tall - 1, 0.0, pltpu.roll(value, value.shape[0] - 1, 0))

    many3, many5 = prev.shape[0] - 16 - count, foll.shape[0] - 16 - count
    sources = (behind2[...], prev[pl.ds(many3, count), :], flat[...], foll[pl.ds(many5, count), :], ahead2[...])
    for n, source in enumerate(sources):
        for half in range(2):
            columns[half, pl.ds(count * n, count), :] = source[:, half * hid:(half + 1) * hid].astype(jnp.float32)
    state = []
    for n in range(8):
        parts = [columns[half, pl.ds(count * ((n + 1) // 2) + (n + 1) % 2, cells, stride=2), :] for half in range(2)]
        state.append(parts[0])
        both = jnp.concatenate(parts, axis=1)
        for a in range(3):
            value = both if a == 1 else moved(both, 1 - a)
            shifted[a, pl.ds(cells * n, cells), :] = value.astype(jnp.bfloat16)
    acc = jnp.zeros((6 * cells, 2 * hid), jnp.float32)
    for a in range(3):
        for b in range(3):
            acc += dot(shifted[a, pl.ds(cells * b, 6 * cells), :], gates[3 * a + b])
    zr = jax.nn.sigmoid(acc)
    reset = zr[:, hid:] * jnp.concatenate(state[1:7], axis=0)
    reset = reset.astype(jnp.bfloat16).astype(jnp.float32)
    acc = jnp.zeros((4 * cells, hid), jnp.float32)
    for a in range(3):
        value = (reset if a == 1 else moved(reset, 1 - a)).astype(jnp.bfloat16)
        for b in range(3):
            lhs = jnp.concatenate([value[cells * b: cells * (b + 4)],
                                   shifted[a, pl.ds(cells * (b + 1), 4 * cells), hid:]], axis=1)
            acc += dot(lhs, cand[3 * a + b])
    q = jnp.tanh(acc)
    z = zr[cells: 5 * cells, :hid]
    fresh = (1.0 - z) * jnp.concatenate(state[2:6], axis=0) + z * q
    rounded = fresh.astype(jnp.bfloat16)
    for n in range(2):
        scratch[pl.ds(n, cells, stride=2), :] = fresh[cells * (n + 1): cells * (n + 2)]
    new[...] = scratch[...].astype(jnp.bfloat16)

    sums = []
    for b in range(3):
        p = []
        for a in range(3):
            w = jnp.concatenate([fine_gates[3 * a + b, 2 * hid:, :], fine_cand[3 * a + b, 2 * hid:, :]], axis=1)
            p.append(dot(rounded, w))
        low = p[0] + p[1]
        sums.append((moved(p[0], 1) + p[1] + p[2], low + p[2], low + moved(p[2], -1)))

    def at(kind, js):
        return sum(sums[b][kind][cells * (js[b] + 1): cells * (js[b] + 2)] for b in range(3))

    for kind in range(3):
        inner = {0: (-1, 0, 0), 7: (0, 0, 1), 8: (0, 1, 1), 15: (1, 1, 2)}
        flat0, flat1 = at(kind, (0, 0, 0)), at(kind, (1, 1, 1))
        for x in range(16):
            value = at(kind, inner[x]) if x in inner else (flat0 if x < 8 else flat1)
            for part, ref in enumerate((up_z, up_r, up_q)):
                ref[pl.ds(kind * 16 + x, cells, stride=48), :] = value[:, part * hid:(part + 1) * hid]
        for side, js in enumerate(((-1, -1, 0), (1, 2, 2))):
            value = at(kind, js)[:, hid: 2 * hid]
            for i in range(images):
                for u in ((0,), range(1, 7), (7,))[kind]:
                    up_edge[i, pl.ds(side * 8 * tall + u, tall, stride=8), :] = value[tall * i: tall * (i + 1)]


def corr_kernel(sc, left, left_edge, right, right_edge, b4, b2, d2, d0, d4, disp, distance, start, table,
                mot3, mot_edge, wide):
    rows = right.shape[0]
    group = 8
    even = sc[1] == 1
    known = (distance[...] >= 0) & (distance[...] < sc[0])
    scale = jnp.where(known, jnp.float32(left.shape[-1] ** -0.5), 0.0)
    lane = lax.broadcasted_iota(jnp.int32, (24, 128), 1)
    keep = (jnp.where(lane < 72, ~7, ~3), jnp.where(lane < 18, ~1, ~0))
    last_lane = lax.broadcasted_iota(jnp.int32, (8, 128), 1) == 127

    def body(g, carry):
        scores, places = [], ([], [])
        for k in range(group):
            h = g * group + k
            b1 = jnp.where(even, d2[h], d0[h])
            b3 = jnp.where(even, d4[h], d2[h])
            window = jnp.concatenate([b4[h], b3, b2[h], b1, right[h], right_edge[h]], axis=0)
            pixels = jnp.concatenate([left[h], left_edge[h]], axis=0)
            s = lax.dot_general(pixels, window, (((1,), (1,)), ((), ())), preferred_element_type=jnp.float32)
            s = jnp.concatenate([s, jnp.zeros((s.shape[0], 128 - s.shape[1]), jnp.float32)], axis=1)
            ends = jnp.where(last_lane, pltpu.roll(s[16:], 32, 1), s[16:])
            scores.append(s[:16] * scale[:16])
            scores.append(ends * scale[16:])
            d = disp[h]
            for n in range(2):
                places[n].append((start[n] - (d & keep[n])) & 127)
        c = jnp.concatenate(scores, axis=0)
        found = [jnp.take_along_axis(c, jnp.concatenate(p, axis=0), axis=1, mode="promise_in_bounds") for p in places]
        motion = jnp.maximum(dot(jnp.concatenate(found, axis=1).astype(jnp.bfloat16), table[...]), 0.0)
        for k in range(group):
            h = g * group + k
            m = motion[24 * k: 24 * k + 24]
            wide[pl.ds(32 * k + 8, 16), :] = m[:16]
            mot_edge[h] = m[16:]
            wide[pl.ds(32 * k + 7, 1), :] = m[18:19]
            wide[pl.ds(32 * k + 24, 1), :] = m[19:20]
        for k in range(group):
            h = g * group + k
            mot3[h] = jnp.concatenate(
                [wide[pl.ds(32 * k + 7 + b, 16), :].astype(jnp.bfloat16) for b in range(3)], axis=1)
        return carry

    lax.fori_loop(0, rows // group, body, 0)


def motion_chunk(i, k, sc, left, left_edge, right, right_edge, b4, b2, d2, d0, d4, disp, distance, start, table):
    rows = b4.shape[0]
    hid = table.shape[1]

    def kernel(sc, left, left_edge, right, right_edge, b4, b2, d2, d0, d4, disp, *rest):
        here = pl.ds(k * rows, rows)
        corr_kernel(sc, left.at[i, here], left_edge.at[i, here], right.at[i, here], right_edge.at[i, here],
                    b4, b2, d2, d0.at[here], d4, disp.at[i, here], *rest)

    return call(kernel, "motion", [((rows, 16, 3 * hid), jnp.bfloat16), ((rows, 8, hid), jnp.float32)],
                [pltpu.VMEM((8 * 32, hid), jnp.float32)],
                (sc, left, left_edge, right, right_edge, b4, b2, d2, d0, d4, disp, distance, start, table), smem=1)


def gru_kernel(count, hid3, state, hid_edge, *refs):
    mots, edges = refs[:count], refs[count:2 * count]
    (up_z, up_r, up_q, up_edge, gates, cand, out, mot, mot_edge, z_keep, wide, res3) = refs[2 * count:]
    rows = state.shape[0]
    hid = state.shape[-1]
    each = rows // count
    zero = jnp.zeros((1, 16, 3 * hid), jnp.bfloat16)
    mot[0:1] = zero
    mot[rows + 1: rows + 2] = zero
    res3[0:1] = zero
    res3[rows + 1: rows + 2] = zero
    mot_edge[0:8] = jnp.zeros((8, hid), jnp.float32)
    mot_edge[8 * (rows + 1): 8 * (rows + 2)] = jnp.zeros((8, hid), jnp.float32)
    for k in range(count):
        mot[1 + each * k: 1 + each * (k + 1)] = mots[k][...]
        mot_edge[8 + 8 * each * k: 8 + 8 * each * (k + 1)] = edges[k][...].reshape(8 * each, hid)
    block = 16

    acc = up_edge[...]
    for a in range(3):
        for b in range(3):
            pieces = [
                jnp.concatenate([src[pl.ds(8 * a + 2 * b + side, rows, stride=8), :] for side in range(2)], axis=0)
                for src in (hid_edge, mot_edge)]
            acc += dot(jnp.concatenate(pieces, axis=1).astype(jnp.bfloat16),
                       gates[3 * a + b, 0: 2 * hid, hid: 2 * hid])
    centre = jnp.concatenate([hid_edge[pl.ds(8 + 2 + side, rows, stride=8), :] for side in range(2)], axis=0)
    reset = jax.nn.sigmoid(acc) * centre
    wide[pl.ds(7, rows, stride=32), :] = reset[:rows]
    wide[pl.ds(24, rows, stride=32), :] = reset[rows:]

    def taps(first, weights, source, r0, start):
        acc = start
        for a in range(3):
            one = source[pl.ds(r0 + a, block)].reshape(block * 16, 3 * hid)
            two = mot[pl.ds(r0 + a, block)].reshape(block * 16, 3 * hid)
            for b in range(3):
                lhs = jnp.concatenate([one[:, b * hid:(b + 1) * hid], two[:, b * hid:(b + 1) * hid]], axis=1)
                acc += dot(lhs, weights[3 * a + b, 0: 2 * hid, :])
        return acc

    def upsampled(g, *refs):
        parts = []
        for cell in range(block // 8):
            kinds = [jnp.concatenate([ref[g * (block // 8) + cell, kind] for ref in refs], axis=1) for kind in range(3)]
            parts += [kinds[0]] + [kinds[1]] * 6 + [kinds[2]]
        return jnp.concatenate(parts, axis=0)

    def gate_body(g, carry):
        r0 = g * block
        acc = taps(0, gates, hid3, r0, upsampled(g, up_z, up_r))
        both = jax.nn.sigmoid(acc)
        h = state[pl.ds(r0, block)].reshape(block * 16, hid).astype(jnp.float32)
        z_keep[pl.ds(r0 * 16, block * 16), :] = both[:, :hid]
        reset = both[:, hid:] * h
        for k in range(block):
            wide[pl.ds(pl.multiple_of((r0 + k) * 32, 32) + 8, 16), :] = reset[16 * k: 16 * k + 16]
        for k in range(block):
            res3[r0 + k + 1] = jnp.concatenate(
                [wide[pl.ds(pl.multiple_of((r0 + k) * 32, 32) + 7 + b, 16), :].astype(jnp.bfloat16)
                 for b in range(3)], axis=1)
        return carry

    lax.fori_loop(0, rows // block, gate_body, 0)

    def cand_body(g, carry):
        r0 = g * block
        q = jnp.tanh(taps(0, cand, res3, r0, upsampled(g, up_q)))
        h = state[pl.ds(r0, block)].reshape(block * 16, hid).astype(jnp.float32)
        z = z_keep[pl.ds(r0 * 16, block * 16), :]
        new = (1.0 - z) * h + z * q
        out[pl.ds(r0, block)] = new.astype(jnp.bfloat16).reshape(block, 16, hid)
        return carry

    lax.fori_loop(0, rows // block, cand_body, 0)


def fine_gru(i, before, hid3, state, hid_edge, mots, edges, ups, up_edge, gates, cand):
    images, rows, cols, hid = state.shape
    count = len(mots)
    vmem = pl.BlockSpec(memory_space=pltpu.VMEM)
    tall = rows // 8

    def kernel(hid3, state, hid_edge, *refs):
        refs = list(refs)
        if before is not None:
            refs = refs[1:]
        for n in range(3):
            refs[2 * count + n] = refs[2 * count + n].at[pl.ds(tall * i, tall)]
        refs[2 * count + 3] = refs[2 * count + 3].at[i]
        gru_kernel(count, hid3.at[i], state.at[i], hid_edge.at[i], *refs)

    args = [hid3, state, hid_edge]
    rest = [*mots, *edges, *(u.reshape(-1, 3, 16, hid) for u in ups), up_edge, gates, cand]
    first = [] if before is None else [before]
    return pl.pallas_call(
        kernel,
        grid=(1,),
        out_shape=jax.ShapeDtypeStruct(state.shape, jnp.bfloat16),
        in_specs=[vmem] * 3 + [pl.BlockSpec(memory_space=pl.ANY)] * len(first) + [vmem] * len(rest),
        out_specs=pl.BlockSpec((None, rows, cols, hid), lambda _: (i, 0, 0, 0)),
        input_output_aliases={3: 0} if first else {},
        compiler_params=pltpu.CompilerParams(vmem_limit_bytes=16 << 20),
        scratch_shapes=[pltpu.VMEM((rows + 2, 16, 3 * hid), jnp.bfloat16),
                        pltpu.VMEM((8 * (rows + 2), hid), jnp.float32),
                        pltpu.VMEM((rows * 16, hid), jnp.float32),
                        pltpu.VMEM((rows * 32, hid), jnp.float32),
                        pltpu.VMEM((rows + 2, 16, 3 * hid), jnp.bfloat16)],
        name="fine_gru",
    )(*(near(v) for v in args), *first, *(near(v) for v in rest))


def lookup_places():
    level = np.full((2, 128), -1)
    offset = np.zeros((2, 128), np.int64)
    for group, first, k in ((0, 0, 3), (0, 72, 2), (1, 0, 1), (1, 18, 0)):
        count = (2 * RADIUS + 1) << k
        level[group, first: first + count] = k
        offset[group, first: first + count] = ((RADIUS + 1) << k) - 1 - np.arange(count)
    tap = np.where(level >= 0, (offset >> np.maximum(level, 0)) + RADIUS, 0)
    return level, offset, tap


def lookup_table(motion_weight):
    level, _, tap = (v.reshape(-1) for v in lookup_places())
    rows = np.maximum(level, 0) * (2 * RADIUS + 1) + tap
    pick = np.zeros((level.size, motion_weight.shape[0]), np.float32)
    pick[np.arange(level.size), rows] = np.where(level >= 0, 0.5 ** np.maximum(level, 0), 0.0)
    return dot(jnp.asarray(pick.astype(jnp.bfloat16)), motion_weight).astype(jnp.bfloat16)


def local(left_feat, right_feat, bounds, disparity, hidden_fine, hidden_coarse, motion_weight,
          fine_gates, fine_candidate, coarse_gates, coarse_candidate):
    images, rows, cols, channels = left_feat.shape
    hid = hidden_fine.shape[-1]
    even = 1 - lax.rem(lax.axis_index("cols"), 2)
    many = images * rows
    each = rows // CHUNKS
    keys = [(i, k) for i in range(images) for k in range(CHUNKS)]
    bf16, f32 = jnp.bfloat16, jnp.float32

    b4, b2, d2, d4 = {}, {}, {}, {}
    for i, k in keys:
        b4[i, k] = permute(right_feat[i, k * each:(k + 1) * each], lambda j: j + 4)
    d0 = [permute(right_feat[i], lambda j: j + 1, lambda j: j % 2 == 0) for i in range(images)]
    straight = [permute(right_feat[i], lambda j: j + 2, lambda j: j % 4 < 2) for i in range(images)]

    disp = disparity.reshape(many, cols)
    cells = hidden_coarse.shape[1] * hidden_coarse.shape[2] * images
    to_next, to_prev, to_far, flat = call(
        pack_kernel, "pack",
        [((3 * many + cells + 16, channels), bf16), ((5 * many + cells + 16, channels), bf16), ((many, channels), bf16),
         ((cells, channels), bf16)],
        [pltpu.VMEM((cells, hid), f32)],
        (left_feat, right_feat, hidden_fine, hidden_coarse.reshape(-1, hid), disp))
    prev = permute(to_next, lambda j: j + 1)
    foll = permute(to_prev, lambda j: j - 1)
    far = permute(to_far, lambda j: j + 5)
    behind2 = permute(flat, lambda j: j + 2)
    ahead2 = permute(flat, lambda j: j - 2)

    for i, k in keys:
        relayed = permute(b4[i, k], lambda j: j - 2, lambda j: j % 4 >= 2)
        b2[i, k] = straight[i][k * each:(k + 1) * each] + relayed
        d4[i, k] = permute(b4[i, k], lambda j: j - 1, lambda j: j % 2 == 1)
        d2[i, k] = permute(b2[i, k], lambda j: j ^ 1)

    left_edge, right_edge, disp24, hid_edge, hid3 = call(
        edge_kernel, "edges",
        [((images, rows, 8, channels), bf16), ((images, rows, 16, channels), bf16), ((images, rows, 24, 128), jnp.int32),
         ((images, 8 * (rows + 2), hid), f32), ((images, rows + 2, cols, 3 * hid), bf16)],
        [pltpu.VMEM((16 * 32, hid), f32)],
        (prev, foll, far, to_next, to_prev, hidden_fine, disp))
    new, *ups, up_edge = call(
        coarse_kernel, "coarse",
        [((cells, hid), bf16)] + [((cells // 2 * 48, hid), f32)] * 3 + [((images, 2 * rows, hid), f32)],
        [pltpu.VMEM((2, 5 * cells, hid), f32), pltpu.VMEM((3, 4 * cells, 2 * hid), bf16), pltpu.VMEM((cells, hid), f32)],
        (behind2, prev, flat, foll, ahead2, coarse_gates, coarse_candidate, fine_gates, fine_candidate))
    coarse_new = new.reshape(hidden_coarse.shape)

    where_x = np.array(list(range(cols)) + list(EDGE), np.int32)[:, None]
    lane = np.arange(128, dtype=np.int32)[None]
    column_of = np.where(lane == 127, -65, np.where(lane < 82, lane - 64, 1000))
    distance = where_x - column_of
    distance = jnp.asarray(np.where((distance >= 0) & (distance < MAXD), distance, -1).astype(np.int32))
    _, offset, _ = lookup_places()
    start = jnp.asarray((where_x + 64 - offset[:, None, :]).astype(np.int32))
    table = lookup_table(motion_weight)

    fine = None
    for i in range(images):
        sc = jnp.stack([bounds[i], even]).astype(jnp.int32)
        done = [motion_chunk(i, k, sc, left_feat, left_edge, right_feat, right_edge, b4[i, k], b2[i, k], d2[i, k], d0[i],
                             d4[i, k], disp24, distance, start, table) for k in range(CHUNKS)]
        fine = fine_gru(i, fine, hid3, hidden_fine, hid_edge, [m for m, _ in done], [e for _, e in done],
                        ups, up_edge, fine_gates, fine_candidate)
    return (fine, coarse_new)


def solution(mesh):
    return jax.shard_map(
        local,
        mesh=mesh,
        in_specs=(
            P("groups", None, "cols", None),
            P("groups", None, "cols", None),
            P("groups"),
            P("groups", None, "cols"),
            P("groups", None, "cols", None),
            P("groups", None, "cols", None),
            P(),
            P(),
            P(),
            P(),
            P(),
        ),
        out_specs=(P("groups", None, "cols", None), P("groups", None, "cols", None)),
        check_vma=False,
    )
```

time: 149 us -> 101 us (0.68)
  waiting for transfers between devices: 49.9 us -> 12 us
  starting transfers between devices: 15.4 us -> 48.1 us
  matrix products: 32.8 us -> 0.98 us
  Pallas kernels: 0 us -> 26 us
  other arithmetic: 24.6 us -> 3.91 us
  local copies, waits for them, and re-layouts: 23.9 us -> 8.66 us
    ppermute x12 -> x25, waiting for transfers between devices: 49.9 us -> 12 us  [permute(): return lax.ppermute(value, 'cols', pairs)]
    ppermute x12 -> x25, starting transfers between devices: 15.4 us -> 48.1 us  [permute(): return lax.ppermute(value, 'cols', pairs)]
    dot_general x38 -> x1, matrix products: 32.8 us -> 0.98 us  [dot(): return jnp.dot(a, b, preferred_element_type=jnp.float32)]
    pallas_call x0 -> x9, Pallas kernels: none -> 26 us  [the longest x7 15.7 us: call(): pl.pallas_call(kernel, out_shape=tuple((pltpu.VMEM(shape, dtype) for shap...]
    reduce_sum x5 -> x0, other arithmetic: 11.6 us -> none  [the longest x4 10.4 us: pyramid_lookup(): jnp.sum(jnp.where(onehot, volume[..., None, :], 0.0), axis=-1)]
    slice x17 -> x1, local copies, waits for them, and re-layouts: 10.9 us -> 0.58 us  [local(): sc = jnp.stack([bounds[i], even]).astype(jnp.int32)]
    concatenate x7 -> x0, other arithmetic: 5.54 us -> none  [the longest x4 3.82 us: with_halo(): value = jnp.concatenate([before, value, after], axis=dim)]
    unnamed x35 -> x46, local copies, waits for them, and re-layouts: 3.61 us -> 6.98 us
  transfers between devices with their start and end apart: 12 -> 25, of which waited for: 7 -> 4; matrix products, arithmetic and copies ran while one was open for 16% -> 7% of each run, Pallas kernels for 0% -> 17%
where the time goes in v1:
time: 101 us
  starting transfers between devices  48.1 us (48%)
  Pallas kernels  26 us (26%)
  waiting for transfers between devices  12 us (12%)
  local copies, waits for them, and re-layouts  8.66 us (9%)
  other arithmetic  3.91 us (4%)
  between operations  1.05 us (1%)
    ppermute x25, starting transfers between devices, permute(): return lax.ppermute(value, 'cols', pairs)  48.1 us
    pallas_call x7, Pallas kernels, call(): pl.pallas_call(kernel, out_shape=tuple((pltpu.VMEM(shape, dtype) for shap...  15.7 us
    ppermute x25, waiting for transfers between devices, permute(): return lax.ppermute(value, 'cols', pairs)  12 us
    pallas_call x2, Pallas kernels, fine_gru(): pl.pallas_call(kernel, grid=(1,), out_shape=jax.ShapeDtypeStruct(state.sh...  10.3 us
    unnamed x46, local copies, waits for them, and re-layouts  6.98 us
    add x2, other arithmetic, local(): b2[i, k] = straight[i][k * each:(k + 1) * each] + relayed  2.49 us
  transfers between devices with their start and end apart: 25, of which 4 were waited for; matrix products, arithmetic and copies ran while one was open for 7% of the time, Pallas kernels for 17%

profile of v1, /device:TPU:0, one launch (start us, length us, event | category | flops | bytes accessed | tf_op | source)
XLA Modules:
  0.0 100.7 jit_solution(2889794237459637139)
XLA Ops:
  6.2 3.0 %collective-permute-start.13 = (bf16[32,256]{1,0:T(8,128)(2,1)S(1)}, bf16[32,256]{1,0:T(8,128)(2,1)S(1)}, u32[]{:S(2)}, u32[]{:S(2)}) collective-permute-start(bf16[32,256]{1,0:T(8,128)(2,1)S(1)} %get-tuple-element.36.flat), channel_id=1, source_target_pairs={{0,2},{1,3},{2,4},{3,5},{4,6},{5,7},{6,8},{7,9},{8,10},{9,11},{10,... | collective-permute-start | bytes 49160 | tf_op jit(solution)/shard_map/ppermute | solution.py:21
  9.2 3.1 %collective-permute-start.14 = (bf16[32,256]{1,0:T(8,128)(2,1)S(1)}, bf16[32,256]{1,0:T(8,128)(2,1)S(1)}, u32[]{:S(2)}, u32[]{:S(2)}) collective-permute-start(bf16[32,256]{1,0:T(8,128)(2,1)S(1)} %get-tuple-element.36.flat), channel_id=1, source_target_pairs={{0,14},{1,15},{2,0},{3,1},{4,2},{5,3},{6,4},{7,5},{8,6},{9,7},{10,... | collective-permute-start | bytes 49160 | tf_op jit(solution)/shard_map/ppermute | solution.py:21
  12.6 1.6 %collective-permute-start.15 = (bf16[32,16,256]{2,1,0:T(8,128)(2,1)S(1)}, bf16[32,16,256]{2,1,0:T(8,128)(2,1)S(1)}, u32[]{:S(2)}, u32[]{:S(2)}) collective-permute-start(bf16[32,16,256]{2,1,0:T(8,128)(2,1)S(1)} %get-tuple-element.47), channel_id=1, source_target_pairs={{0,4},{1,5},{2,6},{3,7},{4,8},{5,9},{6,10},{7,11},{8,12},{9,13},{1... | collective-permute-start | bytes 786440 | tf_op jit(solution)/shard_map/ppermute | solution.py:21
  14.3 1.6 %collective-permute-start.21 = (bf16[32,16,256]{2,1,0:T(8,128)(2,1)S(1)}, bf16[32,16,256]{2,1,0:T(8,128)(2,1)}, u32[]{:S(2)}, u32[]{:S(2)}) collective-permute-start(bf16[32,16,256]{2,1,0:T(8,128)(2,1)S(1)} %get-tuple-element.46), channel_id=1, source_target_pairs={{0,4},{1,5},{2,6},{3,7},{4,8},{5,9},{6,10},{7,11},{8,12},{9,13},{1... | collective-permute-start | bytes 786440 | tf_op jit(solution)/shard_map/ppermute | solution.py:21
  18.5 6.4 %collective-permute-start.3 = (bf16[32,16,256]{2,1,0:T(8,128)(2,1)S(1)}, bf16[32,16,256]{2,1,0:T(8,128)(2,1)}, u32[]{:S(2)}, u32[]{:S(2)}) collective-permute-start(bf16[32,16,256]{2,1,0:T(8,128)(2,1)S(1)} %get-tuple-element.49), channel_id=1, source_target_pairs={{0,4},{1,5},{2,6},{3,7},{4,8},{5,9},{6,10},{7,11},{8,12},{9,13},{1... | collective-permute-start | bytes 786440 | tf_op jit(solution)/shard_map/ppermute | solution.py:21
  24.8 2.1 %collective-permute-start.4 = (bf16[64,16,256]{2,1,0:T(8,128)(2,1)}, bf16[64,16,256]{2,1,0:T(8,128)(2,1)}, u32[]{:S(2)}, u32[]{:S(2)}) collective-permute-start(bf16[64,16,256]{2,1,0:T(8,128)(2,1)} %get-tuple-element.51), channel_id=1, source_target_pairs={{0,2},{1,3},{4,6},{5,7},{8,10},{9,11},{12,14},{13,15},{16,18},{17,... | collective-permute-start | bytes 1572872 | tf_op jit(solution)/shard_map/ppermute | solution.py:21
  26.9 1.6 %collective-permute-start.1 = (bf16[688,256]{1,0:T(8,128)(2,1)S(1)}, bf16[688,256]{1,0:T(8,128)(2,1)S(1)}, u32[]{:S(2)}, u32[]{:S(2)}) collective-permute-start(bf16[688,256]{1,0:T(8,128)(2,1)S(1)} %get-tuple-element.25.to_prev), channel_id=1, source_target_pairs={{0,15},{1,0},{2,1},{3,2},{4,3},{5,4},{6,5},{7,6},{8,7},{9,8},{10,9... | collective-permute-start | bytes 1056776 | tf_op jit(solution)/shard_map/ppermute | solution.py:21
  28.5 6.8 %collective-permute-done.9.b4 = bf16[32,16,256]{2,1,0:T(8,128)(2,1)S(1)} collective-permute-done((bf16[32,16,256]{2,1,0:T(8,128)(2,1)S(1)}, bf16[32,16,256]{2,1,0:T(8,128)(2,1)S(1)}, u32[]{:S(2)}, u32[]{:S(2)}) %collective-permute-start.9) | collective-permute-done | bytes 262176 | tf_op jit(solution)/shard_map/ppermute | solution.py:21
  36.6 5.4 %collective-permute-start.16 = (bf16[64,16,256]{2,1,0:T(8,128)(2,1)}, bf16[64,16,256]{2,1,0:T(8,128)(2,1)}, u32[]{:S(2)}, u32[]{:S(2)}) collective-permute-start(bf16[64,16,256]{2,1,0:T(8,128)(2,1)} %get-tuple-element.50), channel_id=1, source_target_pairs={{0,2},{1,3},{4,6},{5,7},{8,10},{9,11},{12,14},{13,15},{16,18},{17,... | collective-permute-start | bytes 1572872 | tf_op jit(solution)/shard_map/ppermute | solution.py:21
  43.3 1.3 %collective-permute-start.17 = (bf16[32,16,256]{2,1,0:T(8,128)(2,1)S(1)}, bf16[32,16,256]{2,1,0:T(8,128)(2,1)}, u32[]{:S(2)}, u32[]{:S(2)}) collective-permute-start(bf16[32,16,256]{2,1,0:T(8,128)(2,1)S(1)} %collective-permute-done.15.b4), channel_id=1, source_target_pairs={{2,0},{3,1},{6,4},{7,5},{10,8},{11,9},{14,12},{15,13},{18,16},{19,... | collective-permute-start | bytes 786440 | tf_op jit(solution)/shard_map/ppermute | solution.py:21
  47.2 4.0 %collective-permute-done.5 = bf16[32,16,256]{2,1,0:T(8,128)(2,1)} collective-permute-done((bf16[32,16,256]{2,1,0:T(8,128)(2,1)}, bf16[32,16,256]{2,1,0:T(8,128)(2,1)}, u32[]{:S(2)}, u32[]{:S(2)}) %collective-permute-start.5) | collective-permute-done | bytes 262176 | tf_op jit(solution)/shard_map/ppermute | solution.py:21
  51.2 6.4 %collective-permute-start.7 = (bf16[64,16,256]{2,1,0:T(8,128)(2,1)}, bf16[64,16,256]{2,1,0:T(8,128)(2,1)S(1)}, u32[]{:S(2)}, u32[]{:S(2)}) collective-permute-start(bf16[64,16,256]{2,1,0:T(8,128)(2,1)} %get-tuple-element.51), channel_id=1, source_target_pairs={{0,1},{2,3},{4,5},{6,7},{8,9},{10,11},{12,13},{14,15},{16,17},{18,... | collective-permute-start | bytes 1572872 | tf_op jit(solution)/shard_map/ppermute | solution.py:21
  57.6 1.3 %collective-permute-start.12 = (bf16[32,16,256]{2,1,0:T(8,128)(2,1)}, bf16[32,16,256]{2,1,0:T(8,128)(2,1)S(1)}, u32[]{:S(2)}, u32[]{:S(2)}) collective-permute-start(bf16[32,16,256]{2,1,0:T(8,128)(2,1)} %copy-done.12), channel_id=1, source_target_pairs={{1,0},{3,2},{5,4},{7,6},{9,8},{11,10},{13,12},{15,14},{17,16},{19,... | collective-permute-start | bytes 786440 | tf_op jit(solution)/shard_map/ppermute | solution.py:21
  62.4 2.0 %collective-permute-start.11 = (bf16[32,16,256]{2,1,0:T(8,128)(2,1)S(1)}, bf16[32,16,256]{2,1,0:T(8,128)(2,1)S(1)}, u32[]{:S(2)}, u32[]{:S(2)}) collective-permute-start(bf16[32,16,256]{2,1,0:T(8,128)(2,1)S(1)} %get-tuple-element.54.b2), channel_id=1, source_target_pairs={{0,1},{1,0},{2,3},{3,2},{4,5},{5,4},{6,7},{7,6},{8,9},{9,8},{10,11... | collective-permute-start | bytes 786440 | tf_op jit(solution)/shard_map/ppermute | solution.py:21
  65.1 2.4 %collective-permute-start.19 = (bf16[64,16,256]{2,1,0:T(8,128)(2,1)}, bf16[64,16,256]{2,1,0:T(8,128)(2,1)S(1)}, u32[]{:S(2)}, u32[]{:S(2)}) collective-permute-start(bf16[64,16,256]{2,1,0:T(8,128)(2,1)} %get-tuple-element.50), channel_id=1, source_target_pairs={{0,1},{2,3},{4,5},{6,7},{8,9},{10,11},{12,13},{14,15},{16,17},{18,... | collective-permute-start | bytes 1572872 | tf_op jit(solution)/shard_map/ppermute | solution.py:21
  68.8 1.3 %collective-permute-start.24 = (bf16[32,16,256]{2,1,0:T(8,128)(2,1)}, bf16[32,16,256]{2,1,0:T(8,128)(2,1)S(1)}, u32[]{:S(2)}, u32[]{:S(2)}) collective-permute-start(bf16[32,16,256]{2,1,0:T(8,128)(2,1)} %collective-permute-done.21.b4), channel_id=1, source_target_pairs={{1,0},{3,2},{5,4},{7,6},{9,8},{11,10},{13,12},{15,14},{17,16},{19,... | collective-permute-start | bytes 786440 | tf_op jit(solution)/shard_map/ppermute | solution.py:21
  74.5 1.3 %coarse.1 = (bf16[32,128]{1,0:T(8,128)(2,1)S(1)}, f32[768,128]{1,0:T(8,128)S(1)}, f32[768,128]{1,0:T(8,128)S(1)}, f32[768,128]{1,0:T(8,128)S(1)}, f32[2,128,128]{2,1,0:T(8,128)S(1)}) custom-call(bf16[32,256]{1,0:T(8,128)(2,1)S(1)} %collective-permute-done.13.behind2, bf16[432,256]{1,0:T(8,128)(2,1)S(1)} %collective-permute-done.prev, ...), custom_call_target="tpu_custom_call" | custom-call | tf_op jit(solution)/shard_map/coarse/pallas_call | solution.py:40
  76.5 2.0 %edges.1 = (bf16[2,64,8,256]{3,2,1,0:T(8,128)(2,1)S(1)}, bf16[2,64,16,256]{3,2,1,0:T(8,128)(2,1)S(1)}, s32[2,64,24,128]{3,2,1,0:T(8,128)S(1)}, f32[2,528,128]{2,1,0:T(8,128)S(1)}, bf16[2,66,16,384]{3,2,1,0:T(8,128)(2,1)S(1)}) custom-call(bf16[432,256]{1,0:T(8,128)(2,1)S(1)} %collective-permute-done.prev, bf16[688,256]{1,0:T(8,128)(2,1)S(1)} %collective-permute-done.1.foll, ...), custom_call_target="tpu_custom_call" | custom-call | tf_op jit(solution)/shard_map/edges/pallas_call | solution.py:40
  78.6 2.7 %motion.5 = (bf16[32,16,384]{2,1,0:T(8,128)(2,1)S(1)}, f32[32,8,128]{2,1,0:T(8,128)S(1)}) custom-call(s32[2]{0:T(128)S(1)} %pad_add_fusion.sc, bf16[2,64,16,256]{3,2,1,0:T(8,128)(2,1)S(1)} %copy-done.4, bf16[2,64,8,256]{3,2,1,0:T(8,128)(2,1)S(1)} %get-tuple-element.29.left_edge, bf16[2,64,16,256]{3,2,1,0:T(8,128)(2,1)S(1)} %copy-done.2, ...), custom_call_target="tpu_custom_call" | custom-call | tf_op jit(solution)/shard_map/motion/pallas_call | solution.py:40
  81.3 3.2 %motion.4 = (bf16[32,16,384]{2,1,0:T(8,128)(2,1)S(1)}, f32[32,8,128]{2,1,0:T(8,128)S(1)}) custom-call(s32[2]{0:T(128)S(1)} %pad_add_fusion.sc, bf16[2,64,16,256]{3,2,1,0:T(8,128)(2,1)S(1)} %copy-done.4, bf16[2,64,8,256]{3,2,1,0:T(8,128)(2,1)S(1)} %get-tuple-element.29.left_edge, bf16[2,64,16,256]{3,2,1,0:T(8,128)(2,1)S(1)} %copy-done.2, ...), custom_call_target="tpu_custom_call" | custom-call | tf_op jit(solution)/shard_map/motion/pallas_call | solution.py:40
  84.5 5.2 %fine_gru.2.refs_0_ = bf16[2,64,16,128]{3,2,1,0:T(8,128)(2,1)} custom-call(bf16[2,66,16,384]{3,2,1,0:T(8,128)(2,1)S(1)} %get-tuple-element.27.hid3, bf16[2,64,16,128]{3,2,1,0:T(8,128)(2,1)S(1)} %copy-done.7, f32[2,528,128]{2,1,0:T(8,128)S(1)} %get-tuple-element.28.hid_edge, bf16[32,16,384]{2,1,0:T(8,128)(2,1)S(1)} %get-tuple-element.32.refs_0_, ...), custom_call_target="tpu_custom_call" | custom-call | tf_op jit(solution)/shard_map/fine_gru/pallas_call | solution.py:380
  89.7 3.1 %motion.7 = (bf16[32,16,384]{2,1,0:T(8,128)(2,1)S(1)}, f32[32,8,128]{2,1,0:T(8,128)S(1)}) custom-call(s32[2]{0:T(128)S(1)} %pad_add_fusion.1.sc, bf16[2,64,16,256]{3,2,1,0:T(8,128)(2,1)S(1)} %copy-done.4, bf16[2,64,8,256]{3,2,1,0:T(8,128)(2,1)S(1)} %get-tuple-element.29.left_edge, bf16[2,64,16,256]{3,2,1,0:T(8,128)(2,1)S(1)} %copy-done.2, ...), custom_call_target="tpu_custom_call" | custom-call | tf_op jit(solution)/shard_map/motion/pallas_call | solution.py:40
  92.8 2.7 %motion.6 = (bf16[32,16,384]{2,1,0:T(8,128)(2,1)S(1)}, f32[32,8,128]{2,1,0:T(8,128)S(1)}) custom-call(s32[2]{0:T(128)S(1)} %pad_add_fusion.1.sc, bf16[2,64,16,256]{3,2,1,0:T(8,128)(2,1)S(1)} %copy-done.4, bf16[2,64,8,256]{3,2,1,0:T(8,128)(2,1)S(1)} %get-tuple-element.29.left_edge, bf16[2,64,16,256]{3,2,1,0:T(8,128)(2,1)S(1)} %copy-done.2, ...), custom_call_target="tpu_custom_call" | custom-call | tf_op jit(solution)/shard_map/motion/pallas_call | solution.py:40
  95.6 5.2 %fine_gru.3 = bf16[2,64,16,128]{3,2,1,0:T(8,128)(2,1)} custom-call(bf16[2,66,16,384]{3,2,1,0:T(8,128)(2,1)S(1)} %get-tuple-element.27.hid3, bf16[2,64,16,128]{3,2,1,0:T(8,128)(2,1)S(1)} %copy-done.7, f32[2,528,128]{2,1,0:T(8,128)S(1)} %get-tuple-element.28.hid_edge, bf16[2,64,16,128]{3,2,1,0:T(8,128)(2,1)} %fine_gru.2.refs_0_, ...), custom_call_target="tpu_custom_call", output_to_operand_aliasing={{}: (3, {})} | custom-call | tf_op jit(solution)/shard_map/fine_gru/pallas_call | solution.py:380
  (89 shorter events, 24.0 us)
Async XLA Ops:
  6.2 8.1 %collective-permute-start.13 = (bf16[32,256]{1,0:T(8,128)(2,1)S(1)}, bf16[32,256]{1,0:T(8,128)(2,1)S(1)}, u32[]{:S(2)}, u32[]{:S(2)}) collective-permute-start(bf16[32,256]{1,0:T(8,128)(2,1)S(1)} %get-tuple-element.36.flat), channel_id=1, source_target_pairs={{0,2},{1,3},{2,4},{3,5},{4,6},{5,7},{6,8},{7,9},{8,10},{9,11},{10,... | collective-permute-start | bytes 49160 | tf_op jit(solution)/shard_map/ppermute | solution.py:21
  9.2 6.6 %collective-permute-start.14 = (bf16[32,256]{1,0:T(8,128)(2,1)S(1)}, bf16[32,256]{1,0:T(8,128)(2,1)S(1)}, u32[]{:S(2)}, u32[]{:S(2)}) collective-permute-start(bf16[32,256]{1,0:T(8,128)(2,1)S(1)} %get-tuple-element.36.flat), channel_id=1, source_target_pairs={{0,14},{1,15},{2,0},{3,1},{4,2},{5,3},{6,4},{7,5},{8,6},{9,7},{10,... | collective-permute-start | bytes 49160 | tf_op jit(solution)/shard_map/ppermute | solution.py:21
  12.3 12.5 %collective-permute-start = (bf16[432,256]{1,0:T(8,128)(2,1)S(1)}, bf16[432,256]{1,0:T(8,128)(2,1)S(1)}, u32[]{:S(2)}, u32[]{:S(2)}) collective-permute-start(bf16[432,256]{1,0:T(8,128)(2,1)S(1)} %get-tuple-element.24.to_next), channel_id=1, source_target_pairs={{0,1},{1,2},{2,3},{3,4},{4,5},{5,6},{6,7},{7,8},{8,9},{9,10},{10,1... | collective-permute-start | bytes 663560 | tf_op jit(solution)/shard_map/ppermute | solution.py:21
  12.6 14.3 %collective-permute-start.15 = (bf16[32,16,256]{2,1,0:T(8,128)(2,1)S(1)}, bf16[32,16,256]{2,1,0:T(8,128)(2,1)S(1)}, u32[]{:S(2)}, u32[]{:S(2)}) collective-permute-start(bf16[32,16,256]{2,1,0:T(8,128)(2,1)S(1)} %get-tuple-element.47), channel_id=1, source_target_pairs={{0,4},{1,5},{2,6},{3,7},{4,8},{5,9},{6,10},{7,11},{8,12},{9,13},{1... | collective-permute-start | bytes 786440 | tf_op jit(solution)/shard_map/ppermute | solution.py:21
  14.3 22.3 %collective-permute-start.21 = (bf16[32,16,256]{2,1,0:T(8,128)(2,1)S(1)}, bf16[32,16,256]{2,1,0:T(8,128)(2,1)}, u32[]{:S(2)}, u32[]{:S(2)}) collective-permute-start(bf16[32,16,256]{2,1,0:T(8,128)(2,1)S(1)} %get-tuple-element.46), channel_id=1, source_target_pairs={{0,4},{1,5},{2,6},{3,7},{4,8},{5,9},{6,10},{7,11},{8,12},{9,13},{1... | collective-permute-start | bytes 786440 | tf_op jit(solution)/shard_map/ppermute | solution.py:21
  15.9 19.4 %collective-permute-start.9 = (bf16[32,16,256]{2,1,0:T(8,128)(2,1)S(1)}, bf16[32,16,256]{2,1,0:T(8,128)(2,1)S(1)}, u32[]{:S(2)}, u32[]{:S(2)}) collective-permute-start(bf16[32,16,256]{2,1,0:T(8,128)(2,1)S(1)} %get-tuple-element.48), channel_id=1, source_target_pairs={{0,4},{1,5},{2,6},{3,7},{4,8},{5,9},{6,10},{7,11},{8,12},{9,13},{1... | collective-permute-start | bytes 786440 | tf_op jit(solution)/shard_map/ppermute | solution.py:21
  18.5 23.5 %collective-permute-start.3 = (bf16[32,16,256]{2,1,0:T(8,128)(2,1)S(1)}, bf16[32,16,256]{2,1,0:T(8,128)(2,1)}, u32[]{:S(2)}, u32[]{:S(2)}) collective-permute-start(bf16[32,16,256]{2,1,0:T(8,128)(2,1)S(1)} %get-tuple-element.49), channel_id=1, source_target_pairs={{0,4},{1,5},{2,6},{3,7},{4,8},{5,9},{6,10},{7,11},{8,12},{9,13},{1... | collective-permute-start | bytes 786440 | tf_op jit(solution)/shard_map/ppermute | solution.py:21
  24.8 32.7 %collective-permute-start.4 = (bf16[64,16,256]{2,1,0:T(8,128)(2,1)}, bf16[64,16,256]{2,1,0:T(8,128)(2,1)}, u32[]{:S(2)}, u32[]{:S(2)}) collective-permute-start(bf16[64,16,256]{2,1,0:T(8,128)(2,1)} %get-tuple-element.51), channel_id=1, source_target_pairs={{0,2},{1,3},{4,6},{5,7},{8,10},{9,11},{12,14},{13,15},{16,18},{17,... | collective-permute-start | bytes 1572872 | tf_op jit(solution)/shard_map/ppermute | solution.py:21
  26.9 16.3 %collective-permute-start.1 = (bf16[688,256]{1,0:T(8,128)(2,1)S(1)}, bf16[688,256]{1,0:T(8,128)(2,1)S(1)}, u32[]{:S(2)}, u32[]{:S(2)}) collective-permute-start(bf16[688,256]{1,0:T(8,128)(2,1)S(1)} %get-tuple-element.25.to_prev), channel_id=1, source_target_pairs={{0,15},{1,0},{2,1},{3,2},{4,3},{5,4},{6,5},{7,6},{8,7},{9,8},{10,9... | collective-permute-start | bytes 1056776 | tf_op jit(solution)/shard_map/ppermute | solution.py:21
  35.3 9.3 %collective-permute-start.10 = (bf16[32,16,256]{2,1,0:T(8,128)(2,1)S(1)}, bf16[32,16,256]{2,1,0:T(8,128)(2,1)S(1)}, u32[]{:S(2)}, u32[]{:S(2)}) collective-permute-start(bf16[32,16,256]{2,1,0:T(8,128)(2,1)S(1)} %collective-permute-done.9.b4), channel_id=1, source_target_pairs={{2,0},{3,1},{6,4},{7,5},{10,8},{11,9},{14,12},{15,13},{18,16},{19,... | collective-permute-start | bytes 786440 | tf_op jit(solution)/shard_map/ppermute | solution.py:21
  36.6 27.8 %collective-permute-start.16 = (bf16[64,16,256]{2,1,0:T(8,128)(2,1)}, bf16[64,16,256]{2,1,0:T(8,128)(2,1)}, u32[]{:S(2)}, u32[]{:S(2)}) collective-permute-start(bf16[64,16,256]{2,1,0:T(8,128)(2,1)} %get-tuple-element.50), channel_id=1, source_target_pairs={{0,2},{1,3},{4,6},{5,7},{8,10},{9,11},{12,14},{13,15},{16,18},{17,... | collective-permute-start | bytes 1572872 | tf_op jit(solution)/shard_map/ppermute | solution.py:21
  42.0 9.2 %collective-permute-start.5 = (bf16[32,16,256]{2,1,0:T(8,128)(2,1)}, bf16[32,16,256]{2,1,0:T(8,128)(2,1)}, u32[]{:S(2)}, u32[]{:S(2)}) collective-permute-start(bf16[32,16,256]{2,1,0:T(8,128)(2,1)} %collective-permute-done.3.b4), channel_id=1, source_target_pairs={{2,0},{3,1},{6,4},{7,5},{10,8},{11,9},{14,12},{15,13},{18,16},{19,... | collective-permute-start | bytes 786440 | tf_op jit(solution)/shard_map/ppermute | solution.py:21
  43.3 16.8 %collective-permute-start.17 = (bf16[32,16,256]{2,1,0:T(8,128)(2,1)S(1)}, bf16[32,16,256]{2,1,0:T(8,128)(2,1)}, u32[]{:S(2)}, u32[]{:S(2)}) collective-permute-start(bf16[32,16,256]{2,1,0:T(8,128)(2,1)S(1)} %collective-permute-done.15.b4), channel_id=1, source_target_pairs={{2,0},{3,1},{6,4},{7,5},{10,8},{11,9},{14,12},{15,13},{18,16},{19,... | collective-permute-start | bytes 786440 | tf_op jit(solution)/shard_map/ppermute | solution.py:21
  45.3 17.1 %collective-permute-start.22 = (bf16[32,16,256]{2,1,0:T(8,128)(2,1)}, bf16[32,16,256]{2,1,0:T(8,128)(2,1)}, u32[]{:S(2)}, u32[]{:S(2)}) collective-permute-start(bf16[32,16,256]{2,1,0:T(8,128)(2,1)} %collective-permute-done.21.b4), channel_id=1, source_target_pairs={{2,0},{3,1},{6,4},{7,5},{10,8},{11,9},{14,12},{15,13},{18,16},{19,... | collective-permute-start | bytes 786440 | tf_op jit(solution)/shard_map/ppermute | solution.py:21
  51.2 17.6 %collective-permute-start.7 = (bf16[64,16,256]{2,1,0:T(8,128)(2,1)}, bf16[64,16,256]{2,1,0:T(8,128)(2,1)S(1)}, u32[]{:S(2)}, u32[]{:S(2)}) collective-permute-start(bf16[64,16,256]{2,1,0:T(8,128)(2,1)} %get-tuple-element.51), channel_id=1, source_target_pairs={{0,1},{2,3},{4,5},{6,7},{8,9},{10,11},{12,13},{14,15},{16,17},{18,... | collective-permute-start | bytes 1572872 | tf_op jit(solution)/shard_map/ppermute | solution.py:21
  57.6 7.6 %collective-permute-start.12 = (bf16[32,16,256]{2,1,0:T(8,128)(2,1)}, bf16[32,16,256]{2,1,0:T(8,128)(2,1)S(1)}, u32[]{:S(2)}, u32[]{:S(2)}) collective-permute-start(bf16[32,16,256]{2,1,0:T(8,128)(2,1)} %copy-done.12), channel_id=1, source_target_pairs={{1,0},{3,2},{5,4},{7,6},{9,8},{11,10},{13,12},{15,14},{17,16},{19,... | collective-permute-start | bytes 786440 | tf_op jit(solution)/shard_map/ppermute | solution.py:21
  60.1 10.0 %collective-permute-start.8 = (bf16[32,16,256]{2,1,0:T(8,128)(2,1)}, bf16[32,16,256]{2,1,0:T(8,128)(2,1)S(1)}, u32[]{:S(2)}, u32[]{:S(2)}) collective-permute-start(bf16[32,16,256]{2,1,0:T(8,128)(2,1)} %collective-permute-done.3.b4), channel_id=1, source_target_pairs={{1,0},{3,2},{5,4},{7,6},{9,8},{11,10},{13,12},{15,14},{17,16},{19,... | collective-permute-start | bytes 786440 | tf_op jit(solution)/shard_map/ppermute | solution.py:21
  62.4 9.0 %collective-permute-start.11 = (bf16[32,16,256]{2,1,0:T(8,128)(2,1)S(1)}, bf16[32,16,256]{2,1,0:T(8,128)(2,1)S(1)}, u32[]{:S(2)}, u32[]{:S(2)}) collective-permute-start(bf16[32,16,256]{2,1,0:T(8,128)(2,1)S(1)} %get-tuple-element.54.b2), channel_id=1, source_target_pairs={{0,1},{1,0},{2,3},{3,2},{4,5},{5,4},{6,7},{7,6},{8,9},{9,8},{10,11... | collective-permute-start | bytes 786440 | tf_op jit(solution)/shard_map/ppermute | solution.py:21
  64.4 8.3 %collective-permute-start.6 = (bf16[32,16,256]{2,1,0:T(8,128)(2,1)S(1)}, bf16[32,16,256]{2,1,0:T(8,128)(2,1)S(1)}, u32[]{:S(2)}, u32[]{:S(2)}) collective-permute-start(bf16[32,16,256]{2,1,0:T(8,128)(2,1)S(1)} %get-tuple-element.55.b2), channel_id=1, source_target_pairs={{0,1},{1,0},{2,3},{3,2},{4,5},{5,4},{6,7},{7,6},{8,9},{9,8},{10,11... | collective-permute-start | bytes 786440 | tf_op jit(solution)/shard_map/ppermute | solution.py:21
  65.1 24.5 %collective-permute-start.19 = (bf16[64,16,256]{2,1,0:T(8,128)(2,1)}, bf16[64,16,256]{2,1,0:T(8,128)(2,1)S(1)}, u32[]{:S(2)}, u32[]{:S(2)}) collective-permute-start(bf16[64,16,256]{2,1,0:T(8,128)(2,1)} %get-tuple-element.50), channel_id=1, source_target_pairs={{0,1},{2,3},{4,5},{6,7},{8,9},{10,11},{12,13},{14,15},{16,17},{18,... | collective-permute-start | bytes 1572872 | tf_op jit(solution)/shard_map/ppermute | solution.py:21
  68.8 20.8 %collective-permute-start.24 = (bf16[32,16,256]{2,1,0:T(8,128)(2,1)}, bf16[32,16,256]{2,1,0:T(8,128)(2,1)S(1)}, u32[]{:S(2)}, u32[]{:S(2)}) collective-permute-start(bf16[32,16,256]{2,1,0:T(8,128)(2,1)} %collective-permute-done.21.b4), channel_id=1, source_target_pairs={{1,0},{3,2},{5,4},{7,6},{9,8},{11,10},{13,12},{15,14},{17,16},{19,... | collective-permute-start | bytes 786440 | tf_op jit(solution)/shard_map/ppermute | solution.py:21
  70.1 22.7 %collective-permute-start.20 = (bf16[32,16,256]{2,1,0:T(8,128)(2,1)S(1)}, bf16[32,16,256]{2,1,0:T(8,128)(2,1)S(1)}, u32[]{:S(2)}, u32[]{:S(2)}) collective-permute-start(bf16[32,16,256]{2,1,0:T(8,128)(2,1)S(1)} %collective-permute-done.15.b4), channel_id=1, source_target_pairs={{1,0},{3,2},{5,4},{7,6},{9,8},{11,10},{13,12},{15,14},{17,16},{19,... | collective-permute-start | bytes 786440 | tf_op jit(solution)/shard_map/ppermute | solution.py:21
  71.5 18.2 %collective-permute-start.23 = (bf16[32,16,256]{2,1,0:T(8,128)(2,1)S(1)}, bf16[32,16,256]{2,1,0:T(8,128)(2,1)S(1)}, u32[]{:S(2)}, u32[]{:S(2)}) collective-permute-start(bf16[32,16,256]{2,1,0:T(8,128)(2,1)S(1)} %get-tuple-element.52.b2), channel_id=1, source_target_pairs={{0,1},{1,0},{2,3},{3,2},{4,5},{5,4},{6,7},{7,6},{8,9},{9,8},{10,11... | collective-permute-start | bytes 786440 | tf_op jit(solution)/shard_map/ppermute | solution.py:21
  72.7 20.1 %collective-permute-start.18 = (bf16[32,16,256]{2,1,0:T(8,128)(2,1)S(1)}, bf16[32,16,256]{2,1,0:T(8,128)(2,1)S(1)}, u32[]{:S(2)}, u32[]{:S(2)}) collective-permute-start(bf16[32,16,256]{2,1,0:T(8,128)(2,1)S(1)} %get-tuple-element.53.b2), channel_id=1, source_target_pairs={{0,1},{1,0},{2,3},{3,2},{4,5},{5,4},{6,7},{7,6},{8,9},{9,8},{10,11... | collective-permute-start | bytes 786440 | tf_op jit(solution)/shard_map/ppermute | solution.py:21
  (23 other events, 301.0 us)

commit v2 on v1

--- a/solution.py
+++ b/solution.py
@@ -35,7 +35,11 @@
     return jnp.where(column(r, c), 1.0, 0.0).astype(jnp.bfloat16)
 
 
-def call(kernel, name, outs, scratch, args, limit=8, smem=0, **kw):
+def cost(us):
+    return pl.CostEstimate(flops=0, bytes_accessed=int(us * 3.5e6), transcendentals=0)
+
+
+def call(kernel, name, outs, scratch, args, us, limit=8, smem=0, **kw):
     vmem = pl.BlockSpec(memory_space=pltpu.VMEM)
     return pl.pallas_call(
         kernel,
@@ -45,15 +49,19 @@
         scratch_shapes=scratch,
         compiler_params=pltpu.CompilerParams(vmem_limit_bytes=limit << 20),
         name=name,
+        cost_estimate=cost(us),
         **kw,
     )(*args[:smem], *(near(a) for a in args[smem:]))
 
 
-def pack_kernel(left, right, state, coarse, disp, to_next, to_prev, far, flat, pooled):
+def pack_kernel(count, left, *refs):
+    rights = refs[:count]
+    state, coarse, disp, to_next, to_prev, far, flat, pooled = refs[count:]
     images, rows, cols, channels = left.shape
     hid = state.shape[-1]
     many = images * rows
     wide = 16 * cols
+    each = many // count
 
     def end(q):
         return q + jnp.where(q >= 2, cols - 4, 0)
@@ -72,7 +80,7 @@
         put(to_prev, 1, e[16:32])
         put(to_next, 0, e[32:48])
         put(to_next, 1, e[48:])
-        e = dot(ends, right[i, r0: r0 + 16].reshape(wide, channels))
+        e = dot(ends, rights[16 * b // each][16 * b % each: 16 * b % each + 16].reshape(wide, channels))
         put(to_prev, 2, e[:16])
         put(to_prev, 3, e[16:32])
         put(far, 0, e[48:])
@@ -94,10 +102,15 @@
     to_prev[pl.ds(5 * many + flat.shape[0], 16), :] = d
 
 
-def edge_kernel(prev, foll, far, to_next, to_prev, state, disp, left_edge, right_edge, disp24, hid_edge, hid3, wide):
+def edge_kernel(bounds, prev, foll, far, to_next, to_prev, state, disp, pick, motion_weight, distance, left_edge, right_edge, disp24, hid_edge,
+                hid3, table, scale, wide):
+    table[...] = dot(pick[...], motion_weight[...]).astype(jnp.bfloat16)
     images, rows, cols, hid = state.shape
     many = images * rows
     channels = prev.shape[1]
+    for i in range(images):
+        known = (distance[...] >= 0) & (distance[...] < bounds[i])
+        scale[i] = jnp.where(known, jnp.float32(channels ** -0.5), 0.0)
     last = prev.shape[0] - 16
     spread8 = onehot((128, 96), lambda r, c: c == (r & 7) * 16 + (r >> 3))
     spread16 = onehot((256, 48), lambda r, c: c == jnp.where((r & 15) == 15, 2, jnp.where((r & 15) < 2, r & 15, 9)) * 16 + (r >> 4))
@@ -222,13 +235,43 @@
                     up_edge[i, pl.ds(side * 8 * tall + u, tall, stride=8), :] = value[tall * i: tall * (i + 1)]
 
 
-def corr_kernel(sc, left, left_edge, right, right_edge, b4, b2, d2, d0, d4, disp, distance, start, table,
+def copy_either(second_wanted, first, second, out):
+    @pl.when(jnp.logical_not(second_wanted))
+    def _():
+        out[...] = first[...]
+
+    @pl.when(second_wanted)
+    def _():
+        out[...] = second[...]
+
+
+def choose_kernel(mine, came, out):
+    copy_either(lax.rem(lax.axis_index("cols"), 4) >= 2, mine, came, out)
+
+
+def choose(mine, came):
+    return call(choose_kernel, "choose", [(mine.shape, mine.dtype)], [], (mine, came), 0.2)[0]
+
+
+def join_kernel(second, mine, came, out):
+    out[0] = second[...]
+    copy_either(lax.rem(lax.axis_index("cols"), 2) == 1, mine, came, out.at[1])
+
+
+def join(second, mine, came):
+    return call(join_kernel, "join", [((2,) + mine.shape, mine.dtype)], [], (second, mine, came), 0.3)[0]
+
+
+def after(values, *others):
+    return lax.optimization_barrier((values, others))[0]
+
+
+def corr_kernel(scale, left, left_edge, right, right_edge, b4, b2, core, disp, start, table,
                 mot3, mot_edge, wide):
     rows = right.shape[0]
     group = 8
-    even = sc[1] == 1
-    known = (distance[...] >= 0) & (distance[...] < sc[0])
-    scale = jnp.where(known, jnp.float32(left.shape[-1] ** -0.5), 0.0)
+    odd = lax.rem(lax.axis_index("cols"), 2)
+    scale = scale[...]
     lane = lax.broadcasted_iota(jnp.int32, (24, 128), 1)
     keep = (jnp.where(lane < 72, ~7, ~3), jnp.where(lane < 18, ~1, ~0))
     last_lane = lax.broadcasted_iota(jnp.int32, (8, 128), 1) == 127
@@ -237,9 +280,8 @@
         scores, places = [], ([], [])
         for k in range(group):
             h = g * group + k
-            b1 = jnp.where(even, d2[h], d0[h])
-            b3 = jnp.where(even, d4[h], d2[h])
-            window = jnp.concatenate([b4[h], b3, b2[h], b1, right[h], right_edge[h]], axis=0)
+            window = jnp.concatenate(
+                [b4[h], core[1 - odd, h], b2[h], core[odd, h], right[h], right_edge[h]], axis=0)
             pixels = jnp.concatenate([left[h], left_edge[h]], axis=0)
             s = lax.dot_general(pixels, window, (((1,), (1,)), ((), ())), preferred_element_type=jnp.float32)
             s = jnp.concatenate([s, jnp.zeros((s.shape[0], 128 - s.shape[1]), jnp.float32)], axis=1)
@@ -268,18 +310,18 @@
     lax.fori_loop(0, rows // group, body, 0)
 
 
-def motion_chunk(i, k, sc, left, left_edge, right, right_edge, b4, b2, d2, d0, d4, disp, distance, start, table):
+def motion_chunk(i, k, scale, left, left_edge, right, right_edge, b4, b2, core, disp, start, table):
     rows = b4.shape[0]
     hid = table.shape[1]
 
-    def kernel(sc, left, left_edge, right, right_edge, b4, b2, d2, d0, d4, disp, *rest):
+    def kernel(scale, left, left_edge, right, right_edge, b4, b2, core, disp, *rest):
         here = pl.ds(k * rows, rows)
-        corr_kernel(sc, left.at[i, here], left_edge.at[i, here], right.at[i, here], right_edge.at[i, here],
-                    b4, b2, d2, d0.at[here], d4, disp.at[i, here], *rest)
+        corr_kernel(scale.at[i], left.at[i, here], left_edge.at[i, here], right, right_edge.at[i, here],
+                    b4, b2, core, disp.at[i, here], *rest)
 
     return call(kernel, "motion", [((rows, 16, 3 * hid), jnp.bfloat16), ((rows, 8, hid), jnp.float32)],
                 [pltpu.VMEM((8 * 32, hid), jnp.float32)],
-                (sc, left, left_edge, right, right_edge, b4, b2, d2, d0, d4, disp, distance, start, table), smem=1)
+                (scale, left, left_edge, right, right_edge, b4, b2, core, disp, start, table), 2.7)
 
 
 def gru_kernel(count, hid3, state, hid_edge, *refs):
@@ -391,6 +433,7 @@
                         pltpu.VMEM((rows * 32, hid), jnp.float32),
                         pltpu.VMEM((rows + 2, 16, 3 * hid), jnp.bfloat16)],
         name="fine_gru",
+        cost_estimate=cost(5),
     )(*(near(v) for v in args), *first, *(near(v) for v in rest))
 
 
@@ -405,62 +448,50 @@
     return level, offset, tap
 
 
-def lookup_table(motion_weight):
+def lookup_pick(channels):
     level, _, tap = (v.reshape(-1) for v in lookup_places())
     rows = np.maximum(level, 0) * (2 * RADIUS + 1) + tap
-    pick = np.zeros((level.size, motion_weight.shape[0]), np.float32)
+    pick = np.zeros((level.size, channels), np.float32)
     pick[np.arange(level.size), rows] = np.where(level >= 0, 0.5 ** np.maximum(level, 0), 0.0)
-    return dot(jnp.asarray(pick.astype(jnp.bfloat16)), motion_weight).astype(jnp.bfloat16)
+    return jnp.asarray(pick.astype(jnp.bfloat16))
 
 
 def local(left_feat, right_feat, bounds, disparity, hidden_fine, hidden_coarse, motion_weight,
           fine_gates, fine_candidate, coarse_gates, coarse_candidate):
     images, rows, cols, channels = left_feat.shape
     hid = hidden_fine.shape[-1]
-    even = 1 - lax.rem(lax.axis_index("cols"), 2)
     many = images * rows
     each = rows // CHUNKS
     keys = [(i, k) for i in range(images) for k in range(CHUNKS)]
     bf16, f32 = jnp.bfloat16, jnp.float32
 
-    b4, b2, d2, d4 = {}, {}, {}, {}
-    for i, k in keys:
-        b4[i, k] = permute(right_feat[i, k * each:(k + 1) * each], lambda j: j + 4)
-    d0 = [permute(right_feat[i], lambda j: j + 1, lambda j: j % 2 == 0) for i in range(images)]
-    straight = [permute(right_feat[i], lambda j: j + 2, lambda j: j % 4 < 2) for i in range(images)]
+    own = [right_feat[i, k * each:(k + 1) * each] for i, k in keys]
 
     disp = disparity.reshape(many, cols)
     cells = hidden_coarse.shape[1] * hidden_coarse.shape[2] * images
     to_next, to_prev, to_far, flat = call(
-        pack_kernel, "pack",
+        functools.partial(pack_kernel, len(own)), "pack",
         [((3 * many + cells + 16, channels), bf16), ((5 * many + cells + 16, channels), bf16), ((many, channels), bf16),
          ((cells, channels), bf16)],
         [pltpu.VMEM((cells, hid), f32)],
-        (left_feat, right_feat, hidden_fine, hidden_coarse.reshape(-1, hid), disp))
+        (left_feat, *own, hidden_fine, hidden_coarse.reshape(-1, hid), disp), 1)
     prev = permute(to_next, lambda j: j + 1)
     foll = permute(to_prev, lambda j: j - 1)
     far = permute(to_far, lambda j: j + 5)
     behind2 = permute(flat, lambda j: j + 2)
     ahead2 = permute(flat, lambda j: j - 2)
-
-    for i, k in keys:
-        relayed = permute(b4[i, k], lambda j: j - 2, lambda j: j % 4 >= 2)
-        b2[i, k] = straight[i][k * each:(k + 1) * each] + relayed
-        d4[i, k] = permute(b4[i, k], lambda j: j - 1, lambda j: j % 2 == 1)
-        d2[i, k] = permute(b2[i, k], lambda j: j ^ 1)
-
-    left_edge, right_edge, disp24, hid_edge, hid3 = call(
-        edge_kernel, "edges",
-        [((images, rows, 8, channels), bf16), ((images, rows, 16, channels), bf16), ((images, rows, 24, 128), jnp.int32),
-         ((images, 8 * (rows + 2), hid), f32), ((images, rows + 2, cols, 3 * hid), bf16)],
-        [pltpu.VMEM((16 * 32, hid), f32)],
-        (prev, foll, far, to_next, to_prev, hidden_fine, disp))
-    new, *ups, up_edge = call(
-        coarse_kernel, "coarse",
-        [((cells, hid), bf16)] + [((cells // 2 * 48, hid), f32)] * 3 + [((images, 2 * rows, hid), f32)],
-        [pltpu.VMEM((2, 5 * cells, hid), f32), pltpu.VMEM((3, 4 * cells, 2 * hid), bf16), pltpu.VMEM((cells, hid), f32)],
-        (behind2, prev, flat, foll, ahead2, coarse_gates, coarse_candidate, fine_gates, fine_candidate))
-    coarse_new = new.reshape(hidden_coarse.shape)
+    own, prev, foll, far, behind2, ahead2 = lax.optimization_barrier((own, prev, foll, far, behind2, ahead2))
+    b4 = [permute(value, lambda j: j + 4) for value in own]
+    chosen, b2, core = [], [], []
+
+    def along_y(n, *others):
+        chosen.append(choose(own[n], after(b4[n], *others)))
+        b2.append(permute(chosen[n], lambda j: j ^ 2))
+
+    def joined(n, *others):
+        both = join(after(b2[n], *others), own[n], b4[n])
+        core.append(permute(both, lambda j: j ^ 1))
+        return both
 
     where_x = np.array(list(range(cols)) + list(EDGE), np.int32)[:, None]
     lane = np.arange(128, dtype=np.int32)[None]
@@ -469,16 +500,45 @@
     distance = jnp.asarray(np.where((distance >= 0) & (distance < MAXD), distance, -1).astype(np.int32))
     _, offset, _ = lookup_places()
     start = jnp.asarray((where_x + 64 - offset[:, None, :]).astype(np.int32))
-    table = lookup_table(motion_weight)
-
-    fine = None
-    for i in range(images):
-        sc = jnp.stack([bounds[i], even]).astype(jnp.int32)
-        done = [motion_chunk(i, k, sc, left_feat, left_edge, right_feat, right_edge, b4[i, k], b2[i, k], d2[i, k], d0[i],
-                             d4[i, k], disp24, distance, start, table) for k in range(CHUNKS)]
-        fine = fine_gru(i, fine, hid3, hidden_fine, hid_edge, [m for m, _ in done], [e for _, e in done],
+    pick = lookup_pick(motion_weight.shape[0])
+
+    left_edge, right_edge, disp24, hid_edge, hid3, table, scale = call(
+        edge_kernel, "edges",
+        [((images, rows, 8, channels), bf16), ((images, rows, 16, channels), bf16), ((images, rows, 24, 128), jnp.int32),
+         ((images, 8 * (rows + 2), hid), f32), ((images, rows + 2, cols, 3 * hid), bf16), ((pick.shape[0], hid), bf16),
+         ((images, 24, 128), f32)],
+        [pltpu.VMEM((16 * 32, hid), f32)],
+        (bounds, prev, foll, far, to_next, to_prev, hidden_fine, disp, pick, motion_weight, distance), 2, smem=1)
+    new, *ups, up_edge = call(
+        coarse_kernel, "coarse",
+        [((cells, hid), bf16)] + [((cells // 2 * 48, hid), f32)] * 3 + [((images, 2 * rows, hid), f32)],
+        [pltpu.VMEM((2, 5 * cells, hid), f32), pltpu.VMEM((3, 4 * cells, 2 * hid), bf16), pltpu.VMEM((cells, hid), f32)],
+        (behind2, prev, flat, foll, ahead2, coarse_gates, coarse_candidate, fine_gates, fine_candidate), 1.5)
+    coarse_new = new.reshape(hidden_coarse.shape)
+
+    motions = []
+
+    def motion(n, *others):
+        i, k = keys[n]
+        motions.append(motion_chunk(i, k, scale, left_feat, left_edge, own[n], right_edge, b4[n], b2[n],
+                                    after(core[n], *others), disp24, start, table))
+        return motions[n]
+
+    def fine(i, before, *others):
+        mine = [m for m, key in zip(motions, keys) if key[0] == i]
+        return fine_gru(i, before, after(hid3, *others), hidden_fine, hid_edge, [m for m, _ in mine], [e for _, e in mine],
                         ups, up_edge, fine_gates, fine_candidate)
-    return (fine, coarse_new)
+
+    along_y(0, table, new)
+    along_y(1)
+    along_y(2)
+    along_y(3)
+    for n in range(4):
+        joined(n)
+    for n in range(4):
+        motion(n)
+    result = fine(0, None)
+    return (fine(1, result), coarse_new)
 
 
 def solution(mesh):

time: 101 us -> 71.9 us (0.71)
  starting transfers between devices: 48.1 us -> 16.3 us
  waiting for transfers between devices: 12 us -> 28.6 us
  local copies, waits for them, and re-layouts: 8.66 us -> 2.25 us
  other arithmetic: 3.91 us -> 0 us
  Pallas kernels: 26 us -> 23.6 us
    ppermute x25 -> x17, starting transfers between devices: 48.1 us -> 16.3 us  [permute(): return lax.ppermute(value, 'cols', pairs)]
    ppermute x25 -> x17, waiting for transfers between devices: 12 us -> 28.6 us  [permute(): return lax.ppermute(value, 'cols', pairs)]
    unnamed x46 -> x28, local copies, waits for them, and re-layouts: 6.98 us -> 0.88 us
    add x2 -> x0, other arithmetic: 2.49 us -> none  [local(): b2[i, k] = straight[i][k * each:(k + 1) * each] + relayed]
    pallas_call x7 -> x15, Pallas kernels: 15.7 us -> 13.4 us  [call(): pl.pallas_call(kernel, out_shape=tuple((pltpu.VMEM(shape, dtype) for shap...]
    another operation x2 -> x0, other arithmetic: 1.42 us -> none  [local(): sc = jnp.stack([bounds[i], even]).astype(jnp.int32)]
  transfers between devices with their start and end apart: 25 -> 17, of which waited for: 4 -> 8; matrix products, arithmetic and copies ran while one was open for 7% -> 1% of each run, Pallas kernels for 17% -> 22%
where the time goes in v2:
time: 71.9 us; the launch traced here: 71.7 us
  waiting for transfers between devices  28.6 us (40%)
  Pallas kernels  23.6 us (33%)
  starting transfers between devices  16.3 us (23%)
  local copies, waits for them, and re-layouts  2.25 us (3%)
  between operations  0.97 us (1%)
    ppermute x17, waiting for transfers between devices, permute(): return lax.ppermute(value, 'cols', pairs)  28.6 us
    ppermute x17, starting transfers between devices, permute(): return lax.ppermute(value, 'cols', pairs)  16.3 us
    pallas_call x15, Pallas kernels, call(): pl.pallas_call(kernel, out_shape=tuple((pltpu.VMEM(shape, dtype) for shap...  13.4 us
    pallas_call x2, Pallas kernels, fine_gru(): pl.pallas_call(kernel, grid=(1,), out_shape=jax.ShapeDtypeStruct(state.sh...  10.2 us
  transfers between devices with their start and end apart: 17, of which 8 were waited for; matrix products, arithmetic and copies ran while one was open for 1% of the time, Pallas kernels for 22%

profile of v2, /device:TPU:0, one launch (start us, length us, event | category | flops | bytes accessed | tf_op | source)
XLA Modules:
  0.0 71.7 jit_solution(15782638012684649499)
XLA Ops:
  0.7 1.4 %slice_bitcast_fusion = (bf16[32,16,256]{2,1,0:T(8,128)(2,1)S(1)}, bf16[32,16,256]{2,1,0:T(8,128)(2,1)S(1)}, bf16[32,16,256]{2,1,0:T(8,128)(2,1)S(1)}, bf16[32,16,256]{2,1,0:T(8,128)(2,1)S(1)}) fusion(bf16[2,64,16,256]{3,2,1,0:T(8,128)(2,1)} %param.15), kind=kLoop, calls=%fused_computation | loop fusion | bytes 2097152 | tf_op jit(solution)/shard_map/squeeze | solution.py:468
  2.3 0.6 pack.1
  2.9 5.5 %collective-permute-start.1 = (bf16[688,256]{1,0:T(8,128)(2,1)S(1)}, bf16[688,256]{1,0:T(8,128)(2,1)S(1)}, u32[]{:S(2)}, u32[]{:S(2)}) collective-permute-start(bf16[688,256]{1,0:T(8,128)(2,1)S(1)} %get-tuple-element.37.to_prev), channel_id=1, source_target_pairs={{0,15},{1,0},{2,1},{3,2},{4,3},{5,4},{6,5},{7,6},{8,7},{9,8},{10,9... | collective-permute-start | bytes 1056776 | tf_op jit(solution)/shard_map/ppermute | solution.py:21
  8.4 1.2 %collective-permute-start.3 = (bf16[32,256]{1,0:T(8,128)(2,1)S(1)}, bf16[32,256]{1,0:T(8,128)(2,1)S(1)}, u32[]{:S(2)}, u32[]{:S(2)}) collective-permute-start(bf16[32,256]{1,0:T(8,128)(2,1)S(1)} %get-tuple-element.39.flat), channel_id=1, source_target_pairs={{0,2},{1,3},{2,4},{3,5},{4,6},{5,7},{6,8},{7,9},{8,10},{9,11},{10,... | collective-permute-start | bytes 49160 | tf_op jit(solution)/shard_map/ppermute | solution.py:21
  9.6 3.6 %collective-permute-start.4 = (bf16[32,256]{1,0:T(8,128)(2,1)S(1)}, bf16[32,256]{1,0:T(8,128)(2,1)S(1)}, u32[]{:S(2)}, u32[]{:S(2)}) collective-permute-start(bf16[32,256]{1,0:T(8,128)(2,1)S(1)} %get-tuple-element.39.flat), channel_id=1, source_target_pairs={{0,14},{1,15},{2,0},{3,1},{4,2},{5,3},{6,4},{7,5},{8,6},{9,7},{10,... | collective-permute-start | bytes 49160 | tf_op jit(solution)/shard_map/ppermute | solution.py:21
  13.2 1.9 %collective-permute-done.3.behind2 = bf16[32,256]{1,0:T(8,128)(2,1)S(1)} collective-permute-done((bf16[32,256]{1,0:T(8,128)(2,1)S(1)}, bf16[32,256]{1,0:T(8,128)(2,1)S(1)}, u32[]{:S(2)}, u32[]{:S(2)}) %collective-permute-start.3) | collective-permute-done | bytes 16416 | tf_op jit(solution)/shard_map/ppermute | solution.py:21
  15.1 2.5 %collective-permute-done.2.far = bf16[128,256]{1,0:T(8,128)(2,1)S(1)} collective-permute-done((bf16[128,256]{1,0:T(8,128)(2,1)S(1)}, bf16[128,256]{1,0:T(8,128)(2,1)S(1)}, u32[]{:S(2)}, u32[]{:S(2)}) %collective-permute-start.2) | collective-permute-done | bytes 65568 | tf_op jit(solution)/shard_map/ppermute | solution.py:21
  18.3 1.5 %collective-permute-start.11 = (bf16[32,16,256]{2,1,0:T(8,128)(2,1)S(1)}, bf16[32,16,256]{2,1,0:T(8,128)(2,1)S(1)}, u32[]{:S(2)}, u32[]{:S(2)}) collective-permute-start(bf16[32,16,256]{2,1,0:T(8,128)(2,1)S(1)} %get-tuple-element.64.refs_2_.mine.right), channel_id=1, source_target_pairs={{0,4},{1,5},{2,6},{3,7},{4,8},{5,9},{6,10},{7,11},{8,12},{9,13},{1... | collective-permute-start | bytes 786440 | tf_op jit(solution)/shard_map/ppermute | solution.py:21
  19.8 2.8 %collective-permute-start.14 = (bf16[32,16,256]{2,1,0:T(8,128)(2,1)S(1)}, bf16[32,16,256]{2,1,0:T(8,128)(2,1)S(1)}, u32[]{:S(2)}, u32[]{:S(2)}) collective-permute-start(bf16[32,16,256]{2,1,0:T(8,128)(2,1)S(1)} %get-tuple-element.66.refs_3_.mine.right), channel_id=1, source_target_pairs={{0,4},{1,5},{2,6},{3,7},{4,8},{5,9},{6,10},{7,11},{8,12},{9,13},{1... | collective-permute-start | bytes 786440 | tf_op jit(solution)/shard_map/ppermute | solution.py:21
  22.6 2.6 %edges.1 = (bf16[2,64,8,256]{3,2,1,0:T(8,128)(2,1)S(1)}, bf16[2,64,16,256]{3,2,1,0:T(8,128)(2,1)S(1)}, s32[2,64,24,128]{3,2,1,0:T(8,128)S(1)}, f32[2,528,128]{2,...) custom-call(s32[2]{0:T(128)S(1)} %copy-done.11, ...), custom_call_target="tpu_custom_call" | custom-call | bytes 7000000 | tf_op jit(solution)/shard_map/edges/pallas_call | solution.py:44
  25.2 1.3 %coarse.1 = (bf16[32,128]{1,0:T(8,128)(2,1)S(1)}, f32[768,128]{1,0:T(8,128)S(1)}, f32[768,128]{1,0:T(8,128)S(1)}, f32[768,128]{1,0:T(8,128)S(1)}, f32[2,128,128]{2,1,0:T(8,128)S(1)}) custom-call(bf16[32,256]{1,0:T(8,128)(2,1)S(1)} %collective-permute-done.3.behind2, bf16[432,256]{1,0:T(8,128)(2,1)S(1)} %collective-permute-done.prev, ...), custom_call_target="tpu_custom_call" | custom-call | bytes 5250000 | tf_op jit(solution)/shard_map/coarse/pallas_call | solution.py:44
  26.6 2.1 %collective-permute-done.5.came.b4 = bf16[32,16,256]{2,1,0:T(8,128)(2,1)S(1)} collective-permute-done((bf16[32,16,256]{2,1,0:T(8,128)(2,1)S(1)}, bf16[32,16,256]{2,1,0:T(8,128)(2,1)S(1)}, u32[]{:S(2)}, u32[]{:S(2)}) %collective-permute-start.5) | collective-permute-done | bytes 262176 | tf_op jit(solution)/shard_map/ppermute | solution.py:21
  28.7 5.5 %collective-permute-done.8.came.b4 = bf16[32,16,256]{2,1,0:T(8,128)(2,1)S(1)} collective-permute-done((bf16[32,16,256]{2,1,0:T(8,128)(2,1)S(1)}, bf16[32,16,256]{2,1,0:T(8,128)(2,1)S(1)}, u32[]{:S(2)}, u32[]{:S(2)}) %collective-permute-start.8) | collective-permute-done | bytes 262176 | tf_op jit(solution)/shard_map/ppermute | solution.py:21
  34.4 5.5 %collective-permute-done.11.came.b4 = bf16[32,16,256]{2,1,0:T(8,128)(2,1)S(1)} collective-permute-done((bf16[32,16,256]{2,1,0:T(8,128)(2,1)S(1)}, bf16[32,16,256]{2,1,0:T(8,128)(2,1)S(1)}, u32[]{:S(2)}, u32[]{:S(2)}) %collective-permute-start.11) | collective-permute-done | bytes 262176 | tf_op jit(solution)/shard_map/ppermute | solution.py:21
  40.0 4.4 %collective-permute-done.14.came.b4 = bf16[32,16,256]{2,1,0:T(8,128)(2,1)S(1)} collective-permute-done((bf16[32,16,256]{2,1,0:T(8,128)(2,1)S(1)}, bf16[32,16,256]{2,1,0:T(8,128)(2,1)S(1)}, u32[]{:S(2)}, u32[]{:S(2)}) %collective-permute-start.14) | collective-permute-done | bytes 262176 | tf_op jit(solution)/shard_map/ppermute | solution.py:21
  45.2 1.3 %collective-permute-done.12.second.b2 = bf16[32,16,256]{2,1,0:T(8,128)(2,1)S(1)} collective-permute-done((bf16[32,16,256]{2,1,0:T(8,128)(2,1)S(1)}, bf16[32,16,256]{2,1,0:T(8,128)(2,1)S(1)}, u32[]{:S(2)}, u32[]{:S(2)}) %collective-permute-start.12) | collective-permute-done | bytes 262176 | tf_op jit(solution)/shard_map/ppermute | solution.py:21
  46.7 5.3 %collective-permute-done.15.second.b2 = bf16[32,16,256]{2,1,0:T(8,128)(2,1)S(1)} collective-permute-done((bf16[32,16,256]{2,1,0:T(8,128)(2,1)S(1)}, bf16[32,16,256]{2,1,0:T(8,128)(2,1)S(1)}, u32[]{:S(2)}, u32[]{:S(2)}) %collective-permute-start.15) | collective-permute-done | bytes 262176 | tf_op jit(solution)/shard_map/ppermute | solution.py:21
  52.1 0.6 copy.19
  52.7 2.2 %motion.4 = (bf16[32,16,384]{2,1,0:T(8,128)(2,1)S(1)}, f32[32,8,128]{2,1,0:T(8,128)S(1)}) custom-call(f32[2,24,128]{2,1,0:T(8,128)S(1)} %get-tuple-element.45.scale, bf16[2,64,16,256]{3,2,1,0:T(8,128)(2,1)S(1)} %copy-done, bf16[2,64,8,256]{3,2,1,0:T(8,128)(2,1)S(1)} %get-tuple-element.46.left_edge, ...), custom_call_target="tpu_custom_call" | custom-call | bytes 9450000 | tf_op jit(solution)/shard_map/motion/pallas_call | solution.py:44
  54.9 2.2 %motion.5 = (bf16[32,16,384]{2,1,0:T(8,128)(2,1)S(1)}, f32[32,8,128]{2,1,0:T(8,128)S(1)}) custom-call(f32[2,24,128]{2,1,0:T(8,128)S(1)} %get-tuple-element.45.scale, bf16[2,64,16,256]{3,2,1,0:T(8,128)(2,1)S(1)} %copy-done, bf16[2,64,8,256]{3,2,1,0:T(8,128)(2,1)S(1)} %get-tuple-element.46.left_edge, ...), custom_call_target="tpu_custom_call" | custom-call | bytes 9450000 | tf_op jit(solution)/shard_map/motion/pallas_call | solution.py:44
  57.1 5.1 %fine_gru.2.refs_0_ = bf16[2,64,16,128]{3,2,1,0:T(8,128)(2,1)} custom-call(bf16[2,66,16,384]{3,2,1,0:T(8,128)(2,1)S(1)} %get-tuple-element.43.hid3, bf16[2,64,16,128]{3,2,1,0:T(8,128)(2,1)S(1)} %copy-done.2, f32[2,528,128]{2,1,0:T(8,128)S(1)} %get-tuple-element.44.hid_edge, bf16[32,16,384]{2,1,0:T(8,128)(2,1)S(1)} %get-tuple-element.55.refs_0_, ...), custom_call_target="tpu_custom_call" | custom-call | bytes 17500000 | tf_op jit(solution)/shard_map/fine_gru/pallas_call | solution.py:422
  62.2 2.2 %motion.6 = (bf16[32,16,384]{2,1,0:T(8,128)(2,1)S(1)}, f32[32,8,128]{2,1,0:T(8,128)S(1)}) custom-call(f32[2,24,128]{2,1,0:T(8,128)S(1)} %get-tuple-element.45.scale, bf16[2,64,16,256]{3,2,1,0:T(8,128)(2,1)S(1)} %copy-done, bf16[2,64,8,256]{3,2,1,0:T(8,128)(2,1)S(1)} %get-tuple-element.46.left_edge, ...), custom_call_target="tpu_custom_call" | custom-call | bytes 9450000 | tf_op jit(solution)/shard_map/motion/pallas_call | solution.py:44
  64.4 2.2 %motion.7 = (bf16[32,16,384]{2,1,0:T(8,128)(2,1)S(1)}, f32[32,8,128]{2,1,0:T(8,128)S(1)}) custom-call(f32[2,24,128]{2,1,0:T(8,128)S(1)} %get-tuple-element.45.scale, bf16[2,64,16,256]{3,2,1,0:T(8,128)(2,1)S(1)} %copy-done, bf16[2,64,8,256]{3,2,1,0:T(8,128)(2,1)S(1)} %get-tuple-element.46.left_edge, ...), custom_call_target="tpu_custom_call" | custom-call | bytes 9450000 | tf_op jit(solution)/shard_map/motion/pallas_call | solution.py:44
  66.5 5.1 %fine_gru.3 = bf16[2,64,16,128]{3,2,1,0:T(8,128)(2,1)} custom-call(bf16[2,66,16,384]{3,2,1,0:T(8,128)(2,1)S(1)} %get-tuple-element.43.hid3, bf16[2,64,16,128]{3,2,1,0:T(8,128)(2,1)S(1)} %copy-done.2, f32[2,528,128]{2,1,0:T(8,128)S(1)} %get-tuple-element.44.hid_edge, bf16[2,64,16,128]{3,2,1,0:T(8,128)(2,1)} %fine_gru.2.refs_0_, ...), custom_call_target="tpu_custom_call", output_to_operand_aliasing={{}: (3, {})} | custom-call | bytes 17500000 | tf_op jit(solution)/shard_map/fine_gru/pallas_call | solution.py:422
  (56 shorter events, 2.3 us)
Async XLA Ops:
  2.1 20.5 %copy-start.7 = (bf16[256,36]{1,0:T(8,128)(2,1)S(1)}, bf16[256,36]{1,0:T(8,128)(2,1)}, u32[]{:S(2)}) copy-start(bf16[256,36]{1,0:T(8,128)(2,1)} %constant.8.clone.pick) | copy-start | bytes 55300
  2.1 20.5 %copy-start.8 = (s32[24,128]{1,0:T(8,128)S(1)}, s32[24,128]{1,0:T(8,128)}, u32[]{:S(2)}) copy-start(s32[24,128]{1,0:T(8,128)} %constant.6.clone.distance) | copy-start | bytes 36868
  2.1 20.5 %copy-start.9 = (bf16[36,128]{1,0:T(8,128)(2,1)S(1)}, bf16[36,128]{1,0:T(8,128)(2,1)}, u32[]{:S(2)}) copy-start(bf16[36,128]{1,0:T(8,128)(2,1)} %motion_weight.1) | copy-start | bytes 27652
  2.3 22.9 %copy-start.3 = (bf16[9,384,128]{2,1,0:T(8,128)(2,1)S(1)}, bf16[9,384,128]{2,1,0:T(8,128)(2,1)}, u32[]{:S(2)}) copy-start(bf16[9,384,128]{2,1,0:T(8,128)(2,1)} %refs_10_.1) | copy-start | bytes 2654212
  2.3 22.9 %copy-start.4 = (bf16[9,256,256]{2,1,0:T(8,128)(2,1)S(1)}, bf16[9,256,256]{2,1,0:T(8,128)(2,1)}, u32[]{:S(2)}) copy-start(bf16[9,256,256]{2,1,0:T(8,128)(2,1)} %gates.1) | copy-start | bytes 3538948
  2.3 22.9 %copy-start.5 = (bf16[9,256,128]{2,1,0:T(8,128)(2,1)S(1)}, bf16[9,256,128]{2,1,0:T(8,128)(2,1)}, u32[]{:S(2)}) copy-start(bf16[9,256,128]{2,1,0:T(8,128)(2,1)} %cand.1) | copy-start | bytes 1769476
  2.9 22.3 %copy-start.1 = (bf16[9,384,256]{2,1,0:T(8,128)(2,1)S(1)}, bf16[9,384,256]{2,1,0:T(8,128)(2,1)}, u32[]{:S(2)}) copy-start(bf16[9,384,256]{2,1,0:T(8,128)(2,1)} %refs_9_.3) | copy-start | bytes 5308420
  2.9 14.7 %collective-permute-start.1 = (bf16[688,256]{1,0:T(8,128)(2,1)S(1)}, bf16[688,256]{1,0:T(8,128)(2,1)S(1)}, u32[]{:S(2)}, u32[]{:S(2)}) collective-permute-start(bf16[688,256]{1,0:T(8,128)(2,1)S(1)} %get-tuple-element.37.to_prev), channel_id=1, source_target_pairs={{0,15},{1,0},{2,1},{3,2},{4,3},{5,4},{6,5},{7,6},{8,7},{9,8},{10,9... | collective-permute-start | bytes 1056776 | tf_op jit(solution)/shard_map/ppermute | solution.py:21
  8.4 9.2 %collective-permute-start = (bf16[432,256]{1,0:T(8,128)(2,1)S(1)}, bf16[432,256]{1,0:T(8,128)(2,1)S(1)}, u32[]{:S(2)}, u32[]{:S(2)}) collective-permute-start(bf16[432,256]{1,0:T(8,128)(2,1)S(1)} %get-tuple-element.36.to_next), channel_id=1, source_target_pairs={{0,1},{1,2},{2,3},{3,4},{4,5},{5,6},{6,7},{7,8},{8,9},{9,10},{10,1... | collective-permute-start | bytes 663560 | tf_op jit(solution)/shard_map/ppermute | solution.py:21
  8.4 9.2 %collective-permute-start.2 = (bf16[128,256]{1,0:T(8,128)(2,1)S(1)}, bf16[128,256]{1,0:T(8,128)(2,1)S(1)}, u32[]{:S(2)}, u32[]{:S(2)}) collective-permute-start(bf16[128,256]{1,0:T(8,128)(2,1)S(1)} %get-tuple-element.38), channel_id=1, source_target_pairs={{0,5},{1,6},{2,7},{3,8},{4,9},{5,10},{6,11},{7,12},{8,13},{9,14},{... | collective-permute-start | bytes 196616 | tf_op jit(solution)/shard_map/ppermute | solution.py:21
  8.4 6.7 %collective-permute-start.3 = (bf16[32,256]{1,0:T(8,128)(2,1)S(1)}, bf16[32,256]{1,0:T(8,128)(2,1)S(1)}, u32[]{:S(2)}, u32[]{:S(2)}) collective-permute-start(bf16[32,256]{1,0:T(8,128)(2,1)S(1)} %get-tuple-element.39.flat), channel_id=1, source_target_pairs={{0,2},{1,3},{2,4},{3,5},{4,6},{5,7},{6,8},{7,9},{8,10},{9,11},{10,... | collective-permute-start | bytes 49160 | tf_op jit(solution)/shard_map/ppermute | solution.py:21
  9.6 5.5 %collective-permute-start.4 = (bf16[32,256]{1,0:T(8,128)(2,1)S(1)}, bf16[32,256]{1,0:T(8,128)(2,1)S(1)}, u32[]{:S(2)}, u32[]{:S(2)}) collective-permute-start(bf16[32,256]{1,0:T(8,128)(2,1)S(1)} %get-tuple-element.39.flat), channel_id=1, source_target_pairs={{0,14},{1,15},{2,0},{3,1},{4,2},{5,3},{6,4},{7,5},{8,6},{9,7},{10,... | collective-permute-start | bytes 49160 | tf_op jit(solution)/shard_map/ppermute | solution.py:21
  17.6 11.0 %collective-permute-start.5 = (bf16[32,16,256]{2,1,0:T(8,128)(2,1)S(1)}, bf16[32,16,256]{2,1,0:T(8,128)(2,1)S(1)}, u32[]{:S(2)}, u32[]{:S(2)}) collective-permute-start(bf16[32,16,256]{2,1,0:T(8,128)(2,1)S(1)} %get-tuple-element.47.refs_0_.mine.right), channel_id=1, source_target_pairs={{0,4},{1,5},{2,6},{3,7},{4,8},{5,9},{6,10},{7,11},{8,12},{9,13},{1... | collective-permute-start | bytes 786440 | tf_op jit(solution)/shard_map/ppermute | solution.py:21
  18.0 16.2 %collective-permute-start.8 = (bf16[32,16,256]{2,1,0:T(8,128)(2,1)S(1)}, bf16[32,16,256]{2,1,0:T(8,128)(2,1)S(1)}, u32[]{:S(2)}, u32[]{:S(2)}) collective-permute-start(bf16[32,16,256]{2,1,0:T(8,128)(2,1)S(1)} %get-tuple-element.56.refs_1_.mine.right), channel_id=1, source_target_pairs={{0,4},{1,5},{2,6},{3,7},{4,8},{5,9},{6,10},{7,11},{8,12},{9,13},{1... | collective-permute-start | bytes 786440 | tf_op jit(solution)/shard_map/ppermute | solution.py:21
  18.3 21.5 %collective-permute-start.11 = (bf16[32,16,256]{2,1,0:T(8,128)(2,1)S(1)}, bf16[32,16,256]{2,1,0:T(8,128)(2,1)S(1)}, u32[]{:S(2)}, u32[]{:S(2)}) collective-permute-start(bf16[32,16,256]{2,1,0:T(8,128)(2,1)S(1)} %get-tuple-element.64.refs_2_.mine.right), channel_id=1, source_target_pairs={{0,4},{1,5},{2,6},{3,7},{4,8},{5,9},{6,10},{7,11},{8,12},{9,13},{1... | collective-permute-start | bytes 786440 | tf_op jit(solution)/shard_map/ppermute | solution.py:21
  19.8 24.6 %collective-permute-start.14 = (bf16[32,16,256]{2,1,0:T(8,128)(2,1)S(1)}, bf16[32,16,256]{2,1,0:T(8,128)(2,1)S(1)}, u32[]{:S(2)}, u32[]{:S(2)}) collective-permute-start(bf16[32,16,256]{2,1,0:T(8,128)(2,1)S(1)} %get-tuple-element.66.refs_3_.mine.right), channel_id=1, source_target_pairs={{0,4},{1,5},{2,6},{3,7},{4,8},{5,9},{6,10},{7,11},{8,12},{9,13},{1... | collective-permute-start | bytes 786440 | tf_op jit(solution)/shard_map/ppermute | solution.py:21
  28.7 15.8 %collective-permute-start.6 = (bf16[32,16,256]{2,1,0:T(8,128)(2,1)S(1)}, bf16[32,16,256]{2,1,0:T(8,128)(2,1)S(1)}, u32[]{:S(2)}, u32[]{:S(2)}) collective-permute-start(bf16[32,16,256]{2,1,0:T(8,128)(2,1)S(1)} %choose.4), channel_id=1, source_target_pairs={{0,2},{1,3},{2,0},{3,1},{4,6},{5,7},{6,4},{7,5},{8,10},{9,11},{10,... | collective-permute-start | bytes 786440 | tf_op jit(solution)/shard_map/ppermute | solution.py:21
  34.3 10.3 %collective-permute-start.9 = (bf16[32,16,256]{2,1,0:T(8,128)(2,1)S(1)}, bf16[32,16,256]{2,1,0:T(8,128)(2,1)S(1)}, u32[]{:S(2)}, u32[]{:S(2)}) collective-permute-start(bf16[32,16,256]{2,1,0:T(8,128)(2,1)S(1)} %choose.5), channel_id=1, source_target_pairs={{0,2},{1,3},{2,0},{3,1},{4,6},{5,7},{6,4},{7,5},{8,10},{9,11},{10,... | collective-permute-start | bytes 786440 | tf_op jit(solution)/shard_map/ppermute | solution.py:21
  39.9 6.6 %collective-permute-start.12 = (bf16[32,16,256]{2,1,0:T(8,128)(2,1)S(1)}, bf16[32,16,256]{2,1,0:T(8,128)(2,1)S(1)}, u32[]{:S(2)}, u32[]{:S(2)}) collective-permute-start(bf16[32,16,256]{2,1,0:T(8,128)(2,1)S(1)} %choose.6), channel_id=1, source_target_pairs={{0,2},{1,3},{2,0},{3,1},{4,6},{5,7},{6,4},{7,5},{8,10},{9,11},{10,... | collective-permute-start | bytes 786440 | tf_op jit(solution)/shard_map/ppermute | solution.py:21
  44.4 7.6 %collective-permute-start.15 = (bf16[32,16,256]{2,1,0:T(8,128)(2,1)S(1)}, bf16[32,16,256]{2,1,0:T(8,128)(2,1)S(1)}, u32[]{:S(2)}, u32[]{:S(2)}) collective-permute-start(bf16[32,16,256]{2,1,0:T(8,128)(2,1)S(1)} %choose.7), channel_id=1, source_target_pairs={{0,2},{1,3},{2,0},{3,1},{4,6},{5,7},{6,4},{7,5},{8,10},{9,11},{10,... | collective-permute-start | bytes 786440 | tf_op jit(solution)/shard_map/ppermute | solution.py:21
  44.5 8.1 %collective-permute-start.7 = (bf16[2,32,16,256]{3,2,1,0:T(8,128)(2,1)S(1)}, bf16[2,32,16,256]{3,2,1,0:T(8,128)(2,1)S(1)}, u32[]{:S(2)}, u32[]{:S(2)}) collective-permute-start(bf16[2,32,16,256]{3,2,1,0:T(8,128)(2,1)S(1)} %join.4), channel_id=1, source_target_pairs={{0,1},{1,0},{2,3},{3,2},{4,5},{5,4},{6,7},{7,6},{8,9},{9,8},{10,11... | collective-permute-start | bytes 1572872 | tf_op jit(solution)/shard_map/ppermute | solution.py:21
  44.7 8.0 %collective-permute-start.10 = (bf16[2,32,16,256]{3,2,1,0:T(8,128)(2,1)S(1)}, bf16[2,32,16,256]{3,2,1,0:T(8,128)(2,1)S(1)}, u32[]{:S(2)}, u32[]{:S(2)}) collective-permute-start(bf16[2,32,16,256]{3,2,1,0:T(8,128)(2,1)S(1)} %join.5), channel_id=1, source_target_pairs={{0,1},{1,0},{2,3},{3,2},{4,5},{5,4},{6,7},{7,6},{8,9},{9,8},{10,11... | collective-permute-start | bytes 1572872 | tf_op jit(solution)/shard_map/ppermute | solution.py:21
  46.6 15.6 %collective-permute-start.13 = (bf16[2,32,16,256]{3,2,1,0:T(8,128)(2,1)S(1)}, bf16[2,32,16,256]{3,2,1,0:T(8,128)(2,1)S(1)}, u32[]{:S(2)}, u32[]{:S(2)}) collective-permute-start(bf16[2,32,16,256]{3,2,1,0:T(8,128)(2,1)S(1)} %join.6), channel_id=1, source_target_pairs={{0,1},{1,0},{2,3},{3,2},{4,5},{5,4},{6,7},{7,6},{8,9},{9,8},{10,11... | collective-permute-start | bytes 1572872 | tf_op jit(solution)/shard_map/ppermute | solution.py:21
  52.0 12.4 %collective-permute-start.16 = (bf16[2,32,16,256]{3,2,1,0:T(8,128)(2,1)S(1)}, bf16[2,32,16,256]{3,2,1,0:T(8,128)(2,1)S(1)}, u32[]{:S(2)}, u32[]{:S(2)}) collective-permute-start(bf16[2,32,16,256]{3,2,1,0:T(8,128)(2,1)S(1)} %join.7), channel_id=1, source_target_pairs={{0,1},{1,0},{2,3},{3,2},{4,5},{5,4},{6,7},{7,6},{8,9},{9,8},{10,11... | collective-permute-start | bytes 1572872 | tf_op jit(solution)/shard_map/ppermute | solution.py:21
  (6 other events, 34.8 us)

commit v3 on v2

--- a/solution.py
+++ b/solution.py
@@ -340,30 +340,29 @@
     for k in range(count):
         mot[1 + each * k: 1 + each * (k + 1)] = mots[k][...]
         mot_edge[8 + 8 * each * k: 8 + 8 * each * (k + 1)] = edges[k][...].reshape(8 * each, hid)
-    block = 16
-
-    acc = up_edge[...]
+    block = 32
+
+    pieces = []
     for a in range(3):
         for b in range(3):
-            pieces = [
+            pieces += [
                 jnp.concatenate([src[pl.ds(8 * a + 2 * b + side, rows, stride=8), :] for side in range(2)], axis=0)
-                for src in (hid_edge, mot_edge)]
-            acc += dot(jnp.concatenate(pieces, axis=1).astype(jnp.bfloat16),
-                       gates[3 * a + b, 0: 2 * hid, hid: 2 * hid])
+                .astype(jnp.bfloat16) for src in (hid_edge, mot_edge)]
+    weights = jnp.concatenate([gates[t, 0: 2 * hid, hid: 2 * hid] for t in range(9)], axis=0)
+    acc = dot(jnp.concatenate(pieces, axis=1), weights) + up_edge[...]
     centre = jnp.concatenate([hid_edge[pl.ds(8 + 2 + side, rows, stride=8), :] for side in range(2)], axis=0)
     reset = jax.nn.sigmoid(acc) * centre
     wide[pl.ds(7, rows, stride=32), :] = reset[:rows]
     wide[pl.ds(24, rows, stride=32), :] = reset[rows:]
 
-    def taps(first, weights, source, r0, start):
-        acc = start
+    def taps(weights, source, r0):
+        pieces = []
         for a in range(3):
             one = source[pl.ds(r0 + a, block)].reshape(block * 16, 3 * hid)
             two = mot[pl.ds(r0 + a, block)].reshape(block * 16, 3 * hid)
             for b in range(3):
-                lhs = jnp.concatenate([one[:, b * hid:(b + 1) * hid], two[:, b * hid:(b + 1) * hid]], axis=1)
-                acc += dot(lhs, weights[3 * a + b, 0: 2 * hid, :])
-        return acc
+                pieces += [one[:, b * hid:(b + 1) * hid], two[:, b * hid:(b + 1) * hid]]
+        return dot(jnp.concatenate(pieces, axis=1), jnp.concatenate([weights[t, 0: 2 * hid, :] for t in range(9)], axis=0))
 
     def upsampled(g, *refs):
         parts = []
@@ -374,7 +373,7 @@
 
     def gate_body(g, carry):
         r0 = g * block
-        acc = taps(0, gates, hid3, r0, upsampled(g, up_z, up_r))
+        acc = taps(gates, hid3, r0) + upsampled(g, up_z, up_r)
         both = jax.nn.sigmoid(acc)
         h = state[pl.ds(r0, block)].reshape(block * 16, hid).astype(jnp.float32)
         z_keep[pl.ds(r0 * 16, block * 16), :] = both[:, :hid]
@@ -391,7 +390,7 @@
 
     def cand_body(g, carry):
         r0 = g * block
-        q = jnp.tanh(taps(0, cand, res3, r0, upsampled(g, up_q)))
+        q = jnp.tanh(taps(cand, res3, r0) + upsampled(g, up_q))
         h = state[pl.ds(r0, block)].reshape(block * 16, hid).astype(jnp.float32)
         z = z_keep[pl.ds(r0 * 16, block * 16), :]
         new = (1.0 - z) * h + z * q

time: 71.9 us -> 70.5 us (0.981)
  Pallas kernels: 23.6 us -> 22.2 us
    pallas_call x2, Pallas kernels: 10.2 us -> 8.88 us  [fine_gru(): pl.pallas_call(kernel, grid=(1,), out_shape=jax.ShapeDtypeStruct(state.sh...]
  transfers between devices with their start and end apart: 17 -> 17, of which waited for: 8 -> 8; matrix products, arithmetic and copies ran while one was open for 1% -> 1% of each run, Pallas kernels for 22% -> 21%
where the time goes in v3:
time: 70.5 us; the launch traced here: 70.3 us
  waiting for transfers between devices  28.6 us (41%)
  Pallas kernels  22.2 us (31%)
  starting transfers between devices  16.3 us (23%)
  local copies, waits for them, and re-layouts  2.25 us (3%)
  between operations  0.97 us (1%)
    ppermute x17, waiting for transfers between devices, permute(): return lax.ppermute(value, 'cols', pairs)  28.6 us
    ppermute x17, starting transfers between devices, permute(): return lax.ppermute(value, 'cols', pairs)  16.3 us
    pallas_call x15, Pallas kernels, call(): pl.pallas_call(kernel, out_shape=tuple((pltpu.VMEM(shape, dtype) for shap...  13.4 us
    pallas_call x2, Pallas kernels, fine_gru(): pl.pallas_call(kernel, grid=(1,), out_shape=jax.ShapeDtypeStruct(state.sh...  8.88 us
  transfers between devices with their start and end apart: 17, of which 8 were waited for; matrix products, arithmetic and copies ran while one was open for 1% of the time, Pallas kernels for 21%

profile of v3, /device:TPU:0, one launch (start us, length us, event | category | flops | bytes accessed | tf_op | source)
XLA Modules:
  0.0 70.3 jit_solution(6583072684324256996)
XLA Ops:
  0.7 1.4 %slice_bitcast_fusion = (bf16[32,16,256]{2,1,0:T(8,128)(2,1)S(1)}, bf16[32,16,256]{2,1,0:T(8,128)(2,1)S(1)}, bf16[32,16,256]{2,1,0:T(8,128)(2,1)S(1)}, bf16[32,16,256]{2,1,0:T(8,128)(2,1)S(1)}) fusion(bf16[2,64,16,256]{3,2,1,0:T(8,128)(2,1)} %param.15), kind=kLoop, calls=%fused_computation | loop fusion | bytes 2097152 | tf_op jit(solution)/shard_map/squeeze | solution.py:467
  2.3 0.6 pack.1
  2.9 5.5 %collective-permute-start.1 = (bf16[688,256]{1,0:T(8,128)(2,1)S(1)}, bf16[688,256]{1,0:T(8,128)(2,1)S(1)}, u32[]{:S(2)}, u32[]{:S(2)}) collective-permute-start(bf16[688,256]{1,0:T(8,128)(2,1)S(1)} %get-tuple-element.37.to_prev), channel_id=1, source_target_pairs={{0,15},{1,0},{2,1},{3,2},{4,3},{5,4},{6,5},{7,6},{8,7},{9,8},{10,9... | collective-permute-start | bytes 1056776 | tf_op jit(solution)/shard_map/ppermute | solution.py:21
  8.4 1.2 %collective-permute-start.3 = (bf16[32,256]{1,0:T(8,128)(2,1)S(1)}, bf16[32,256]{1,0:T(8,128)(2,1)S(1)}, u32[]{:S(2)}, u32[]{:S(2)}) collective-permute-start(bf16[32,256]{1,0:T(8,128)(2,1)S(1)} %get-tuple-element.39.flat), channel_id=1, source_target_pairs={{0,2},{1,3},{2,4},{3,5},{4,6},{5,7},{6,8},{7,9},{8,10},{9,11},{10,... | collective-permute-start | bytes 49160 | tf_op jit(solution)/shard_map/ppermute | solution.py:21
  9.6 3.6 %collective-permute-start.4 = (bf16[32,256]{1,0:T(8,128)(2,1)S(1)}, bf16[32,256]{1,0:T(8,128)(2,1)S(1)}, u32[]{:S(2)}, u32[]{:S(2)}) collective-permute-start(bf16[32,256]{1,0:T(8,128)(2,1)S(1)} %get-tuple-element.39.flat), channel_id=1, source_target_pairs={{0,14},{1,15},{2,0},{3,1},{4,2},{5,3},{6,4},{7,5},{8,6},{9,7},{10,... | collective-permute-start | bytes 49160 | tf_op jit(solution)/shard_map/ppermute | solution.py:21
  13.2 1.9 %collective-permute-done.3.behind2 = bf16[32,256]{1,0:T(8,128)(2,1)S(1)} collective-permute-done((bf16[32,256]{1,0:T(8,128)(2,1)S(1)}, bf16[32,256]{1,0:T(8,128)(2,1)S(1)}, u32[]{:S(2)}, u32[]{:S(2)}) %collective-permute-start.3) | collective-permute-done | bytes 16416 | tf_op jit(solution)/shard_map/ppermute | solution.py:21
  15.1 2.5 %collective-permute-done.2.far = bf16[128,256]{1,0:T(8,128)(2,1)S(1)} collective-permute-done((bf16[128,256]{1,0:T(8,128)(2,1)S(1)}, bf16[128,256]{1,0:T(8,128)(2,1)S(1)}, u32[]{:S(2)}, u32[]{:S(2)}) %collective-permute-start.2) | collective-permute-done | bytes 65568 | tf_op jit(solution)/shard_map/ppermute | solution.py:21
  18.3 1.5 %collective-permute-start.11 = (bf16[32,16,256]{2,1,0:T(8,128)(2,1)S(1)}, bf16[32,16,256]{2,1,0:T(8,128)(2,1)S(1)}, u32[]{:S(2)}, u32[]{:S(2)}) collective-permute-start(bf16[32,16,256]{2,1,0:T(8,128)(2,1)S(1)} %get-tuple-element.64.refs_2_.mine.right), channel_id=1, source_target_pairs={{0,4},{1,5},{2,6},{3,7},{4,8},{5,9},{6,10},{7,11},{8,12},{9,13},{1... | collective-permute-start | bytes 786440 | tf_op jit(solution)/shard_map/ppermute | solution.py:21
  19.8 2.8 %collective-permute-start.14 = (bf16[32,16,256]{2,1,0:T(8,128)(2,1)S(1)}, bf16[32,16,256]{2,1,0:T(8,128)(2,1)S(1)}, u32[]{:S(2)}, u32[]{:S(2)}) collective-permute-start(bf16[32,16,256]{2,1,0:T(8,128)(2,1)S(1)} %get-tuple-element.66.refs_3_.mine.right), channel_id=1, source_target_pairs={{0,4},{1,5},{2,6},{3,7},{4,8},{5,9},{6,10},{7,11},{8,12},{9,13},{1... | collective-permute-start | bytes 786440 | tf_op jit(solution)/shard_map/ppermute | solution.py:21
  22.6 2.6 %edges.1 = (bf16[2,64,8,256]{3,2,1,0:T(8,128)(2,1)S(1)}, bf16[2,64,16,256]{3,2,1,0:T(8,128)(2,1)S(1)}, s32[2,64,24,128]{3,2,1,0:T(8,128)S(1)}, f32[2,528,128]{2,...) custom-call(s32[2]{0:T(128)S(1)} %copy-done.11, ...), custom_call_target="tpu_custom_call" | custom-call | bytes 7000000 | tf_op jit(solution)/shard_map/edges/pallas_call | solution.py:44
  25.2 1.3 %coarse.1 = (bf16[32,128]{1,0:T(8,128)(2,1)S(1)}, f32[768,128]{1,0:T(8,128)S(1)}, f32[768,128]{1,0:T(8,128)S(1)}, f32[768,128]{1,0:T(8,128)S(1)}, f32[2,128,128]{2,1,0:T(8,128)S(1)}) custom-call(bf16[32,256]{1,0:T(8,128)(2,1)S(1)} %collective-permute-done.3.behind2, bf16[432,256]{1,0:T(8,128)(2,1)S(1)} %collective-permute-done.prev, ...), custom_call_target="tpu_custom_call" | custom-call | bytes 5250000 | tf_op jit(solution)/shard_map/coarse/pallas_call | solution.py:44
  26.6 2.1 %collective-permute-done.5.came.b4 = bf16[32,16,256]{2,1,0:T(8,128)(2,1)S(1)} collective-permute-done((bf16[32,16,256]{2,1,0:T(8,128)(2,1)S(1)}, bf16[32,16,256]{2,1,0:T(8,128)(2,1)S(1)}, u32[]{:S(2)}, u32[]{:S(2)}) %collective-permute-start.5) | collective-permute-done | bytes 262176 | tf_op jit(solution)/shard_map/ppermute | solution.py:21
  28.7 5.5 %collective-permute-done.8.came.b4 = bf16[32,16,256]{2,1,0:T(8,128)(2,1)S(1)} collective-permute-done((bf16[32,16,256]{2,1,0:T(8,128)(2,1)S(1)}, bf16[32,16,256]{2,1,0:T(8,128)(2,1)S(1)}, u32[]{:S(2)}, u32[]{:S(2)}) %collective-permute-start.8) | collective-permute-done | bytes 262176 | tf_op jit(solution)/shard_map/ppermute | solution.py:21
  34.4 5.5 %collective-permute-done.11.came.b4 = bf16[32,16,256]{2,1,0:T(8,128)(2,1)S(1)} collective-permute-done((bf16[32,16,256]{2,1,0:T(8,128)(2,1)S(1)}, bf16[32,16,256]{2,1,0:T(8,128)(2,1)S(1)}, u32[]{:S(2)}, u32[]{:S(2)}) %collective-permute-start.11) | collective-permute-done | bytes 262176 | tf_op jit(solution)/shard_map/ppermute | solution.py:21
  40.0 4.4 %collective-permute-done.14.came.b4 = bf16[32,16,256]{2,1,0:T(8,128)(2,1)S(1)} collective-permute-done((bf16[32,16,256]{2,1,0:T(8,128)(2,1)S(1)}, bf16[32,16,256]{2,1,0:T(8,128)(2,1)S(1)}, u32[]{:S(2)}, u32[]{:S(2)}) %collective-permute-start.14) | collective-permute-done | bytes 262176 | tf_op jit(solution)/shard_map/ppermute | solution.py:21
  45.2 1.3 %collective-permute-done.12.second.b2 = bf16[32,16,256]{2,1,0:T(8,128)(2,1)S(1)} collective-permute-done((bf16[32,16,256]{2,1,0:T(8,128)(2,1)S(1)}, bf16[32,16,256]{2,1,0:T(8,128)(2,1)S(1)}, u32[]{:S(2)}, u32[]{:S(2)}) %collective-permute-start.12) | collective-permute-done | bytes 262176 | tf_op jit(solution)/shard_map/ppermute | solution.py:21
  46.7 5.3 %collective-permute-done.15.second.b2 = bf16[32,16,256]{2,1,0:T(8,128)(2,1)S(1)} collective-permute-done((bf16[32,16,256]{2,1,0:T(8,128)(2,1)S(1)}, bf16[32,16,256]{2,1,0:T(8,128)(2,1)S(1)}, u32[]{:S(2)}, u32[]{:S(2)}) %collective-permute-start.15) | collective-permute-done | bytes 262176 | tf_op jit(solution)/shard_map/ppermute | solution.py:21
  52.1 0.6 copy.19
  52.7 2.2 %motion.4 = (bf16[32,16,384]{2,1,0:T(8,128)(2,1)S(1)}, f32[32,8,128]{2,1,0:T(8,128)S(1)}) custom-call(f32[2,24,128]{2,1,0:T(8,128)S(1)} %get-tuple-element.45.scale, bf16[2,64,16,256]{3,2,1,0:T(8,128)(2,1)S(1)} %copy-done, bf16[2,64,8,256]{3,2,1,0:T(8,128)(2,1)S(1)} %get-tuple-element.46.left_edge, ...), custom_call_target="tpu_custom_call" | custom-call | bytes 9450000 | tf_op jit(solution)/shard_map/motion/pallas_call | solution.py:44
  54.9 2.2 %motion.5 = (bf16[32,16,384]{2,1,0:T(8,128)(2,1)S(1)}, f32[32,8,128]{2,1,0:T(8,128)S(1)}) custom-call(f32[2,24,128]{2,1,0:T(8,128)S(1)} %get-tuple-element.45.scale, bf16[2,64,16,256]{3,2,1,0:T(8,128)(2,1)S(1)} %copy-done, bf16[2,64,8,256]{3,2,1,0:T(8,128)(2,1)S(1)} %get-tuple-element.46.left_edge, ...), custom_call_target="tpu_custom_call" | custom-call | bytes 9450000 | tf_op jit(solution)/shard_map/motion/pallas_call | solution.py:44
  57.1 4.4 %fine_gru.2.refs_0_ = bf16[2,64,16,128]{3,2,1,0:T(8,128)(2,1)} custom-call(bf16[2,66,16,384]{3,2,1,0:T(8,128)(2,1)S(1)} %get-tuple-element.43.hid3, bf16[2,64,16,128]{3,2,1,0:T(8,128)(2,1)S(1)} %copy-done.2, f32[2,528,128]{2,1,0:T(8,128)S(1)} %get-tuple-element.44.hid_edge, bf16[32,16,384]{2,1,0:T(8,128)(2,1)S(1)} %get-tuple-element.55.refs_0_, ...), custom_call_target="tpu_custom_call" | custom-call | bytes 17500000 | tf_op jit(solution)/shard_map/fine_gru/pallas_call | solution.py:421
  61.5 2.2 %motion.6 = (bf16[32,16,384]{2,1,0:T(8,128)(2,1)S(1)}, f32[32,8,128]{2,1,0:T(8,128)S(1)}) custom-call(f32[2,24,128]{2,1,0:T(8,128)S(1)} %get-tuple-element.45.scale, bf16[2,64,16,256]{3,2,1,0:T(8,128)(2,1)S(1)} %copy-done, bf16[2,64,8,256]{3,2,1,0:T(8,128)(2,1)S(1)} %get-tuple-element.46.left_edge, ...), custom_call_target="tpu_custom_call" | custom-call | bytes 9450000 | tf_op jit(solution)/shard_map/motion/pallas_call | solution.py:44
  63.7 2.2 %motion.7 = (bf16[32,16,384]{2,1,0:T(8,128)(2,1)S(1)}, f32[32,8,128]{2,1,0:T(8,128)S(1)}) custom-call(f32[2,24,128]{2,1,0:T(8,128)S(1)} %get-tuple-element.45.scale, bf16[2,64,16,256]{3,2,1,0:T(8,128)(2,1)S(1)} %copy-done, bf16[2,64,8,256]{3,2,1,0:T(8,128)(2,1)S(1)} %get-tuple-element.46.left_edge, ...), custom_call_target="tpu_custom_call" | custom-call | bytes 9450000 | tf_op jit(solution)/shard_map/motion/pallas_call | solution.py:44
  65.9 4.4 %fine_gru.3 = bf16[2,64,16,128]{3,2,1,0:T(8,128)(2,1)} custom-call(bf16[2,66,16,384]{3,2,1,0:T(8,128)(2,1)S(1)} %get-tuple-element.43.hid3, bf16[2,64,16,128]{3,2,1,0:T(8,128)(2,1)S(1)} %copy-done.2, f32[2,528,128]{2,1,0:T(8,128)S(1)} %get-tuple-element.44.hid_edge, bf16[2,64,16,128]{3,2,1,0:T(8,128)(2,1)} %fine_gru.2.refs_0_, ...), custom_call_target="tpu_custom_call", output_to_operand_aliasing={{}: (3, {})} | custom-call | bytes 17500000 | tf_op jit(solution)/shard_map/fine_gru/pallas_call | solution.py:421
  (56 shorter events, 2.3 us)
Async XLA Ops:
  2.1 20.5 %copy-start.7 = (bf16[256,36]{1,0:T(8,128)(2,1)S(1)}, bf16[256,36]{1,0:T(8,128)(2,1)}, u32[]{:S(2)}) copy-start(bf16[256,36]{1,0:T(8,128)(2,1)} %constant.8.clone.pick) | copy-start | bytes 55300
  2.1 20.5 %copy-start.8 = (s32[24,128]{1,0:T(8,128)S(1)}, s32[24,128]{1,0:T(8,128)}, u32[]{:S(2)}) copy-start(s32[24,128]{1,0:T(8,128)} %constant.6.clone.distance) | copy-start | bytes 36868
  2.1 20.5 %copy-start.9 = (bf16[36,128]{1,0:T(8,128)(2,1)S(1)}, bf16[36,128]{1,0:T(8,128)(2,1)}, u32[]{:S(2)}) copy-start(bf16[36,128]{1,0:T(8,128)(2,1)} %motion_weight.1) | copy-start | bytes 27652
  2.3 22.9 %copy-start.3 = (bf16[9,384,128]{2,1,0:T(8,128)(2,1)S(1)}, bf16[9,384,128]{2,1,0:T(8,128)(2,1)}, u32[]{:S(2)}) copy-start(bf16[9,384,128]{2,1,0:T(8,128)(2,1)} %refs_10_.1) | copy-start | bytes 2654212
  2.3 22.9 %copy-start.4 = (bf16[9,256,256]{2,1,0:T(8,128)(2,1)S(1)}, bf16[9,256,256]{2,1,0:T(8,128)(2,1)}, u32[]{:S(2)}) copy-start(bf16[9,256,256]{2,1,0:T(8,128)(2,1)} %gates.1) | copy-start | bytes 3538948
  2.3 22.9 %copy-start.5 = (bf16[9,256,128]{2,1,0:T(8,128)(2,1)S(1)}, bf16[9,256,128]{2,1,0:T(8,128)(2,1)}, u32[]{:S(2)}) copy-start(bf16[9,256,128]{2,1,0:T(8,128)(2,1)} %cand.1) | copy-start | bytes 1769476
  2.9 22.3 %copy-start.1 = (bf16[9,384,256]{2,1,0:T(8,128)(2,1)S(1)}, bf16[9,384,256]{2,1,0:T(8,128)(2,1)}, u32[]{:S(2)}) copy-start(bf16[9,384,256]{2,1,0:T(8,128)(2,1)} %refs_9_.3) | copy-start | bytes 5308420
  2.9 14.7 %collective-permute-start.1 = (bf16[688,256]{1,0:T(8,128)(2,1)S(1)}, bf16[688,256]{1,0:T(8,128)(2,1)S(1)}, u32[]{:S(2)}, u32[]{:S(2)}) collective-permute-start(bf16[688,256]{1,0:T(8,128)(2,1)S(1)} %get-tuple-element.37.to_prev), channel_id=1, source_target_pairs={{0,15},{1,0},{2,1},{3,2},{4,3},{5,4},{6,5},{7,6},{8,7},{9,8},{10,9... | collective-permute-start | bytes 1056776 | tf_op jit(solution)/shard_map/ppermute | solution.py:21
  8.4 9.2 %collective-permute-start = (bf16[432,256]{1,0:T(8,128)(2,1)S(1)}, bf16[432,256]{1,0:T(8,128)(2,1)S(1)}, u32[]{:S(2)}, u32[]{:S(2)}) collective-permute-start(bf16[432,256]{1,0:T(8,128)(2,1)S(1)} %get-tuple-element.36.to_next), channel_id=1, source_target_pairs={{0,1},{1,2},{2,3},{3,4},{4,5},{5,6},{6,7},{7,8},{8,9},{9,10},{10,1... | collective-permute-start | bytes 663560 | tf_op jit(solution)/shard_map/ppermute | solution.py:21
  8.4 9.2 %collective-permute-start.2 = (bf16[128,256]{1,0:T(8,128)(2,1)S(1)}, bf16[128,256]{1,0:T(8,128)(2,1)S(1)}, u32[]{:S(2)}, u32[]{:S(2)}) collective-permute-start(bf16[128,256]{1,0:T(8,128)(2,1)S(1)} %get-tuple-element.38), channel_id=1, source_target_pairs={{0,5},{1,6},{2,7},{3,8},{4,9},{5,10},{6,11},{7,12},{8,13},{9,14},{... | collective-permute-start | bytes 196616 | tf_op jit(solution)/shard_map/ppermute | solution.py:21
  8.4 6.7 %collective-permute-start.3 = (bf16[32,256]{1,0:T(8,128)(2,1)S(1)}, bf16[32,256]{1,0:T(8,128)(2,1)S(1)}, u32[]{:S(2)}, u32[]{:S(2)}) collective-permute-start(bf16[32,256]{1,0:T(8,128)(2,1)S(1)} %get-tuple-element.39.flat), channel_id=1, source_target_pairs={{0,2},{1,3},{2,4},{3,5},{4,6},{5,7},{6,8},{7,9},{8,10},{9,11},{10,... | collective-permute-start | bytes 49160 | tf_op jit(solution)/shard_map/ppermute | solution.py:21
  9.6 5.5 %collective-permute-start.4 = (bf16[32,256]{1,0:T(8,128)(2,1)S(1)}, bf16[32,256]{1,0:T(8,128)(2,1)S(1)}, u32[]{:S(2)}, u32[]{:S(2)}) collective-permute-start(bf16[32,256]{1,0:T(8,128)(2,1)S(1)} %get-tuple-element.39.flat), channel_id=1, source_target_pairs={{0,14},{1,15},{2,0},{3,1},{4,2},{5,3},{6,4},{7,5},{8,6},{9,7},{10,... | collective-permute-start | bytes 49160 | tf_op jit(solution)/shard_map/ppermute | solution.py:21
  17.6 11.0 %collective-permute-start.5 = (bf16[32,16,256]{2,1,0:T(8,128)(2,1)S(1)}, bf16[32,16,256]{2,1,0:T(8,128)(2,1)S(1)}, u32[]{:S(2)}, u32[]{:S(2)}) collective-permute-start(bf16[32,16,256]{2,1,0:T(8,128)(2,1)S(1)} %get-tuple-element.47.refs_0_.mine.right), channel_id=1, source_target_pairs={{0,4},{1,5},{2,6},{3,7},{4,8},{5,9},{6,10},{7,11},{8,12},{9,13},{1... | collective-permute-start | bytes 786440 | tf_op jit(solution)/shard_map/ppermute | solution.py:21
  18.0 16.2 %collective-permute-start.8 = (bf16[32,16,256]{2,1,0:T(8,128)(2,1)S(1)}, bf16[32,16,256]{2,1,0:T(8,128)(2,1)S(1)}, u32[]{:S(2)}, u32[]{:S(2)}) collective-permute-start(bf16[32,16,256]{2,1,0:T(8,128)(2,1)S(1)} %get-tuple-element.56.refs_1_.mine.right), channel_id=1, source_target_pairs={{0,4},{1,5},{2,6},{3,7},{4,8},{5,9},{6,10},{7,11},{8,12},{9,13},{1... | collective-permute-start | bytes 786440 | tf_op jit(solution)/shard_map/ppermute | solution.py:21
  18.3 21.5 %collective-permute-start.11 = (bf16[32,16,256]{2,1,0:T(8,128)(2,1)S(1)}, bf16[32,16,256]{2,1,0:T(8,128)(2,1)S(1)}, u32[]{:S(2)}, u32[]{:S(2)}) collective-permute-start(bf16[32,16,256]{2,1,0:T(8,128)(2,1)S(1)} %get-tuple-element.64.refs_2_.mine.right), channel_id=1, source_target_pairs={{0,4},{1,5},{2,6},{3,7},{4,8},{5,9},{6,10},{7,11},{8,12},{9,13},{1... | collective-permute-start | bytes 786440 | tf_op jit(solution)/shard_map/ppermute | solution.py:21
  19.8 24.6 %collective-permute-start.14 = (bf16[32,16,256]{2,1,0:T(8,128)(2,1)S(1)}, bf16[32,16,256]{2,1,0:T(8,128)(2,1)S(1)}, u32[]{:S(2)}, u32[]{:S(2)}) collective-permute-start(bf16[32,16,256]{2,1,0:T(8,128)(2,1)S(1)} %get-tuple-element.66.refs_3_.mine.right), channel_id=1, source_target_pairs={{0,4},{1,5},{2,6},{3,7},{4,8},{5,9},{6,10},{7,11},{8,12},{9,13},{1... | collective-permute-start | bytes 786440 | tf_op jit(solution)/shard_map/ppermute | solution.py:21
  28.7 15.8 %collective-permute-start.6 = (bf16[32,16,256]{2,1,0:T(8,128)(2,1)S(1)}, bf16[32,16,256]{2,1,0:T(8,128)(2,1)S(1)}, u32[]{:S(2)}, u32[]{:S(2)}) collective-permute-start(bf16[32,16,256]{2,1,0:T(8,128)(2,1)S(1)} %choose.4), channel_id=1, source_target_pairs={{0,2},{1,3},{2,0},{3,1},{4,6},{5,7},{6,4},{7,5},{8,10},{9,11},{10,... | collective-permute-start | bytes 786440 | tf_op jit(solution)/shard_map/ppermute | solution.py:21
  34.3 10.3 %collective-permute-start.9 = (bf16[32,16,256]{2,1,0:T(8,128)(2,1)S(1)}, bf16[32,16,256]{2,1,0:T(8,128)(2,1)S(1)}, u32[]{:S(2)}, u32[]{:S(2)}) collective-permute-start(bf16[32,16,256]{2,1,0:T(8,128)(2,1)S(1)} %choose.5), channel_id=1, source_target_pairs={{0,2},{1,3},{2,0},{3,1},{4,6},{5,7},{6,4},{7,5},{8,10},{9,11},{10,... | collective-permute-start | bytes 786440 | tf_op jit(solution)/shard_map/ppermute | solution.py:21
  39.9 6.6 %collective-permute-start.12 = (bf16[32,16,256]{2,1,0:T(8,128)(2,1)S(1)}, bf16[32,16,256]{2,1,0:T(8,128)(2,1)S(1)}, u32[]{:S(2)}, u32[]{:S(2)}) collective-permute-start(bf16[32,16,256]{2,1,0:T(8,128)(2,1)S(1)} %choose.6), channel_id=1, source_target_pairs={{0,2},{1,3},{2,0},{3,1},{4,6},{5,7},{6,4},{7,5},{8,10},{9,11},{10,... | collective-permute-start | bytes 786440 | tf_op jit(solution)/shard_map/ppermute | solution.py:21
  44.4 7.6 %collective-permute-start.15 = (bf16[32,16,256]{2,1,0:T(8,128)(2,1)S(1)}, bf16[32,16,256]{2,1,0:T(8,128)(2,1)S(1)}, u32[]{:S(2)}, u32[]{:S(2)}) collective-permute-start(bf16[32,16,256]{2,1,0:T(8,128)(2,1)S(1)} %choose.7), channel_id=1, source_target_pairs={{0,2},{1,3},{2,0},{3,1},{4,6},{5,7},{6,4},{7,5},{8,10},{9,11},{10,... | collective-permute-start | bytes 786440 | tf_op jit(solution)/shard_map/ppermute | solution.py:21
  44.5 8.1 %collective-permute-start.7 = (bf16[2,32,16,256]{3,2,1,0:T(8,128)(2,1)S(1)}, bf16[2,32,16,256]{3,2,1,0:T(8,128)(2,1)S(1)}, u32[]{:S(2)}, u32[]{:S(2)}) collective-permute-start(bf16[2,32,16,256]{3,2,1,0:T(8,128)(2,1)S(1)} %join.4), channel_id=1, source_target_pairs={{0,1},{1,0},{2,3},{3,2},{4,5},{5,4},{6,7},{7,6},{8,9},{9,8},{10,11... | collective-permute-start | bytes 1572872 | tf_op jit(solution)/shard_map/ppermute | solution.py:21
  44.7 8.0 %collective-permute-start.10 = (bf16[2,32,16,256]{3,2,1,0:T(8,128)(2,1)S(1)}, bf16[2,32,16,256]{3,2,1,0:T(8,128)(2,1)S(1)}, u32[]{:S(2)}, u32[]{:S(2)}) collective-permute-start(bf16[2,32,16,256]{3,2,1,0:T(8,128)(2,1)S(1)} %join.5), channel_id=1, source_target_pairs={{0,1},{1,0},{2,3},{3,2},{4,5},{5,4},{6,7},{7,6},{8,9},{9,8},{10,11... | collective-permute-start | bytes 1572872 | tf_op jit(solution)/shard_map/ppermute | solution.py:21
  46.6 14.9 %collective-permute-start.13 = (bf16[2,32,16,256]{3,2,1,0:T(8,128)(2,1)S(1)}, bf16[2,32,16,256]{3,2,1,0:T(8,128)(2,1)S(1)}, u32[]{:S(2)}, u32[]{:S(2)}) collective-permute-start(bf16[2,32,16,256]{3,2,1,0:T(8,128)(2,1)S(1)} %join.6), channel_id=1, source_target_pairs={{0,1},{1,0},{2,3},{3,2},{4,5},{5,4},{6,7},{7,6},{8,9},{9,8},{10,11... | collective-permute-start | bytes 1572872 | tf_op jit(solution)/shard_map/ppermute | solution.py:21
  52.0 11.7 %collective-permute-start.16 = (bf16[2,32,16,256]{3,2,1,0:T(8,128)(2,1)S(1)}, bf16[2,32,16,256]{3,2,1,0:T(8,128)(2,1)S(1)}, u32[]{:S(2)}, u32[]{:S(2)}) collective-permute-start(bf16[2,32,16,256]{3,2,1,0:T(8,128)(2,1)S(1)} %join.7), channel_id=1, source_target_pairs={{0,1},{1,0},{2,3},{3,2},{4,5},{5,4},{6,7},{7,6},{8,9},{9,8},{10,11... | collective-permute-start | bytes 1572872 | tf_op jit(solution)/shard_map/ppermute | solution.py:21
  (6 other events, 34.8 us)

commit v4 on v3

--- a/solution.py
+++ b/solution.py
@@ -269,7 +269,7 @@
 def corr_kernel(scale, left, left_edge, right, right_edge, b4, b2, core, disp, start, table,
                 mot3, mot_edge, wide):
     rows = right.shape[0]
-    group = 8
+    group = 32
     odd = lax.rem(lax.axis_index("cols"), 2)
     scale = scale[...]
     lane = lax.broadcasted_iota(jnp.int32, (24, 128), 1)
@@ -320,7 +320,7 @@
                     b4, b2, core, disp.at[i, here], *rest)
 
     return call(kernel, "motion", [((rows, 16, 3 * hid), jnp.bfloat16), ((rows, 8, hid), jnp.float32)],
-                [pltpu.VMEM((8 * 32, hid), jnp.float32)],
+                [pltpu.VMEM((32 * 32, hid), jnp.float32)],
                 (scale, left, left_edge, right, right_edge, b4, b2, core, disp, start, table), 2.7)
 
 

time: 70.5 us -> 66.4 us (0.942)
  Pallas kernels: 22.2 us -> 18.2 us
    pallas_call x15, Pallas kernels: 13.4 us -> 9.33 us  [call(): pl.pallas_call(kernel, out_shape=tuple((pltpu.VMEM(shape, dtype) for shap...]
  transfers between devices with their start and end apart: 17 -> 17, of which waited for: 8 -> 8; matrix products, arithmetic and copies ran while one was open for 1% -> 1% of each run, Pallas kernels for 21% -> 18%
where the time goes in v4:
time: 66.4 us; the launch traced here: 66.2 us
  waiting for transfers between devices  28.6 us (43%)
  Pallas kernels  18.2 us (27%)
  starting transfers between devices  16.3 us (25%)
  local copies, waits for them, and re-layouts  2.25 us (3%)
  between operations  0.95 us (1%)
    ppermute x17, waiting for transfers between devices, permute(): return lax.ppermute(value, 'cols', pairs)  28.6 us
    ppermute x17, starting transfers between devices, permute(): return lax.ppermute(value, 'cols', pairs)  16.3 us
    pallas_call x15, Pallas kernels, call(): pl.pallas_call(kernel, out_shape=tuple((pltpu.VMEM(shape, dtype) for shap...  9.33 us
    pallas_call x2, Pallas kernels, fine_gru(): pl.pallas_call(kernel, grid=(1,), out_shape=jax.ShapeDtypeStruct(state.sh...  8.88 us
    squeeze x1, local copies, waits for them, and re-layouts, local(): own = [right_feat[i, k * each:(k + 1) * each] for i, k in keys]  1.37 us
  transfers between devices with their start and end apart: 17, of which 8 were waited for; matrix products, arithmetic and copies ran while one was open for 1% of the time, Pallas kernels for 18%

profile of v4, /device:TPU:0, one launch (start us, length us, event | category | flops | bytes accessed | tf_op | source)
XLA Modules:
  0.0 66.2 jit_solution(12784009796250973537)
XLA Ops:
  0.7 1.4 %slice_bitcast_fusion = (bf16[32,16,256]{2,1,0:T(8,128)(2,1)S(1)}, bf16[32,16,256]{2,1,0:T(8,128)(2,1)S(1)}, bf16[32,16,256]{2,1,0:T(8,128)(2,1)S(1)}, bf16[32,16,256]{2,1,0:T(8,128)(2,1)S(1)}) fusion(bf16[2,64,16,256]{3,2,1,0:T(8,128)(2,1)} %param.15), kind=kLoop, calls=%fused_computation | loop fusion | bytes 2097152 | tf_op jit(solution)/shard_map/squeeze | solution.py:467
  2.3 0.6 pack.1
  2.9 5.5 %collective-permute-start.1 = (bf16[688,256]{1,0:T(8,128)(2,1)S(1)}, bf16[688,256]{1,0:T(8,128)(2,1)S(1)}, u32[]{:S(2)}, u32[]{:S(2)}) collective-permute-start(bf16[688,256]{1,0:T(8,128)(2,1)S(1)} %get-tuple-element.37.to_prev), channel_id=1, source_target_pairs={{0,15},{1,0},{2,1},{3,2},{4,3},{5,4},{6,5},{7,6},{8,7},{9,8},{10,9... | collective-permute-start | bytes 1056776 | tf_op jit(solution)/shard_map/ppermute | solution.py:21
  8.4 1.2 %collective-permute-start.3 = (bf16[32,256]{1,0:T(8,128)(2,1)S(1)}, bf16[32,256]{1,0:T(8,128)(2,1)S(1)}, u32[]{:S(2)}, u32[]{:S(2)}) collective-permute-start(bf16[32,256]{1,0:T(8,128)(2,1)S(1)} %get-tuple-element.39.flat), channel_id=1, source_target_pairs={{0,2},{1,3},{2,4},{3,5},{4,6},{5,7},{6,8},{7,9},{8,10},{9,11},{10,... | collective-permute-start | bytes 49160 | tf_op jit(solution)/shard_map/ppermute | solution.py:21
  9.6 3.6 %collective-permute-start.4 = (bf16[32,256]{1,0:T(8,128)(2,1)S(1)}, bf16[32,256]{1,0:T(8,128)(2,1)S(1)}, u32[]{:S(2)}, u32[]{:S(2)}) collective-permute-start(bf16[32,256]{1,0:T(8,128)(2,1)S(1)} %get-tuple-element.39.flat), channel_id=1, source_target_pairs={{0,14},{1,15},{2,0},{3,1},{4,2},{5,3},{6,4},{7,5},{8,6},{9,7},{10,... | collective-permute-start | bytes 49160 | tf_op jit(solution)/shard_map/ppermute | solution.py:21
  13.2 1.9 %collective-permute-done.3.behind2 = bf16[32,256]{1,0:T(8,128)(2,1)S(1)} collective-permute-done((bf16[32,256]{1,0:T(8,128)(2,1)S(1)}, bf16[32,256]{1,0:T(8,128)(2,1)S(1)}, u32[]{:S(2)}, u32[]{:S(2)}) %collective-permute-start.3) | collective-permute-done | bytes 16416 | tf_op jit(solution)/shard_map/ppermute | solution.py:21
  15.1 2.5 %collective-permute-done.2.far = bf16[128,256]{1,0:T(8,128)(2,1)S(1)} collective-permute-done((bf16[128,256]{1,0:T(8,128)(2,1)S(1)}, bf16[128,256]{1,0:T(8,128)(2,1)S(1)}, u32[]{:S(2)}, u32[]{:S(2)}) %collective-permute-start.2) | collective-permute-done | bytes 65568 | tf_op jit(solution)/shard_map/ppermute | solution.py:21
  18.3 1.5 %collective-permute-start.11 = (bf16[32,16,256]{2,1,0:T(8,128)(2,1)S(1)}, bf16[32,16,256]{2,1,0:T(8,128)(2,1)S(1)}, u32[]{:S(2)}, u32[]{:S(2)}) collective-permute-start(bf16[32,16,256]{2,1,0:T(8,128)(2,1)S(1)} %get-tuple-element.64.refs_2_.mine.right), channel_id=1, source_target_pairs={{0,4},{1,5},{2,6},{3,7},{4,8},{5,9},{6,10},{7,11},{8,12},{9,13},{1... | collective-permute-start | bytes 786440 | tf_op jit(solution)/shard_map/ppermute | solution.py:21
  19.8 2.8 %collective-permute-start.14 = (bf16[32,16,256]{2,1,0:T(8,128)(2,1)S(1)}, bf16[32,16,256]{2,1,0:T(8,128)(2,1)S(1)}, u32[]{:S(2)}, u32[]{:S(2)}) collective-permute-start(bf16[32,16,256]{2,1,0:T(8,128)(2,1)S(1)} %get-tuple-element.66.refs_3_.mine.right), channel_id=1, source_target_pairs={{0,4},{1,5},{2,6},{3,7},{4,8},{5,9},{6,10},{7,11},{8,12},{9,13},{1... | collective-permute-start | bytes 786440 | tf_op jit(solution)/shard_map/ppermute | solution.py:21
  22.6 2.6 %edges.1 = (bf16[2,64,8,256]{3,2,1,0:T(8,128)(2,1)S(1)}, bf16[2,64,16,256]{3,2,1,0:T(8,128)(2,1)S(1)}, s32[2,64,24,128]{3,2,1,0:T(8,128)S(1)}, f32[2,528,128]{2,...) custom-call(s32[2]{0:T(128)S(1)} %copy-done.11, ...), custom_call_target="tpu_custom_call" | custom-call | bytes 7000000 | tf_op jit(solution)/shard_map/edges/pallas_call | solution.py:44
  25.2 1.3 %coarse.1 = (bf16[32,128]{1,0:T(8,128)(2,1)S(1)}, f32[768,128]{1,0:T(8,128)S(1)}, f32[768,128]{1,0:T(8,128)S(1)}, f32[768,128]{1,0:T(8,128)S(1)}, f32[2,128,128]{2,1,0:T(8,128)S(1)}) custom-call(bf16[32,256]{1,0:T(8,128)(2,1)S(1)} %collective-permute-done.3.behind2, bf16[432,256]{1,0:T(8,128)(2,1)S(1)} %collective-permute-done.prev, ...), custom_call_target="tpu_custom_call" | custom-call | bytes 5250000 | tf_op jit(solution)/shard_map/coarse/pallas_call | solution.py:44
  26.6 2.1 %collective-permute-done.5.came.b4 = bf16[32,16,256]{2,1,0:T(8,128)(2,1)S(1)} collective-permute-done((bf16[32,16,256]{2,1,0:T(8,128)(2,1)S(1)}, bf16[32,16,256]{2,1,0:T(8,128)(2,1)S(1)}, u32[]{:S(2)}, u32[]{:S(2)}) %collective-permute-start.5) | collective-permute-done | bytes 262176 | tf_op jit(solution)/shard_map/ppermute | solution.py:21
  28.7 5.5 %collective-permute-done.8.came.b4 = bf16[32,16,256]{2,1,0:T(8,128)(2,1)S(1)} collective-permute-done((bf16[32,16,256]{2,1,0:T(8,128)(2,1)S(1)}, bf16[32,16,256]{2,1,0:T(8,128)(2,1)S(1)}, u32[]{:S(2)}, u32[]{:S(2)}) %collective-permute-start.8) | collective-permute-done | bytes 262176 | tf_op jit(solution)/shard_map/ppermute | solution.py:21
  34.4 5.5 %collective-permute-done.11.came.b4 = bf16[32,16,256]{2,1,0:T(8,128)(2,1)S(1)} collective-permute-done((bf16[32,16,256]{2,1,0:T(8,128)(2,1)S(1)}, bf16[32,16,256]{2,1,0:T(8,128)(2,1)S(1)}, u32[]{:S(2)}, u32[]{:S(2)}) %collective-permute-start.11) | collective-permute-done | bytes 262176 | tf_op jit(solution)/shard_map/ppermute | solution.py:21
  40.0 4.4 %collective-permute-done.14.came.b4 = bf16[32,16,256]{2,1,0:T(8,128)(2,1)S(1)} collective-permute-done((bf16[32,16,256]{2,1,0:T(8,128)(2,1)S(1)}, bf16[32,16,256]{2,1,0:T(8,128)(2,1)S(1)}, u32[]{:S(2)}, u32[]{:S(2)}) %collective-permute-start.14) | collective-permute-done | bytes 262176 | tf_op jit(solution)/shard_map/ppermute | solution.py:21
  45.2 1.3 %collective-permute-done.12.second.b2 = bf16[32,16,256]{2,1,0:T(8,128)(2,1)S(1)} collective-permute-done((bf16[32,16,256]{2,1,0:T(8,128)(2,1)S(1)}, bf16[32,16,256]{2,1,0:T(8,128)(2,1)S(1)}, u32[]{:S(2)}, u32[]{:S(2)}) %collective-permute-start.12) | collective-permute-done | bytes 262176 | tf_op jit(solution)/shard_map/ppermute | solution.py:21
  46.7 5.3 %collective-permute-done.15.second.b2 = bf16[32,16,256]{2,1,0:T(8,128)(2,1)S(1)} collective-permute-done((bf16[32,16,256]{2,1,0:T(8,128)(2,1)S(1)}, bf16[32,16,256]{2,1,0:T(8,128)(2,1)S(1)}, u32[]{:S(2)}, u32[]{:S(2)}) %collective-permute-start.15) | collective-permute-done | bytes 262176 | tf_op jit(solution)/shard_map/ppermute | solution.py:21
  52.1 0.6 copy.19
  52.7 1.2 %motion.4 = (bf16[32,16,384]{2,1,0:T(8,128)(2,1)S(1)}, f32[32,8,128]{2,1,0:T(8,128)S(1)}) custom-call(f32[2,24,128]{2,1,0:T(8,128)S(1)} %get-tuple-element.45.scale, bf16[2,64,16,256]{3,2,1,0:T(8,128)(2,1)S(1)} %copy-done, bf16[2,64,8,256]{3,2,1,0:T(8,128)(2,1)S(1)} %get-tuple-element.46.left_edge, ...), custom_call_target="tpu_custom_call" | custom-call | bytes 9450000 | tf_op jit(solution)/shard_map/motion/pallas_call | solution.py:44
  53.9 1.2 %motion.5 = (bf16[32,16,384]{2,1,0:T(8,128)(2,1)S(1)}, f32[32,8,128]{2,1,0:T(8,128)S(1)}) custom-call(f32[2,24,128]{2,1,0:T(8,128)S(1)} %get-tuple-element.45.scale, bf16[2,64,16,256]{3,2,1,0:T(8,128)(2,1)S(1)} %copy-done, bf16[2,64,8,256]{3,2,1,0:T(8,128)(2,1)S(1)} %get-tuple-element.46.left_edge, ...), custom_call_target="tpu_custom_call" | custom-call | bytes 9450000 | tf_op jit(solution)/shard_map/motion/pallas_call | solution.py:44
  55.0 4.4 %fine_gru.2.refs_0_ = bf16[2,64,16,128]{3,2,1,0:T(8,128)(2,1)} custom-call(bf16[2,66,16,384]{3,2,1,0:T(8,128)(2,1)S(1)} %get-tuple-element.43.hid3, bf16[2,64,16,128]{3,2,1,0:T(8,128)(2,1)S(1)} %copy-done.2, f32[2,528,128]{2,1,0:T(8,128)S(1)} %get-tuple-element.44.hid_edge, bf16[32,16,384]{2,1,0:T(8,128)(2,1)S(1)} %get-tuple-element.55.refs_0_, ...), custom_call_target="tpu_custom_call" | custom-call | bytes 17500000 | tf_op jit(solution)/shard_map/fine_gru/pallas_call | solution.py:421
  59.5 1.2 %motion.6 = (bf16[32,16,384]{2,1,0:T(8,128)(2,1)S(1)}, f32[32,8,128]{2,1,0:T(8,128)S(1)}) custom-call(f32[2,24,128]{2,1,0:T(8,128)S(1)} %get-tuple-element.45.scale, bf16[2,64,16,256]{3,2,1,0:T(8,128)(2,1)S(1)} %copy-done, bf16[2,64,8,256]{3,2,1,0:T(8,128)(2,1)S(1)} %get-tuple-element.46.left_edge, ...), custom_call_target="tpu_custom_call" | custom-call | bytes 9450000 | tf_op jit(solution)/shard_map/motion/pallas_call | solution.py:44
  60.6 1.2 %motion.7 = (bf16[32,16,384]{2,1,0:T(8,128)(2,1)S(1)}, f32[32,8,128]{2,1,0:T(8,128)S(1)}) custom-call(f32[2,24,128]{2,1,0:T(8,128)S(1)} %get-tuple-element.45.scale, bf16[2,64,16,256]{3,2,1,0:T(8,128)(2,1)S(1)} %copy-done, bf16[2,64,8,256]{3,2,1,0:T(8,128)(2,1)S(1)} %get-tuple-element.46.left_edge, ...), custom_call_target="tpu_custom_call" | custom-call | bytes 9450000 | tf_op jit(solution)/shard_map/motion/pallas_call | solution.py:44
  61.8 4.4 %fine_gru.3 = bf16[2,64,16,128]{3,2,1,0:T(8,128)(2,1)} custom-call(bf16[2,66,16,384]{3,2,1,0:T(8,128)(2,1)S(1)} %get-tuple-element.43.hid3, bf16[2,64,16,128]{3,2,1,0:T(8,128)(2,1)S(1)} %copy-done.2, f32[2,528,128]{2,1,0:T(8,128)S(1)} %get-tuple-element.44.hid_edge, bf16[2,64,16,128]{3,2,1,0:T(8,128)(2,1)} %fine_gru.2.refs_0_, ...), custom_call_target="tpu_custom_call", output_to_operand_aliasing={{}: (3, {})} | custom-call | bytes 17500000 | tf_op jit(solution)/shard_map/fine_gru/pallas_call | solution.py:421
  (56 shorter events, 2.3 us)
Async XLA Ops:
  2.1 20.5 %copy-start.7 = (bf16[256,36]{1,0:T(8,128)(2,1)S(1)}, bf16[256,36]{1,0:T(8,128)(2,1)}, u32[]{:S(2)}) copy-start(bf16[256,36]{1,0:T(8,128)(2,1)} %constant.8.clone.pick) | copy-start | bytes 55300
  2.1 20.5 %copy-start.8 = (s32[24,128]{1,0:T(8,128)S(1)}, s32[24,128]{1,0:T(8,128)}, u32[]{:S(2)}) copy-start(s32[24,128]{1,0:T(8,128)} %constant.6.clone.distance) | copy-start | bytes 36868
  2.1 20.5 %copy-start.9 = (bf16[36,128]{1,0:T(8,128)(2,1)S(1)}, bf16[36,128]{1,0:T(8,128)(2,1)}, u32[]{:S(2)}) copy-start(bf16[36,128]{1,0:T(8,128)(2,1)} %motion_weight.1) | copy-start | bytes 27652
  2.3 22.9 %copy-start.3 = (bf16[9,384,128]{2,1,0:T(8,128)(2,1)S(1)}, bf16[9,384,128]{2,1,0:T(8,128)(2,1)}, u32[]{:S(2)}) copy-start(bf16[9,384,128]{2,1,0:T(8,128)(2,1)} %refs_10_.1) | copy-start | bytes 2654212
  2.3 22.9 %copy-start.4 = (bf16[9,256,256]{2,1,0:T(8,128)(2,1)S(1)}, bf16[9,256,256]{2,1,0:T(8,128)(2,1)}, u32[]{:S(2)}) copy-start(bf16[9,256,256]{2,1,0:T(8,128)(2,1)} %gates.1) | copy-start | bytes 3538948
  2.3 22.9 %copy-start.5 = (bf16[9,256,128]{2,1,0:T(8,128)(2,1)S(1)}, bf16[9,256,128]{2,1,0:T(8,128)(2,1)}, u32[]{:S(2)}) copy-start(bf16[9,256,128]{2,1,0:T(8,128)(2,1)} %cand.1) | copy-start | bytes 1769476
  2.9 22.3 %copy-start.1 = (bf16[9,384,256]{2,1,0:T(8,128)(2,1)S(1)}, bf16[9,384,256]{2,1,0:T(8,128)(2,1)}, u32[]{:S(2)}) copy-start(bf16[9,384,256]{2,1,0:T(8,128)(2,1)} %refs_9_.3) | copy-start | bytes 5308420
  2.9 14.7 %collective-permute-start.1 = (bf16[688,256]{1,0:T(8,128)(2,1)S(1)}, bf16[688,256]{1,0:T(8,128)(2,1)S(1)}, u32[]{:S(2)}, u32[]{:S(2)}) collective-permute-start(bf16[688,256]{1,0:T(8,128)(2,1)S(1)} %get-tuple-element.37.to_prev), channel_id=1, source_target_pairs={{0,15},{1,0},{2,1},{3,2},{4,3},{5,4},{6,5},{7,6},{8,7},{9,8},{10,9... | collective-permute-start | bytes 1056776 | tf_op jit(solution)/shard_map/ppermute | solution.py:21
  8.4 9.2 %collective-permute-start = (bf16[432,256]{1,0:T(8,128)(2,1)S(1)}, bf16[432,256]{1,0:T(8,128)(2,1)S(1)}, u32[]{:S(2)}, u32[]{:S(2)}) collective-permute-start(bf16[432,256]{1,0:T(8,128)(2,1)S(1)} %get-tuple-element.36.to_next), channel_id=1, source_target_pairs={{0,1},{1,2},{2,3},{3,4},{4,5},{5,6},{6,7},{7,8},{8,9},{9,10},{10,1... | collective-permute-start | bytes 663560 | tf_op jit(solution)/shard_map/ppermute | solution.py:21
  8.4 9.2 %collective-permute-start.2 = (bf16[128,256]{1,0:T(8,128)(2,1)S(1)}, bf16[128,256]{1,0:T(8,128)(2,1)S(1)}, u32[]{:S(2)}, u32[]{:S(2)}) collective-permute-start(bf16[128,256]{1,0:T(8,128)(2,1)S(1)} %get-tuple-element.38), channel_id=1, source_target_pairs={{0,5},{1,6},{2,7},{3,8},{4,9},{5,10},{6,11},{7,12},{8,13},{9,14},{... | collective-permute-start | bytes 196616 | tf_op jit(solution)/shard_map/ppermute | solution.py:21
  8.4 6.7 %collective-permute-start.3 = (bf16[32,256]{1,0:T(8,128)(2,1)S(1)}, bf16[32,256]{1,0:T(8,128)(2,1)S(1)}, u32[]{:S(2)}, u32[]{:S(2)}) collective-permute-start(bf16[32,256]{1,0:T(8,128)(2,1)S(1)} %get-tuple-element.39.flat), channel_id=1, source_target_pairs={{0,2},{1,3},{2,4},{3,5},{4,6},{5,7},{6,8},{7,9},{8,10},{9,11},{10,... | collective-permute-start | bytes 49160 | tf_op jit(solution)/shard_map/ppermute | solution.py:21
  9.6 5.5 %collective-permute-start.4 = (bf16[32,256]{1,0:T(8,128)(2,1)S(1)}, bf16[32,256]{1,0:T(8,128)(2,1)S(1)}, u32[]{:S(2)}, u32[]{:S(2)}) collective-permute-start(bf16[32,256]{1,0:T(8,128)(2,1)S(1)} %get-tuple-element.39.flat), channel_id=1, source_target_pairs={{0,14},{1,15},{2,0},{3,1},{4,2},{5,3},{6,4},{7,5},{8,6},{9,7},{10,... | collective-permute-start | bytes 49160 | tf_op jit(solution)/shard_map/ppermute | solution.py:21
  17.6 11.0 %collective-permute-start.5 = (bf16[32,16,256]{2,1,0:T(8,128)(2,1)S(1)}, bf16[32,16,256]{2,1,0:T(8,128)(2,1)S(1)}, u32[]{:S(2)}, u32[]{:S(2)}) collective-permute-start(bf16[32,16,256]{2,1,0:T(8,128)(2,1)S(1)} %get-tuple-element.47.refs_0_.mine.right), channel_id=1, source_target_pairs={{0,4},{1,5},{2,6},{3,7},{4,8},{5,9},{6,10},{7,11},{8,12},{9,13},{1... | collective-permute-start | bytes 786440 | tf_op jit(solution)/shard_map/ppermute | solution.py:21
  18.0 16.2 %collective-permute-start.8 = (bf16[32,16,256]{2,1,0:T(8,128)(2,1)S(1)}, bf16[32,16,256]{2,1,0:T(8,128)(2,1)S(1)}, u32[]{:S(2)}, u32[]{:S(2)}) collective-permute-start(bf16[32,16,256]{2,1,0:T(8,128)(2,1)S(1)} %get-tuple-element.56.refs_1_.mine.right), channel_id=1, source_target_pairs={{0,4},{1,5},{2,6},{3,7},{4,8},{5,9},{6,10},{7,11},{8,12},{9,13},{1... | collective-permute-start | bytes 786440 | tf_op jit(solution)/shard_map/ppermute | solution.py:21
  18.3 21.5 %collective-permute-start.11 = (bf16[32,16,256]{2,1,0:T(8,128)(2,1)S(1)}, bf16[32,16,256]{2,1,0:T(8,128)(2,1)S(1)}, u32[]{:S(2)}, u32[]{:S(2)}) collective-permute-start(bf16[32,16,256]{2,1,0:T(8,128)(2,1)S(1)} %get-tuple-element.64.refs_2_.mine.right), channel_id=1, source_target_pairs={{0,4},{1,5},{2,6},{3,7},{4,8},{5,9},{6,10},{7,11},{8,12},{9,13},{1... | collective-permute-start | bytes 786440 | tf_op jit(solution)/shard_map/ppermute | solution.py:21
  19.8 24.6 %collective-permute-start.14 = (bf16[32,16,256]{2,1,0:T(8,128)(2,1)S(1)}, bf16[32,16,256]{2,1,0:T(8,128)(2,1)S(1)}, u32[]{:S(2)}, u32[]{:S(2)}) collective-permute-start(bf16[32,16,256]{2,1,0:T(8,128)(2,1)S(1)} %get-tuple-element.66.refs_3_.mine.right), channel_id=1, source_target_pairs={{0,4},{1,5},{2,6},{3,7},{4,8},{5,9},{6,10},{7,11},{8,12},{9,13},{1... | collective-permute-start | bytes 786440 | tf_op jit(solution)/shard_map/ppermute | solution.py:21
  28.7 15.8 %collective-permute-start.6 = (bf16[32,16,256]{2,1,0:T(8,128)(2,1)S(1)}, bf16[32,16,256]{2,1,0:T(8,128)(2,1)S(1)}, u32[]{:S(2)}, u32[]{:S(2)}) collective-permute-start(bf16[32,16,256]{2,1,0:T(8,128)(2,1)S(1)} %choose.4), channel_id=1, source_target_pairs={{0,2},{1,3},{2,0},{3,1},{4,6},{5,7},{6,4},{7,5},{8,10},{9,11},{10,... | collective-permute-start | bytes 786440 | tf_op jit(solution)/shard_map/ppermute | solution.py:21
  34.3 10.3 %collective-permute-start.9 = (bf16[32,16,256]{2,1,0:T(8,128)(2,1)S(1)}, bf16[32,16,256]{2,1,0:T(8,128)(2,1)S(1)}, u32[]{:S(2)}, u32[]{:S(2)}) collective-permute-start(bf16[32,16,256]{2,1,0:T(8,128)(2,1)S(1)} %choose.5), channel_id=1, source_target_pairs={{0,2},{1,3},{2,0},{3,1},{4,6},{5,7},{6,4},{7,5},{8,10},{9,11},{10,... | collective-permute-start | bytes 786440 | tf_op jit(solution)/shard_map/ppermute | solution.py:21
  39.9 6.6 %collective-permute-start.12 = (bf16[32,16,256]{2,1,0:T(8,128)(2,1)S(1)}, bf16[32,16,256]{2,1,0:T(8,128)(2,1)S(1)}, u32[]{:S(2)}, u32[]{:S(2)}) collective-permute-start(bf16[32,16,256]{2,1,0:T(8,128)(2,1)S(1)} %choose.6), channel_id=1, source_target_pairs={{0,2},{1,3},{2,0},{3,1},{4,6},{5,7},{6,4},{7,5},{8,10},{9,11},{10,... | collective-permute-start | bytes 786440 | tf_op jit(solution)/shard_map/ppermute | solution.py:21
  44.4 7.6 %collective-permute-start.15 = (bf16[32,16,256]{2,1,0:T(8,128)(2,1)S(1)}, bf16[32,16,256]{2,1,0:T(8,128)(2,1)S(1)}, u32[]{:S(2)}, u32[]{:S(2)}) collective-permute-start(bf16[32,16,256]{2,1,0:T(8,128)(2,1)S(1)} %choose.7), channel_id=1, source_target_pairs={{0,2},{1,3},{2,0},{3,1},{4,6},{5,7},{6,4},{7,5},{8,10},{9,11},{10,... | collective-permute-start | bytes 786440 | tf_op jit(solution)/shard_map/ppermute | solution.py:21
  44.5 8.1 %collective-permute-start.7 = (bf16[2,32,16,256]{3,2,1,0:T(8,128)(2,1)S(1)}, bf16[2,32,16,256]{3,2,1,0:T(8,128)(2,1)S(1)}, u32[]{:S(2)}, u32[]{:S(2)}) collective-permute-start(bf16[2,32,16,256]{3,2,1,0:T(8,128)(2,1)S(1)} %join.4), channel_id=1, source_target_pairs={{0,1},{1,0},{2,3},{3,2},{4,5},{5,4},{6,7},{7,6},{8,9},{9,8},{10,11... | collective-permute-start | bytes 1572872 | tf_op jit(solution)/shard_map/ppermute | solution.py:21
  44.7 8.0 %collective-permute-start.10 = (bf16[2,32,16,256]{3,2,1,0:T(8,128)(2,1)S(1)}, bf16[2,32,16,256]{3,2,1,0:T(8,128)(2,1)S(1)}, u32[]{:S(2)}, u32[]{:S(2)}) collective-permute-start(bf16[2,32,16,256]{3,2,1,0:T(8,128)(2,1)S(1)} %join.5), channel_id=1, source_target_pairs={{0,1},{1,0},{2,3},{3,2},{4,5},{5,4},{6,7},{7,6},{8,9},{9,8},{10,11... | collective-permute-start | bytes 1572872 | tf_op jit(solution)/shard_map/ppermute | solution.py:21
  46.6 12.9 %collective-permute-start.13 = (bf16[2,32,16,256]{3,2,1,0:T(8,128)(2,1)S(1)}, bf16[2,32,16,256]{3,2,1,0:T(8,128)(2,1)S(1)}, u32[]{:S(2)}, u32[]{:S(2)}) collective-permute-start(bf16[2,32,16,256]{3,2,1,0:T(8,128)(2,1)S(1)} %join.6), channel_id=1, source_target_pairs={{0,1},{1,0},{2,3},{3,2},{4,5},{5,4},{6,7},{7,6},{8,9},{9,8},{10,11... | collective-permute-start | bytes 1572872 | tf_op jit(solution)/shard_map/ppermute | solution.py:21
  52.0 8.6 %collective-permute-start.16 = (bf16[2,32,16,256]{3,2,1,0:T(8,128)(2,1)S(1)}, bf16[2,32,16,256]{3,2,1,0:T(8,128)(2,1)S(1)}, u32[]{:S(2)}, u32[]{:S(2)}) collective-permute-start(bf16[2,32,16,256]{3,2,1,0:T(8,128)(2,1)S(1)} %join.7), channel_id=1, source_target_pairs={{0,1},{1,0},{2,3},{3,2},{4,5},{5,4},{6,7},{7,6},{8,9},{9,8},{10,11... | collective-permute-start | bytes 1572872 | tf_op jit(solution)/shard_map/ppermute | solution.py:21
  (6 other events, 34.8 us)

commit v5 on v4

--- a/solution.py
+++ b/solution.py
@@ -388,6 +388,8 @@
 
     lax.fori_loop(0, rows // block, gate_body, 0)
 
+    block = 64
+
     def cand_body(g, carry):
         r0 = g * block
         q = jnp.tanh(taps(cand, res3, r0) + upsampled(g, up_q))

time: 66.4 us -> 66.2 us (level)
  no operation moved by 1% of the time
where the time goes in v5:
time: 66.2 us; the launch traced here: 66 us
  waiting for transfers between devices  28.6 us (43%)
  Pallas kernels  18 us (27%)
  starting transfers between devices  16.3 us (25%)
  local copies, waits for them, and re-layouts  2.25 us (3%)
  between operations  0.96 us (1%)
    ppermute x17, waiting for transfers between devices, permute(): return lax.ppermute(value, 'cols', pairs)  28.6 us
    ppermute x17, starting transfers between devices, permute(): return lax.ppermute(value, 'cols', pairs)  16.3 us
    pallas_call x15, Pallas kernels, call(): pl.pallas_call(kernel, out_shape=tuple((pltpu.VMEM(shape, dtype) for shap...  9.51 us
    pallas_call x2, Pallas kernels, fine_gru(): pl.pallas_call(kernel, grid=(1,), out_shape=jax.ShapeDtypeStruct(state.sh...  8.48 us
    squeeze x1, local copies, waits for them, and re-layouts, local(): own = [right_feat[i, k * each:(k + 1) * each] for i, k in keys]  1.37 us
  transfers between devices with their start and end apart: 17, of which 8 were waited for; matrix products, arithmetic and copies ran while one was open for 1% of the time, Pallas kernels for 18%

profile of v5, /device:TPU:0, one launch (start us, length us, event | category | flops | bytes accessed | tf_op | source)
XLA Modules:
  0.0 66.0 jit_solution(17912538994032566059)
XLA Ops:
  0.7 1.4 %slice_bitcast_fusion = (bf16[32,16,256]{2,1,0:T(8,128)(2,1)S(1)}, bf16[32,16,256]{2,1,0:T(8,128)(2,1)S(1)}, bf16[32,16,256]{2,1,0:T(8,128)(2,1)S(1)}, bf16[32,16,256]{2,1,0:T(8,128)(2,1)S(1)}) fusion(bf16[2,64,16,256]{3,2,1,0:T(8,128)(2,1)} %param.15), kind=kLoop, calls=%fused_computation | loop fusion | bytes 2097152 | tf_op jit(solution)/shard_map/squeeze | solution.py:469
  2.3 0.6 pack.1
  2.9 5.5 %collective-permute-start.1 = (bf16[688,256]{1,0:T(8,128)(2,1)S(1)}, bf16[688,256]{1,0:T(8,128)(2,1)S(1)}, u32[]{:S(2)}, u32[]{:S(2)}) collective-permute-start(bf16[688,256]{1,0:T(8,128)(2,1)S(1)} %get-tuple-element.37.to_prev), channel_id=1, source_target_pairs={{0,15},{1,0},{2,1},{3,2},{4,3},{5,4},{6,5},{7,6},{8,7},{9,8},{10,9... | collective-permute-start | bytes 1056776 | tf_op jit(solution)/shard_map/ppermute | solution.py:21
  8.4 1.2 %collective-permute-start.3 = (bf16[32,256]{1,0:T(8,128)(2,1)S(1)}, bf16[32,256]{1,0:T(8,128)(2,1)S(1)}, u32[]{:S(2)}, u32[]{:S(2)}) collective-permute-start(bf16[32,256]{1,0:T(8,128)(2,1)S(1)} %get-tuple-element.39.flat), channel_id=1, source_target_pairs={{0,2},{1,3},{2,4},{3,5},{4,6},{5,7},{6,8},{7,9},{8,10},{9,11},{10,... | collective-permute-start | bytes 49160 | tf_op jit(solution)/shard_map/ppermute | solution.py:21
  9.6 3.6 %collective-permute-start.4 = (bf16[32,256]{1,0:T(8,128)(2,1)S(1)}, bf16[32,256]{1,0:T(8,128)(2,1)S(1)}, u32[]{:S(2)}, u32[]{:S(2)}) collective-permute-start(bf16[32,256]{1,0:T(8,128)(2,1)S(1)} %get-tuple-element.39.flat), channel_id=1, source_target_pairs={{0,14},{1,15},{2,0},{3,1},{4,2},{5,3},{6,4},{7,5},{8,6},{9,7},{10,... | collective-permute-start | bytes 49160 | tf_op jit(solution)/shard_map/ppermute | solution.py:21
  13.2 1.9 %collective-permute-done.3.behind2 = bf16[32,256]{1,0:T(8,128)(2,1)S(1)} collective-permute-done((bf16[32,256]{1,0:T(8,128)(2,1)S(1)}, bf16[32,256]{1,0:T(8,128)(2,1)S(1)}, u32[]{:S(2)}, u32[]{:S(2)}) %collective-permute-start.3) | collective-permute-done | bytes 16416 | tf_op jit(solution)/shard_map/ppermute | solution.py:21
  15.1 2.5 %collective-permute-done.2.far = bf16[128,256]{1,0:T(8,128)(2,1)S(1)} collective-permute-done((bf16[128,256]{1,0:T(8,128)(2,1)S(1)}, bf16[128,256]{1,0:T(8,128)(2,1)S(1)}, u32[]{:S(2)}, u32[]{:S(2)}) %collective-permute-start.2) | collective-permute-done | bytes 65568 | tf_op jit(solution)/shard_map/ppermute | solution.py:21
  18.3 1.5 %collective-permute-start.11 = (bf16[32,16,256]{2,1,0:T(8,128)(2,1)S(1)}, bf16[32,16,256]{2,1,0:T(8,128)(2,1)S(1)}, u32[]{:S(2)}, u32[]{:S(2)}) collective-permute-start(bf16[32,16,256]{2,1,0:T(8,128)(2,1)S(1)} %get-tuple-element.64.refs_2_.mine.right), channel_id=1, source_target_pairs={{0,4},{1,5},{2,6},{3,7},{4,8},{5,9},{6,10},{7,11},{8,12},{9,13},{1... | collective-permute-start | bytes 786440 | tf_op jit(solution)/shard_map/ppermute | solution.py:21
  19.8 2.8 %collective-permute-start.14 = (bf16[32,16,256]{2,1,0:T(8,128)(2,1)S(1)}, bf16[32,16,256]{2,1,0:T(8,128)(2,1)S(1)}, u32[]{:S(2)}, u32[]{:S(2)}) collective-permute-start(bf16[32,16,256]{2,1,0:T(8,128)(2,1)S(1)} %get-tuple-element.66.refs_3_.mine.right), channel_id=1, source_target_pairs={{0,4},{1,5},{2,6},{3,7},{4,8},{5,9},{6,10},{7,11},{8,12},{9,13},{1... | collective-permute-start | bytes 786440 | tf_op jit(solution)/shard_map/ppermute | solution.py:21
  22.6 2.5 %edges.1 = (bf16[2,64,8,256]{3,2,1,0:T(8,128)(2,1)S(1)}, bf16[2,64,16,256]{3,2,1,0:T(8,128)(2,1)S(1)}, s32[2,64,24,128]{3,2,1,0:T(8,128)S(1)}, f32[2,528,128]{2,...) custom-call(s32[2]{0:T(128)S(1)} %copy-done.11, ...), custom_call_target="tpu_custom_call" | custom-call | bytes 7000000 | tf_op jit(solution)/shard_map/edges/pallas_call | solution.py:44
  25.2 1.3 %coarse.1 = (bf16[32,128]{1,0:T(8,128)(2,1)S(1)}, f32[768,128]{1,0:T(8,128)S(1)}, f32[768,128]{1,0:T(8,128)S(1)}, f32[768,128]{1,0:T(8,128)S(1)}, f32[2,128,128]{2,1,0:T(8,128)S(1)}) custom-call(bf16[32,256]{1,0:T(8,128)(2,1)S(1)} %collective-permute-done.3.behind2, bf16[432,256]{1,0:T(8,128)(2,1)S(1)} %collective-permute-done.prev, ...), custom_call_target="tpu_custom_call" | custom-call | bytes 5250000 | tf_op jit(solution)/shard_map/coarse/pallas_call | solution.py:44
  26.6 2.1 %collective-permute-done.5.came.b4 = bf16[32,16,256]{2,1,0:T(8,128)(2,1)S(1)} collective-permute-done((bf16[32,16,256]{2,1,0:T(8,128)(2,1)S(1)}, bf16[32,16,256]{2,1,0:T(8,128)(2,1)S(1)}, u32[]{:S(2)}, u32[]{:S(2)}) %collective-permute-start.5) | collective-permute-done | bytes 262176 | tf_op jit(solution)/shard_map/ppermute | solution.py:21
  28.7 5.5 %collective-permute-done.8.came.b4 = bf16[32,16,256]{2,1,0:T(8,128)(2,1)S(1)} collective-permute-done((bf16[32,16,256]{2,1,0:T(8,128)(2,1)S(1)}, bf16[32,16,256]{2,1,0:T(8,128)(2,1)S(1)}, u32[]{:S(2)}, u32[]{:S(2)}) %collective-permute-start.8) | collective-permute-done | bytes 262176 | tf_op jit(solution)/shard_map/ppermute | solution.py:21
  34.4 5.5 %collective-permute-done.11.came.b4 = bf16[32,16,256]{2,1,0:T(8,128)(2,1)S(1)} collective-permute-done((bf16[32,16,256]{2,1,0:T(8,128)(2,1)S(1)}, bf16[32,16,256]{2,1,0:T(8,128)(2,1)S(1)}, u32[]{:S(2)}, u32[]{:S(2)}) %collective-permute-start.11) | collective-permute-done | bytes 262176 | tf_op jit(solution)/shard_map/ppermute | solution.py:21
  40.0 4.4 %collective-permute-done.14.came.b4 = bf16[32,16,256]{2,1,0:T(8,128)(2,1)S(1)} collective-permute-done((bf16[32,16,256]{2,1,0:T(8,128)(2,1)S(1)}, bf16[32,16,256]{2,1,0:T(8,128)(2,1)S(1)}, u32[]{:S(2)}, u32[]{:S(2)}) %collective-permute-start.14) | collective-permute-done | bytes 262176 | tf_op jit(solution)/shard_map/ppermute | solution.py:21
  45.2 1.3 %collective-permute-done.12.second.b2 = bf16[32,16,256]{2,1,0:T(8,128)(2,1)S(1)} collective-permute-done((bf16[32,16,256]{2,1,0:T(8,128)(2,1)S(1)}, bf16[32,16,256]{2,1,0:T(8,128)(2,1)S(1)}, u32[]{:S(2)}, u32[]{:S(2)}) %collective-permute-start.12) | collective-permute-done | bytes 262176 | tf_op jit(solution)/shard_map/ppermute | solution.py:21
  46.7 5.3 %collective-permute-done.15.second.b2 = bf16[32,16,256]{2,1,0:T(8,128)(2,1)S(1)} collective-permute-done((bf16[32,16,256]{2,1,0:T(8,128)(2,1)S(1)}, bf16[32,16,256]{2,1,0:T(8,128)(2,1)S(1)}, u32[]{:S(2)}, u32[]{:S(2)}) %collective-permute-start.15) | collective-permute-done | bytes 262176 | tf_op jit(solution)/shard_map/ppermute | solution.py:21
  52.3 0.6 copy.19
  52.9 1.2 %motion.4 = (bf16[32,16,384]{2,1,0:T(8,128)(2,1)S(1)}, f32[32,8,128]{2,1,0:T(8,128)S(1)}) custom-call(f32[2,24,128]{2,1,0:T(8,128)S(1)} %get-tuple-element.45.scale, bf16[2,64,16,256]{3,2,1,0:T(8,128)(2,1)S(1)} %copy-done, bf16[2,64,8,256]{3,2,1,0:T(8,128)(2,1)S(1)} %get-tuple-element.46.left_edge, ...), custom_call_target="tpu_custom_call" | custom-call | bytes 9450000 | tf_op jit(solution)/shard_map/motion/pallas_call | solution.py:44
  54.0 1.2 %motion.5 = (bf16[32,16,384]{2,1,0:T(8,128)(2,1)S(1)}, f32[32,8,128]{2,1,0:T(8,128)S(1)}) custom-call(f32[2,24,128]{2,1,0:T(8,128)S(1)} %get-tuple-element.45.scale, bf16[2,64,16,256]{3,2,1,0:T(8,128)(2,1)S(1)} %copy-done, bf16[2,64,8,256]{3,2,1,0:T(8,128)(2,1)S(1)} %get-tuple-element.46.left_edge, ...), custom_call_target="tpu_custom_call" | custom-call | bytes 9450000 | tf_op jit(solution)/shard_map/motion/pallas_call | solution.py:44
  55.2 4.2 %fine_gru.2.refs_0_ = bf16[2,64,16,128]{3,2,1,0:T(8,128)(2,1)} custom-call(bf16[2,66,16,384]{3,2,1,0:T(8,128)(2,1)S(1)} %get-tuple-element.43.hid3, bf16[2,64,16,128]{3,2,1,0:T(8,128)(2,1)S(1)} %copy-done.2, f32[2,528,128]{2,1,0:T(8,128)S(1)} %get-tuple-element.44.hid_edge, bf16[32,16,384]{2,1,0:T(8,128)(2,1)S(1)} %get-tuple-element.55.refs_0_, ...), custom_call_target="tpu_custom_call" | custom-call | bytes 17500000 | tf_op jit(solution)/shard_map/fine_gru/pallas_call | solution.py:423
  59.5 1.2 %motion.6 = (bf16[32,16,384]{2,1,0:T(8,128)(2,1)S(1)}, f32[32,8,128]{2,1,0:T(8,128)S(1)}) custom-call(f32[2,24,128]{2,1,0:T(8,128)S(1)} %get-tuple-element.45.scale, bf16[2,64,16,256]{3,2,1,0:T(8,128)(2,1)S(1)} %copy-done, bf16[2,64,8,256]{3,2,1,0:T(8,128)(2,1)S(1)} %get-tuple-element.46.left_edge, ...), custom_call_target="tpu_custom_call" | custom-call | bytes 9450000 | tf_op jit(solution)/shard_map/motion/pallas_call | solution.py:44
  60.6 1.2 %motion.7 = (bf16[32,16,384]{2,1,0:T(8,128)(2,1)S(1)}, f32[32,8,128]{2,1,0:T(8,128)S(1)}) custom-call(f32[2,24,128]{2,1,0:T(8,128)S(1)} %get-tuple-element.45.scale, bf16[2,64,16,256]{3,2,1,0:T(8,128)(2,1)S(1)} %copy-done, bf16[2,64,8,256]{3,2,1,0:T(8,128)(2,1)S(1)} %get-tuple-element.46.left_edge, ...), custom_call_target="tpu_custom_call" | custom-call | bytes 9450000 | tf_op jit(solution)/shard_map/motion/pallas_call | solution.py:44
  61.8 4.2 %fine_gru.3 = bf16[2,64,16,128]{3,2,1,0:T(8,128)(2,1)} custom-call(bf16[2,66,16,384]{3,2,1,0:T(8,128)(2,1)S(1)} %get-tuple-element.43.hid3, bf16[2,64,16,128]{3,2,1,0:T(8,128)(2,1)S(1)} %copy-done.2, f32[2,528,128]{2,1,0:T(8,128)S(1)} %get-tuple-element.44.hid_edge, bf16[2,64,16,128]{3,2,1,0:T(8,128)(2,1)} %fine_gru.2.refs_0_, ...), custom_call_target="tpu_custom_call", output_to_operand_aliasing={{}: (3, {})} | custom-call | bytes 17500000 | tf_op jit(solution)/shard_map/fine_gru/pallas_call | solution.py:423
  (56 shorter events, 2.5 us)
Async XLA Ops:
  2.1 20.5 %copy-start.7 = (bf16[256,36]{1,0:T(8,128)(2,1)S(1)}, bf16[256,36]{1,0:T(8,128)(2,1)}, u32[]{:S(2)}) copy-start(bf16[256,36]{1,0:T(8,128)(2,1)} %constant.8.clone.pick) | copy-start | bytes 55300
  2.1 20.5 %copy-start.8 = (s32[24,128]{1,0:T(8,128)S(1)}, s32[24,128]{1,0:T(8,128)}, u32[]{:S(2)}) copy-start(s32[24,128]{1,0:T(8,128)} %constant.6.clone.distance) | copy-start | bytes 36868
  2.1 20.5 %copy-start.9 = (bf16[36,128]{1,0:T(8,128)(2,1)S(1)}, bf16[36,128]{1,0:T(8,128)(2,1)}, u32[]{:S(2)}) copy-start(bf16[36,128]{1,0:T(8,128)(2,1)} %motion_weight.1) | copy-start | bytes 27652
  2.3 22.9 %copy-start.3 = (bf16[9,384,128]{2,1,0:T(8,128)(2,1)S(1)}, bf16[9,384,128]{2,1,0:T(8,128)(2,1)}, u32[]{:S(2)}) copy-start(bf16[9,384,128]{2,1,0:T(8,128)(2,1)} %refs_10_.1) | copy-start | bytes 2654212
  2.3 22.9 %copy-start.4 = (bf16[9,256,256]{2,1,0:T(8,128)(2,1)S(1)}, bf16[9,256,256]{2,1,0:T(8,128)(2,1)}, u32[]{:S(2)}) copy-start(bf16[9,256,256]{2,1,0:T(8,128)(2,1)} %gates.1) | copy-start | bytes 3538948
  2.3 22.9 %copy-start.5 = (bf16[9,256,128]{2,1,0:T(8,128)(2,1)S(1)}, bf16[9,256,128]{2,1,0:T(8,128)(2,1)}, u32[]{:S(2)}) copy-start(bf16[9,256,128]{2,1,0:T(8,128)(2,1)} %cand.1) | copy-start | bytes 1769476
  2.9 22.3 %copy-start.1 = (bf16[9,384,256]{2,1,0:T(8,128)(2,1)S(1)}, bf16[9,384,256]{2,1,0:T(8,128)(2,1)}, u32[]{:S(2)}) copy-start(bf16[9,384,256]{2,1,0:T(8,128)(2,1)} %refs_9_.3) | copy-start | bytes 5308420
  2.9 14.7 %collective-permute-start.1 = (bf16[688,256]{1,0:T(8,128)(2,1)S(1)}, bf16[688,256]{1,0:T(8,128)(2,1)S(1)}, u32[]{:S(2)}, u32[]{:S(2)}) collective-permute-start(bf16[688,256]{1,0:T(8,128)(2,1)S(1)} %get-tuple-element.37.to_prev), channel_id=1, source_target_pairs={{0,15},{1,0},{2,1},{3,2},{4,3},{5,4},{6,5},{7,6},{8,7},{9,8},{10,9... | collective-permute-start | bytes 1056776 | tf_op jit(solution)/shard_map/ppermute | solution.py:21
  8.4 9.2 %collective-permute-start = (bf16[432,256]{1,0:T(8,128)(2,1)S(1)}, bf16[432,256]{1,0:T(8,128)(2,1)S(1)}, u32[]{:S(2)}, u32[]{:S(2)}) collective-permute-start(bf16[432,256]{1,0:T(8,128)(2,1)S(1)} %get-tuple-element.36.to_next), channel_id=1, source_target_pairs={{0,1},{1,2},{2,3},{3,4},{4,5},{5,6},{6,7},{7,8},{8,9},{9,10},{10,1... | collective-permute-start | bytes 663560 | tf_op jit(solution)/shard_map/ppermute | solution.py:21
  8.4 9.2 %collective-permute-start.2 = (bf16[128,256]{1,0:T(8,128)(2,1)S(1)}, bf16[128,256]{1,0:T(8,128)(2,1)S(1)}, u32[]{:S(2)}, u32[]{:S(2)}) collective-permute-start(bf16[128,256]{1,0:T(8,128)(2,1)S(1)} %get-tuple-element.38), channel_id=1, source_target_pairs={{0,5},{1,6},{2,7},{3,8},{4,9},{5,10},{6,11},{7,12},{8,13},{9,14},{... | collective-permute-start | bytes 196616 | tf_op jit(solution)/shard_map/ppermute | solution.py:21
  8.4 6.7 %collective-permute-start.3 = (bf16[32,256]{1,0:T(8,128)(2,1)S(1)}, bf16[32,256]{1,0:T(8,128)(2,1)S(1)}, u32[]{:S(2)}, u32[]{:S(2)}) collective-permute-start(bf16[32,256]{1,0:T(8,128)(2,1)S(1)} %get-tuple-element.39.flat), channel_id=1, source_target_pairs={{0,2},{1,3},{2,4},{3,5},{4,6},{5,7},{6,8},{7,9},{8,10},{9,11},{10,... | collective-permute-start | bytes 49160 | tf_op jit(solution)/shard_map/ppermute | solution.py:21
  9.6 5.5 %collective-permute-start.4 = (bf16[32,256]{1,0:T(8,128)(2,1)S(1)}, bf16[32,256]{1,0:T(8,128)(2,1)S(1)}, u32[]{:S(2)}, u32[]{:S(2)}) collective-permute-start(bf16[32,256]{1,0:T(8,128)(2,1)S(1)} %get-tuple-element.39.flat), channel_id=1, source_target_pairs={{0,14},{1,15},{2,0},{3,1},{4,2},{5,3},{6,4},{7,5},{8,6},{9,7},{10,... | collective-permute-start | bytes 49160 | tf_op jit(solution)/shard_map/ppermute | solution.py:21
  17.6 11.0 %collective-permute-start.5 = (bf16[32,16,256]{2,1,0:T(8,128)(2,1)S(1)}, bf16[32,16,256]{2,1,0:T(8,128)(2,1)S(1)}, u32[]{:S(2)}, u32[]{:S(2)}) collective-permute-start(bf16[32,16,256]{2,1,0:T(8,128)(2,1)S(1)} %get-tuple-element.47.refs_0_.mine.right), channel_id=1, source_target_pairs={{0,4},{1,5},{2,6},{3,7},{4,8},{5,9},{6,10},{7,11},{8,12},{9,13},{1... | collective-permute-start | bytes 786440 | tf_op jit(solution)/shard_map/ppermute | solution.py:21
  18.0 16.2 %collective-permute-start.8 = (bf16[32,16,256]{2,1,0:T(8,128)(2,1)S(1)}, bf16[32,16,256]{2,1,0:T(8,128)(2,1)S(1)}, u32[]{:S(2)}, u32[]{:S(2)}) collective-permute-start(bf16[32,16,256]{2,1,0:T(8,128)(2,1)S(1)} %get-tuple-element.56.refs_1_.mine.right), channel_id=1, source_target_pairs={{0,4},{1,5},{2,6},{3,7},{4,8},{5,9},{6,10},{7,11},{8,12},{9,13},{1... | collective-permute-start | bytes 786440 | tf_op jit(solution)/shard_map/ppermute | solution.py:21
  18.3 21.5 %collective-permute-start.11 = (bf16[32,16,256]{2,1,0:T(8,128)(2,1)S(1)}, bf16[32,16,256]{2,1,0:T(8,128)(2,1)S(1)}, u32[]{:S(2)}, u32[]{:S(2)}) collective-permute-start(bf16[32,16,256]{2,1,0:T(8,128)(2,1)S(1)} %get-tuple-element.64.refs_2_.mine.right), channel_id=1, source_target_pairs={{0,4},{1,5},{2,6},{3,7},{4,8},{5,9},{6,10},{7,11},{8,12},{9,13},{1... | collective-permute-start | bytes 786440 | tf_op jit(solution)/shard_map/ppermute | solution.py:21
  19.8 24.6 %collective-permute-start.14 = (bf16[32,16,256]{2,1,0:T(8,128)(2,1)S(1)}, bf16[32,16,256]{2,1,0:T(8,128)(2,1)S(1)}, u32[]{:S(2)}, u32[]{:S(2)}) collective-permute-start(bf16[32,16,256]{2,1,0:T(8,128)(2,1)S(1)} %get-tuple-element.66.refs_3_.mine.right), channel_id=1, source_target_pairs={{0,4},{1,5},{2,6},{3,7},{4,8},{5,9},{6,10},{7,11},{8,12},{9,13},{1... | collective-permute-start | bytes 786440 | tf_op jit(solution)/shard_map/ppermute | solution.py:21
  28.7 15.8 %collective-permute-start.6 = (bf16[32,16,256]{2,1,0:T(8,128)(2,1)S(1)}, bf16[32,16,256]{2,1,0:T(8,128)(2,1)S(1)}, u32[]{:S(2)}, u32[]{:S(2)}) collective-permute-start(bf16[32,16,256]{2,1,0:T(8,128)(2,1)S(1)} %choose.4), channel_id=1, source_target_pairs={{0,2},{1,3},{2,0},{3,1},{4,6},{5,7},{6,4},{7,5},{8,10},{9,11},{10,... | collective-permute-start | bytes 786440 | tf_op jit(solution)/shard_map/ppermute | solution.py:21
  34.3 10.3 %collective-permute-start.9 = (bf16[32,16,256]{2,1,0:T(8,128)(2,1)S(1)}, bf16[32,16,256]{2,1,0:T(8,128)(2,1)S(1)}, u32[]{:S(2)}, u32[]{:S(2)}) collective-permute-start(bf16[32,16,256]{2,1,0:T(8,128)(2,1)S(1)} %choose.5), channel_id=1, source_target_pairs={{0,2},{1,3},{2,0},{3,1},{4,6},{5,7},{6,4},{7,5},{8,10},{9,11},{10,... | collective-permute-start | bytes 786440 | tf_op jit(solution)/shard_map/ppermute | solution.py:21
  39.9 6.6 %collective-permute-start.12 = (bf16[32,16,256]{2,1,0:T(8,128)(2,1)S(1)}, bf16[32,16,256]{2,1,0:T(8,128)(2,1)S(1)}, u32[]{:S(2)}, u32[]{:S(2)}) collective-permute-start(bf16[32,16,256]{2,1,0:T(8,128)(2,1)S(1)} %choose.6), channel_id=1, source_target_pairs={{0,2},{1,3},{2,0},{3,1},{4,6},{5,7},{6,4},{7,5},{8,10},{9,11},{10,... | collective-permute-start | bytes 786440 | tf_op jit(solution)/shard_map/ppermute | solution.py:21
  44.4 7.6 %collective-permute-start.15 = (bf16[32,16,256]{2,1,0:T(8,128)(2,1)S(1)}, bf16[32,16,256]{2,1,0:T(8,128)(2,1)S(1)}, u32[]{:S(2)}, u32[]{:S(2)}) collective-permute-start(bf16[32,16,256]{2,1,0:T(8,128)(2,1)S(1)} %choose.7), channel_id=1, source_target_pairs={{0,2},{1,3},{2,0},{3,1},{4,6},{5,7},{6,4},{7,5},{8,10},{9,11},{10,... | collective-permute-start | bytes 786440 | tf_op jit(solution)/shard_map/ppermute | solution.py:21
  44.5 8.3 %collective-permute-start.7 = (bf16[2,32,16,256]{3,2,1,0:T(8,128)(2,1)S(1)}, bf16[2,32,16,256]{3,2,1,0:T(8,128)(2,1)S(1)}, u32[]{:S(2)}, u32[]{:S(2)}) collective-permute-start(bf16[2,32,16,256]{3,2,1,0:T(8,128)(2,1)S(1)} %join.4), channel_id=1, source_target_pairs={{0,1},{1,0},{2,3},{3,2},{4,5},{5,4},{6,7},{7,6},{8,9},{9,8},{10,11... | collective-permute-start | bytes 1572872 | tf_op jit(solution)/shard_map/ppermute | solution.py:21
  44.7 8.2 %collective-permute-start.10 = (bf16[2,32,16,256]{3,2,1,0:T(8,128)(2,1)S(1)}, bf16[2,32,16,256]{3,2,1,0:T(8,128)(2,1)S(1)}, u32[]{:S(2)}, u32[]{:S(2)}) collective-permute-start(bf16[2,32,16,256]{3,2,1,0:T(8,128)(2,1)S(1)} %join.5), channel_id=1, source_target_pairs={{0,1},{1,0},{2,3},{3,2},{4,5},{5,4},{6,7},{7,6},{8,9},{9,8},{10,11... | collective-permute-start | bytes 1572872 | tf_op jit(solution)/shard_map/ppermute | solution.py:21
  46.6 12.9 %collective-permute-start.13 = (bf16[2,32,16,256]{3,2,1,0:T(8,128)(2,1)S(1)}, bf16[2,32,16,256]{3,2,1,0:T(8,128)(2,1)S(1)}, u32[]{:S(2)}, u32[]{:S(2)}) collective-permute-start(bf16[2,32,16,256]{3,2,1,0:T(8,128)(2,1)S(1)} %join.6), channel_id=1, source_target_pairs={{0,1},{1,0},{2,3},{3,2},{4,5},{5,4},{6,7},{7,6},{8,9},{9,8},{10,11... | collective-permute-start | bytes 1572872 | tf_op jit(solution)/shard_map/ppermute | solution.py:21
  52.2 8.4 %collective-permute-start.16 = (bf16[2,32,16,256]{3,2,1,0:T(8,128)(2,1)S(1)}, bf16[2,32,16,256]{3,2,1,0:T(8,128)(2,1)S(1)}, u32[]{:S(2)}, u32[]{:S(2)}) collective-permute-start(bf16[2,32,16,256]{3,2,1,0:T(8,128)(2,1)S(1)} %join.7), channel_id=1, source_target_pairs={{0,1},{1,0},{2,3},{3,2},{4,5},{5,4},{6,7},{7,6},{8,9},{9,8},{10,11... | collective-permute-start | bytes 1572872 | tf_op jit(solution)/shard_map/ppermute | solution.py:21
  (6 other events, 35.0 us)
